TPU v7x, 32 devices: a whole 2x2x4 slice. The times are simulated.
32 devices in a mesh: dp: 8 (over z, core), mp: 4 (over y, x).
Axes of the slice: x: 2, y: 2, z: 4, core: 2. Of those that a mesh axis runs over, the one named last changes fastest.
Arguments:
- tokens: bfloat16 [8192, 2048], P(('dp', 'mp')), may hold values from -6 to 6
- ln_gain: float32 [2048], replicated, may hold values from 0.1 to 1.9
- ln_bias: float32 [2048], replicated, may hold values from -4 to 4
- qkv_weight: float32 [2048, 3, 2048], P('dp', None, 'mp'), may hold values from -0.125 to 0.125
- qkv_bias: float32 [3, 2048], P(None, 'mp'), may hold values from -1.5 to 1.5
- dense_weight: float32 [2048, 2048], P('dp', 'mp'), may hold values from -1 to 1
- dense_bias: float32 [2048], replicated, may hold values from -4 to 4
- fc1_weight: float32 [2048, 8192], P('dp', 'mp'), may hold values from -0.125 to 0.125
- fc1_bias: float32 [8192], P('mp'), may hold values from -6 to 6
- fc2_weight: float32 [2048, 8192], P('dp', 'mp'), may hold values from -0.0625 to 0.0625
- fc2_bias: float32 [2048], replicated, may hold values from -4 to 4
- starts: int32 [8], P('dp'), may hold values from 0 to 768
- cotangent: bfloat16 [8192, 2048], P(('dp', 'mp')), may hold values from -18 to 18
Outputs:
- output: bfloat16 [8192, 2048], P(('dp', 'mp'))
- input_grad: bfloat16 [8192, 2048], P(('dp', 'mp'))
- ln_gain_grad: float32 [2048], replicated
- ln_bias_grad: float32 [2048], replicated
- qkv_weight_grad: float32 [2048, 3, 2048], P('dp', None, 'mp')
- qkv_bias_grad: float32 [3, 2048], P(None, 'mp')
- dense_weight_grad: float32 [2048, 2048], P('dp', 'mp')
- dense_bias_grad: float32 [2048], replicated
- fc1_weight_grad: float32 [2048, 8192], P('dp', 'mp')
- fc1_bias_grad: float32 [8192], P('mp')
- fc2_weight_grad: float32 [2048, 8192], P('dp', 'mp')
- fc2_bias_grad: float32 [2048], replicated
Inputs may be any that keep to these rules, and one draw needn't show every extreme that they name: Each sequence holds one picture piece of 256 tokens that begins at its entry of starts.
All inputs are finite; a program needn't handle non-finite values.
Results may differ from a plain program's by a relative error of at most 0.012.
The roundings to bfloat16 on the way count: a program that leaves them out, or rounds other values in their place, can miss the bound.
Values may be sent and summed in bfloat16 or wider, within the bound.
A program may use at most 320 MiB of HBM per device.

v0:
```python
from functools import partial

import jax
import jax.numpy as jnp
from jax import lax
from jax.sharding import PartitionSpec as P

HEAD_DIM = 64
ROT_DIM = 32
LENGTH = 1024
PIECE = 256


EPSILON = 1e-05
NEGATIVE = -1e30


def normalize(values, gain_vec, shift_vec):
    centre = values - jnp.mean(values, axis=-1, keepdims=True)
    spread = jnp.mean(centre * centre, axis=-1, keepdims=True)
    scaled = centre * lax.rsqrt(spread + EPSILON)
    return scaled * gain_vec + shift_vec


def rotary_tables(row_count):
    half_dim = ROT_DIM // 2
    places = (jnp.arange(row_count) % LENGTH).astype(jnp.float32)
    frequency = 10000.0 ** (-jnp.arange(half_dim).astype(jnp.float32) * 2.0 / ROT_DIM)
    angles = places[:, None] * frequency[None, :]
    return (jnp.cos(angles), jnp.sin(angles))


def rotate(values, cosine_table, sine_table):
    half_dim = ROT_DIM // 2
    first_part = values[..., :half_dim]
    second_part = values[..., half_dim:ROT_DIM]
    cosine_row = cosine_table[:, None, :]
    sine_row = sine_table[:, None, :]
    return jnp.concatenate(
        [
            first_part * cosine_row - second_part * sine_row,
            second_part * cosine_row + first_part * sine_row,
            values[..., ROT_DIM:],
        ],
        axis=-1,
    )


def unrotate(gradient, cosine_table, sine_table):
    half_dim = ROT_DIM // 2
    first_part = gradient[..., :half_dim]
    second_part = gradient[..., half_dim:ROT_DIM]
    cosine_row = cosine_table[:, None, :]
    sine_row = sine_table[:, None, :]
    return jnp.concatenate(
        [
            first_part * cosine_row + second_part * sine_row,
            second_part * cosine_row - first_part * sine_row,
            gradient[..., ROT_DIM:],
        ],
        axis=-1,
    )


def allowed_mask(piece_start):
    places = jnp.arange(LENGTH)
    inside = (places >= piece_start) & (places < piece_start + PIECE)
    return (places[None, :] <= places[:, None]) | inside[:, None] & inside[None, :]


def masked_scores(queries, key_rows, piece_start):
    scores = jnp.einsum(
        "qhd,khd->hqk", queries, key_rows, preferred_element_type=jnp.float32
    ) * HEAD_DIM ** (-0.5)
    return jnp.where(allowed_mask(piece_start)[None], scores, NEGATIVE)


def attend_forward(members):
    queries, key_rows, values_in, piece_start = members
    masked = masked_scores(queries, key_rows, piece_start)
    row_max = jnp.max(masked, axis=-1, keepdims=True)
    expo_values = jnp.exp(masked - row_max)
    row_total = jnp.sum(expo_values, axis=-1, keepdims=True)
    prob_low = (expo_values / row_total).astype(jnp.bfloat16)
    attended = jnp.einsum("hqk,khd->qhd", prob_low, values_in, preferred_element_type=jnp.float32)
    return (attended.astype(jnp.bfloat16), (row_max + jnp.log(row_total))[..., 0])


def attend_backward(members):
    queries, key_rows, values_in, piece_start, logsum, out_grad = members
    masked = masked_scores(queries, key_rows, piece_start)
    prob_values = jnp.exp(masked - logsum[..., None])
    prob_low = prob_values.astype(jnp.bfloat16)
    value_grad = jnp.einsum("hqk,qhd->khd", prob_low, out_grad, preferred_element_type=jnp.float32)
    prob_grad = jnp.einsum("qhd,khd->hqk", out_grad, values_in, preferred_element_type=jnp.float32)
    inner_sum = jnp.sum(prob_values * prob_grad, axis=-1, keepdims=True)
    score_grad = (prob_values * (prob_grad - inner_sum)).astype(jnp.bfloat16)
    query_grad = jnp.einsum(
        "hqk,khd->qhd", score_grad, key_rows, preferred_element_type=jnp.float32
    ) * HEAD_DIM ** (-0.5)
    key_grad = jnp.einsum(
        "hqk,qhd->khd", score_grad, queries, preferred_element_type=jnp.float32
    ) * HEAD_DIM ** (-0.5)
    return (query_grad, key_grad, value_grad)


def right_product(left_side, right_side):
    return lax.dot_general(
        left_side, right_side, (((1,), (1,)), ((), ())), preferred_element_type=jnp.float32
    )


def rows_product(left_side, right_side):
    return lax.dot_general(
        left_side, right_side, (((0,), (0,)), ((), ())), preferred_element_type=jnp.float32
    )


def body(
    tokens,
    ln_gain,
    ln_bias,
    qkv_weight,
    qkv_bias,
    dense_weight,
    dense_bias,
    fc1_weight,
    fc1_bias,
    fc2_weight,
    fc2_bias,
    starts,
    cotangent,
):
    token_float = tokens.astype(jnp.float32)
    normed_low = normalize(token_float, ln_gain, ln_bias).astype(jnp.bfloat16)
    gathered = lax.all_gather(normed_low, "mp", axis=0, tiled=True)
    group_rows = gathered.shape[0]
    masters = (
        qkv_weight.astype(jnp.bfloat16),
        dense_weight.astype(jnp.bfloat16),
        fc1_weight.astype(jnp.bfloat16),
        fc2_weight.astype(jnp.bfloat16),
    )
    qkv_full, dense_full, up_full, down_full = (
        lax.all_gather(masters[0], "dp", axis=0, tiled=True),
        lax.all_gather(masters[1], "dp", axis=0, tiled=True),
        lax.all_gather(masters[2], "dp", axis=0, tiled=True),
        lax.all_gather(masters[3], "dp", axis=0, tiled=True),
    )
    model_width = qkv_full.shape[0]
    local_width = qkv_full.shape[2]
    heads_local = local_width // HEAD_DIM
    seq_count = group_rows // LENGTH

    def to_sequences(tensor):
        return tensor.reshape(seq_count, LENGTH, heads_local, HEAD_DIM)

    def to_heads(tensor):
        return tensor.reshape(group_rows, heads_local, HEAD_DIM)

    projected = jnp.dot(
        gathered, qkv_full.reshape(model_width, 3 * local_width), preferred_element_type=jnp.float32
    ) + qkv_bias.reshape(3 * local_width)
    cosine_table, sine_table = rotary_tables(group_rows)
    queries = rotate(to_heads(projected[:, :local_width]), cosine_table, sine_table).astype(
        jnp.bfloat16
    )
    key_rows = rotate(
        to_heads(projected[:, local_width : 2 * local_width]), cosine_table, sine_table
    ).astype(jnp.bfloat16)
    values_in = to_heads(projected[:, 2 * local_width :]).astype(jnp.bfloat16)
    attended, logsum = lax.map(
        attend_forward,
        (to_sequences(queries), to_sequences(key_rows), to_sequences(values_in), starts),
    )
    attended = attended.reshape(group_rows, local_width)
    attn_part = right_product(attended, dense_full)
    hidden_pre = jnp.dot(gathered, up_full, preferred_element_type=jnp.float32) + fc1_bias
    hidden_low = jax.nn.gelu(hidden_pre, approximate=True).astype(jnp.bfloat16)
    mlp_part = right_product(hidden_low, down_full)
    mixed_sum = lax.psum_scatter(attn_part + mlp_part, "mp", scatter_dimension=0, tiled=True)
    output = (token_float + mixed_sum + dense_bias + fc2_bias).astype(jnp.bfloat16)
    out_rows = lax.all_gather(cotangent, "mp", axis=0, tiled=True)
    qkv_full, dense_full, up_full, down_full = (
        lax.all_gather(masters[0], "dp", axis=0, tiled=True),
        lax.all_gather(masters[1], "dp", axis=0, tiled=True),
        lax.all_gather(masters[2], "dp", axis=0, tiled=True),
        lax.all_gather(masters[3], "dp", axis=0, tiled=True),
    )
    attended_grad = jnp.dot(out_rows, dense_full, preferred_element_type=jnp.float32).astype(
        jnp.bfloat16
    )
    dense_grad = rows_product(out_rows, attended)
    down_grad = rows_product(out_rows, hidden_low)
    hidden_grad = jnp.dot(out_rows, down_full, preferred_element_type=jnp.float32)
    gelu_value, gelu_back = jax.vjp(partial(jax.nn.gelu, approximate=True), hidden_pre)
    pre_grad = gelu_back(hidden_grad)[0].astype(jnp.bfloat16)
    up_grad = rows_product(gathered, pre_grad)
    up_bias_grad = jnp.sum(pre_grad.astype(jnp.float32), axis=0)
    query_grad, key_grad, value_grad = lax.map(
        attend_backward,
        (
            to_sequences(queries),
            to_sequences(key_rows),
            to_sequences(values_in),
            starts,
            logsum,
            to_sequences(attended_grad),
        ),
    )
    query_grad = unrotate(to_heads(query_grad), cosine_table, sine_table).reshape(
        group_rows, local_width
    )
    key_grad = unrotate(to_heads(key_grad), cosine_table, sine_table).reshape(
        group_rows, local_width
    )
    projected_grad = jnp.concatenate(
        [query_grad, key_grad, value_grad.reshape(group_rows, local_width)], axis=1
    ).astype(jnp.bfloat16)
    qkv_grad = rows_product(gathered, projected_grad).reshape(model_width, 3, local_width)
    qkv_bias_grad = jnp.sum(projected_grad.astype(jnp.float32), axis=0).reshape(3, local_width)
    attn_input = right_product(projected_grad, qkv_full.reshape(model_width, 3 * local_width))
    mlp_input = right_product(pre_grad, up_full)
    normed_grad = lax.psum_scatter(attn_input + mlp_input, "mp", scatter_dimension=0, tiled=True)
    norm_value, norm_back = jax.vjp(normalize, token_float, ln_gain, ln_bias)
    token_grad, gain_grad, shift_grad = norm_back(normed_grad)
    cot_float = cotangent.astype(jnp.float32)
    input_grad = (cot_float + token_grad).astype(jnp.bfloat16)
    out_bias_grad = jnp.sum(cot_float, axis=0)
    gain_total, shift_total, bias_total = lax.psum(
        (gain_grad, shift_grad, out_bias_grad), ("dp", "mp")
    )
    qkv_bias_total, up_bias_total = lax.psum((qkv_bias_grad, up_bias_grad), "dp")
    qkv_share, dense_share, up_share, down_share = (
        lax.psum_scatter(qkv_grad, "dp", scatter_dimension=0, tiled=True),
        lax.psum_scatter(dense_grad, "dp", scatter_dimension=0, tiled=True),
        lax.psum_scatter(up_grad, "dp", scatter_dimension=0, tiled=True),
        lax.psum_scatter(down_grad, "dp", scatter_dimension=0, tiled=True),
    )
    return (
        output,
        input_grad,
        gain_total,
        shift_total,
        qkv_share,
        qkv_bias_total,
        dense_share,
        bias_total,
        up_share,
        up_bias_total,
        down_share,
        bias_total,
    )


def solution(mesh):
    in_specs = (
        P(("dp", "mp"), None),
        P(),
        P(),
        P("dp", None, "mp"),
        P(None, "mp"),
        P("dp", "mp"),
        P(),
        P("dp", "mp"),
        P("mp"),
        P("dp", "mp"),
        P(),
        P("dp"),
        P(("dp", "mp"), None),
    )
    out_specs = (
        P(("dp", "mp"), None),
        P(("dp", "mp"), None),
        P(),
        P(),
        P("dp", None, "mp"),
        P(None, "mp"),
        P("dp", "mp"),
        P(),
        P("dp", "mp"),
        P("mp"),
        P("dp", "mp"),
        P(),
    )
    return jax.shard_map(body, mesh=mesh, in_specs=in_specs, out_specs=out_specs, check_vma=False)
```

profile of v0, /device:TPU:0, one launch (start us, length us, event | category | flops | bytes accessed | tf_op | source)
XLA Modules:
  0.0 1090.3 jit_solution(6903509558316797406)
XLA Ops:
  7.3 1.9 convert_element_type.151
  9.9 1.6 convert_reduce_fusion.2
  11.5 1.6 fusion.24
  15.8 2.6 copy.40
  19.7 2.8 convert_element_type.154
  23.3 1.6 fusion.13
  25.8 16.3 %all-gather.11.cloned.1.call-done = bf16[2048,512]{1,0:T(8,128)(2,1)} async-done(((bf16[256,512]{1,0:T(8,128)(2,1)}), bf16[2048,512]{1,0:T(8,128)(2,1)}) %all-gather.11.cloned.1.call-update) | async-done | bytes 2097168 | tf_op jit(solution)/shard_map/all_gather | solution.py:146
  42.1 53.8 %all-gather.17.cloned.1.call-done = bf16[1024,2048]{1,0:T(8,128)(2,1)} async-done(((bf16[256,2048]{1,0:T(8,128)(2,1)}), bf16[1024,2048]{1,0:T(8,128)(2,1)}) %all-gather.17.cloned.1.call-update) | async-done | bytes 4194320 | tf_op jit(solution)/shard_map/all_gather | solution.py:183
  95.9 5.2 convolution_convert_fusion
  101.2 49.8 %all-gather.7.cloned.1.call-done = bf16[1024,2048]{1,0:T(8,128)(2,1)} async-done(((bf16[256,2048]{1,0:T(8,128)(2,1)}), bf16[1024,2048]{1,0:T(8,128)(2,1)}) %all-gather.7.cloned.1.call-update) | async-done | bytes 4194320 | tf_op jit(solution)/shard_map/all_gather | solution.py:136
  151.0 67.2 %all-gather.9.cloned.1.call-done = bf16[2048,3,512]{0,2,1:T(8,128)(2,1)} async-done(((bf16[256,3,512]{0,2,1:T(8,128)(2,1)}), bf16[2048,3,512]{0,2,1:T(8,128)(2,1)}) %all-gather.9.cloned.1.call-update) | async-done | bytes 6291472 | tf_op jit(solution)/shard_map/all_gather | solution.py:145
  218.2 10.2 convolution_add_fusion
  228.4 1.8 fusion.47
  231.3 2.9 copy.42
  234.2 1.8 copy.43
  237.4 1.5 slice.105
  238.9 2.1 subtract_convert_fusion.3
  241.0 14.0 %fusion.48 = (f32[8,1024]{1,0:T(8,128)S(1)}, f32[8,1024,1024]{1,2,0:T(8,128)}) fusion(bf16[1024,8,32]{0,2,1:T(8,128)(2,1)S(1)} %slice.104, bf16[1024,8,16]{0,2,1:T(8,128)(2,1)S(1)} %get-tuple-element.113, bf16[1024,8,16]{0,2,1:T(8,128)(2,1)S(1)} %get-tuple-element.114, bf16[1024,8,32]{0,2,1:T(8,128)(2,1)S(1)} %slice.105, ...), kind=kOutput, calls=%fused_computation.100 | convolution fusion | flops 1105190912 | bytes 36732928 | tf_op jit(solution)/shard_map/while/body/eval_jaxpr/qhd,khd->hqk/dot_general | solution.py:72
  255.1 13.4 %fusion = f32[8,1024]{1,0:T(8,128)S(1)} fusion(f32[8,1024,1024]{1,2,0:T(8,128)} %get-tuple-element.118, f32[8,1024]{1,0:T(8,128)S(1)} %get-tuple-element.117), kind=kLoop, calls=%fused_computation.6 | loop fusion | flops 16769024 | bytes 33619968 | tf_op jit(solution)/shard_map/while/body/eval_jaxpr/reduce_sum | solution.py:83
  269.7 22.6 %multiply_reduce_fusion = (f32[8,1024]{1,0:T(8,128)S(1)}, f32[8,1024,1024]{1,2,0:T(8,128)}) fusion(f32[8,1024,1024]{1,2,0:T(8,128)} %get-tuple-element.118, f32[8,1024]{1,0:T(8,128)S(1)} %log_add_fusion, bf16[1024,8,64]{0,2,1:T(8,128)(2,1)S(1)} %bitcast.56, bf16[1024,8,64]{0,2,1:T(8,128)(2,1)S(1)} %bitcast.58), kind=kOutput, calls=%fused_computation.1 | convolution fusion | flops 1098899456 | bytes 69271552 | tf_op jit(solution)/shard_map/while/body/eval_jaxpr/qhd,khd->hqk/dot_general | solution.py:95
  292.3 29.3 %multiply_convert_fusion = bf16[8,1024,1024]{1,2,0:T(8,128)(2,1)} fusion(f32[8,1024,1024]{1,2,0:T(8,128)} %get-tuple-element.120, f32[8,1024,1024]{1,2,0:T(8,128)} %get-tuple-element.118, f32[8,1024]{1,0:T(8,128)S(1)} %get-tuple-element.119, f32[8,1024]{1,0:T(8,128)S(1)} %log_add_fusion), kind=kLoop, calls=%fused_computation | loop fusion | flops 33554432 | bytes 83951616 | tf_op jit(solution)/shard_map/while/body/eval_jaxpr/convert_element_type | solution.py:97
  321.6 11.4 %multiply_bitcast_fusion = f32[1024,8,64]{0,2,1:T(8,128)S(1)} fusion(bf16[8,1024,1024]{1,2,0:T(8,128)(2,1)} %multiply_convert_fusion, bf16[1024,8,32]{0,2,1:T(8,128)(2,1)} %copy-done.11, bf16[1024,8,16]{0,2,1:T(8,128)(2,1)} %copy-done.15, bf16[1024,8,16]{0,2,1:T(8,128)(2,1)} %copy-done.14), kind=kOutput, calls=%fused_computation.53 | convolution fusion | flops 1077411840 | bytes 19922944 | tf_op jit(solution)/shard_map/while/body/eval_jaxpr/hqk,qhd->khd/dot_general | solution.py:101
  333.9 9.2 multiply_bitcast_fusion.1
  345.2 14.0 %fusion.32 = bf16[8,64,1024]{2,1,0:T(8,128)(2,1)S(1)} fusion(bf16[1024,8,64]{0,2,1:T(8,128)(2,1)S(1)} %bitcast.59, f32[8,1024,1024]{1,2,0:T(8,128)} %get-tuple-element.118, f32[8,1024]{1,0:T(8,128)S(1)} %copy-done.21, f32[8,1024]{1,0:T(8,128)S(1)} %get-tuple-element.117), kind=kOutput, calls=%fused_computation.57 | convolution fusion | flops 1099431936 | bytes 35717120 | tf_op jit(solution)/shard_map/while/body/eval_jaxpr/hqk,khd->qhd/dot_general | solution.py:85
  360.2 4.4 convolution_bitcast_fusion.1
  364.6 13.9 %fusion.29 = bf16[8,64,1024]{2,1,0:T(8,128)(2,1)S(1)} fusion(bf16[1024,8,64]{0,2,1:T(8,128)(2,1)S(1)} %bitcast.57, f32[8,1024,1024]{1,2,0:T(8,128)} %get-tuple-element.118, f32[8,1024]{1,0:T(8,128)S(1)} %log_add_fusion), kind=kOutput, calls=%fused_computation.55 | convolution fusion | flops 1091043328 | bytes 35684352 | tf_op jit(solution)/shard_map/while/body/eval_jaxpr/hqk,qhd->khd/dot_general | solution.py:94
  378.6 1.7 pad_maximum_fusion.3
  380.3 15.0 %fusion.49 = f32[1024,2048]{1,0:T(8,128)} fusion(bf16[1024,2048]{1,0:T(8,128)(2,1)} %all-gather.7.cloned.1.call-done, bf16[2048,2048]{1,0:T(8,128)(2,1)} %all-gather.13.cloned.1.call-done), kind=kOutput, calls=%fused_computation.101 | convolution fusion | flops 8589934592 | bytes 20971520 | tf_op jit(solution)/shard_map/dot_general | solution.py:178
  395.4 19.0 %convert_reduce_fusion = (f32[2048]{0:T(1024)S(1)}, bf16[1024,2048]{1,0:T(8,128)(2,1)S(1)}) fusion(f32[1024,2048]{1,0:T(8,128)} %fusion.49, f32[2048]{0:T(1024)S(1)} %copy-done.35, bf16[1024,2048]{1,0:T(8,128)(2,1)} %all-gather.17.cloned.1.call-done, bf16[2048,2048]{1,0:T(8,128)(2,1)} %all-gather.15.cloned.1.call-done), kind=kOutput, calls=%fused_computation.21 | convolution fusion | flops 8638167040 | bytes 25182208 | tf_op jit(solution)/shard_map/dot_general | solution.py:195
  414.4 8.8 fusion.50
  423.2 11.0 %convolution_add_fusion.2 = f32[1024,2048]{1,0:T(8,128)} fusion(f32[1024,2048]{1,0:T(8,128)S(1)} %fusion.50, bf16[2048,1536]{0,1:T(8,128)(2,1)} %bitcast.72, bf16[1024,512]{0,1:T(8,128)(2,1)S(1)} %bitcast.60, bf16[1024,512]{0,1:T(8,128)(2,1)S(1)} %bitcast.66, bf16[1024,512]{0,1:T(8,128)(2,1)S(1)} %bitcast.63), kind=kOutput, calls=%fused_computation.28 | convolution fusion | flops 6453985280 | bytes 26214400 | tf_op jit(solution)/shard_map/dot_general | solution.py:108
  434.3 15.8 %fusion.44 = f32[1024,2048]{1,0:T(8,128)S(1)} fusion(bf16[2048,2048]{1,0:T(8,128)(2,1)} %all-gather.15.cloned.1.call-done, f32[1024,2048]{1,0:T(8,128)} %fusion.49, f32[2048]{0:T(1024)S(1)} %copy-done.35), kind=kOutput, calls=%fused_computation.97 | convolution fusion | flops 8610906112 | bytes 25174016 | tf_op jit(solution)/shard_map/dot_general | solution.py:108
  450.2 5.6 convolution_add_fusion.1
  455.9 17.4 %convolution_bitcast_fusion = f32[2048,2048]{0,1:T(8,128)} fusion(bf16[1024,2048]{1,0:T(8,128)(2,1)} %all-gather.17.cloned.1.call-done, f32[1024,2048]{1,0:T(8,128)} %fusion.49, f32[2048]{0:T(1024)S(1)} %copy-done.35), kind=kOutput, calls=%fused_computation.13 | convolution fusion | flops 8610906112 | bytes 29368320 | tf_op jit(solution)/shard_map/dot_general | solution.py:114
  473.4 14.4 %fusion.42 = f32[2048,1536]{0,1:T(8,128)} fusion(bf16[1024,2048]{1,0:T(8,128)(2,1)} %all-gather.7.cloned.1.call-done, bf16[1024,512]{0,1:T(8,128)(2,1)S(1)} %bitcast.61, bf16[1024,512]{0,1:T(8,128)(2,1)S(1)} %bitcast.67, bf16[1024,512]{0,1:T(8,128)(2,1)S(1)} %bitcast.64), kind=kOutput, calls=%fused_computation.95 | convolution fusion | flops 6451888128 | bytes 19922944 | tf_op jit(solution)/shard_map/dot_general | solution.py:114
  487.8 12.6 %copy.48 = f32[2048,3,512]{2,0,1:T(8,128)} copy(f32[2048,3,512]{0,2,1:T(8,128)} %bitcast.51) | data formatting | bytes 25165824 | tf_op jit(solution)/shard_map/reshape | solution.py:220
  500.5 15.6 %fusion.51 = f32[2048,2048]{1,0:T(8,128)} fusion(bf16[1024,2048]{1,0:T(8,128)(2,1)} %all-gather.7.cloned.1.call-done, bf16[1024,2048]{1,0:T(8,128)(2,1)} %copy-done.36), kind=kOutput, calls=%fused_computation.103 | convolution fusion | flops 8589934592 | bytes 25165824 | tf_op jit(solution)/shard_map/dot_general | solution.py:114
  516.2 1.7 convert_reduce_fusion.1
  517.9 28.1 %all-reduce.1 = (f32[3,512]{1,0:T(4,128)}, f32[2048]{0:T(1024)}) all-reduce(f32[3,512]{1,0:T(4,128)S(1)} %reshape.255, f32[2048]{0:T(1024)S(1)} %get-tuple-element.96), channel_id=1, replica_groups=mesh['dp'=8,'mp'=4] {'dp'}, use_global_device_ids=true, to_apply=%region_15.16 | all-reduce | flops 3584 | bytes 28672 | tf_op jit(solution)/shard_map/psum | solution.py:233
  546.0 2.1 copy.49
  548.1 2.5 fusion.45
  551.6 59.4 %reduce-scatter.7.cloned.1.call-done = f32[256,2048]{1,0:T(8,128)} async-done(((f32[1024,2048]{1,0:T(8,128)}), f32[256,2048]{1,0:T(8,128)}) %reduce-scatter.7.cloned.1.call-update) | async-done | bytes 2097168 | tf_op jit(solution)/shard_map/reduce_scatter | solution.py:181
  611.0 4.8 convert_reduce_fusion.3
  615.8 41.1 %all-reduce = (f32[2048]{0:T(1024)}, f32[2048]{0:T(1024)}, f32[2048]{0:T(1024)S(1)}) all-reduce(f32[2048]{0:T(1024)S(1)} %get-tuple-element.87, f32[2048]{0:T(1024)S(1)} %get-tuple-element.89, f32[2048]{0:T(1024)S(1)} %get-tuple-element.108), channel_id=1, replica_groups=mesh['dp'=8,'mp'=4] {'dp','mp'}, use_global_device_ids=true, to_apply=%region_10.11 | all-reduce | flops 6144 | bytes 49152 | tf_op jit(solution)/shard_map/psum | solution.py:230
  657.0 125.5 %reduce-scatter.17.cloned.1.call-done = f32[256,2048]{0,1:T(8,128)} async-done(((f32[2048,2048]{0,1:T(8,128)}), f32[256,2048]{0,1:T(8,128)}) %reduce-scatter.17.cloned.1.call-update) | async-done | bytes 2097168 | tf_op jit(solution)/shard_map/reduce_scatter | solution.py:238
  782.5 2.9 copy.50
  785.4 127.6 %reduce-scatter.11.cloned.1.call-done = f32[256,3,512]{2,0,1:T(8,128)} async-done(((f32[2048,3,512]{2,0,1:T(8,128)}), f32[256,3,512]{2,0,1:T(8,128)}) %reduce-scatter.11.cloned.1.call-update) | async-done | bytes 1572880 | tf_op jit(solution)/shard_map/reduce_scatter | solution.py:235
  913.0 169.4 %reduce-scatter.15.cloned.1.call-done = f32[256,2048]{1,0:T(8,128)} async-done(((f32[2048,2048]{1,0:T(8,128)}), f32[256,2048]{1,0:T(8,128)}) %reduce-scatter.15.cloned.1.call-update) | async-done | bytes 2097168 | tf_op jit(solution)/shard_map/reduce_scatter | solution.py:237
  (123 shorter events, 15.3 us)
Async XLA Ops:
  7.2 7.2 copy-start
  7.2 7.1 copy-start.18
  7.2 7.1 copy-start.28
  7.2 34.9 %all-gather.11.cloned.1.call-start = ((), (), s32[]{:S(2)}) async-start(), calls=%async_computation.8 | async-start | bytes 2359296 | tf_op jit(solution)/shard_map/all_gather | solution.py:146
  9.1 86.8 %all-gather.17.cloned.1.call-start = ((), (), s32[]{:S(2)}) async-start(), calls=%async_computation.12 | async-start | bytes 5242880 | tf_op jit(solution)/shard_map/all_gather | solution.py:183
  9.9 8.6 copy-start.12
  9.9 141.1 %all-gather.7.cloned.1.call-start = ((), (), s32[]{:S(2)}) async-start(), calls=%async_computation.6 | async-start | bytes 5242880 | tf_op jit(solution)/shard_map/all_gather | solution.py:136
  11.5 2.2 copy-start.22
  13.8 0.6 copy-start.24
  15.8 202.4 %all-gather.9.cloned.1.call-start = ((), (), s32[]{:S(2)}) async-start(), calls=%async_computation.7 | async-start | bytes 7077888 | tf_op jit(solution)/shard_map/all_gather | solution.py:145
  18.4 4.1 copy-start.29
  18.4 361.9 %all-gather.13.cloned.1.call-start = ((), (), s32[]{:S(2)}) async-start(), calls=%async_computation.9 | async-start | bytes 9437184 | tf_op jit(solution)/shard_map/all_gather | solution.py:147
  19.6 375.7 %all-gather.15.cloned.1.call-start = ((), (), s32[]{:S(2)}) async-start(), calls=%async_computation.10 | async-start | bytes 9437184 | tf_op jit(solution)/shard_map/all_gather | solution.py:148
  22.5 523.5 %reduce-scatter.13.cloned.1.call-start = ((), (), s32[]{:S(2)}) async-start(), calls=%async_computation.15 | async-start | bytes 4718592 | tf_op jit(solution)/shard_map/reduce_scatter | solution.py:236
  236.0 5.1 copy-start.16
  237.3 17.7 %copy-start.10 = (bf16[1024,8,32]{0,2,1:T(8,128)(2,1)}, bf16[1024,8,32]{0,2,1:T(8,128)(2,1)S(1)}, u32[]{:S(2)}) copy-start(bf16[1024,8,32]{0,2,1:T(8,128)(2,1)S(1)} %slice.104) | copy-start | bytes 1572868
  238.9 16.1 %copy-start.11 = (bf16[1024,8,32]{0,2,1:T(8,128)(2,1)}, bf16[1024,8,32]{0,2,1:T(8,128)(2,1)S(1)}, u32[]{:S(2)}) copy-start(bf16[1024,8,32]{0,2,1:T(8,128)(2,1)S(1)} %slice.105) | copy-start | bytes 1572868
  241.0 14.1 %copy-start.13 = (bf16[1024,8,16]{0,2,1:T(8,128)(2,1)}, bf16[1024,8,16]{0,2,1:T(8,128)(2,1)S(1)}, u32[]{:S(2)}) copy-start(bf16[1024,8,16]{0,2,1:T(8,128)(2,1)S(1)} %get-tuple-element.114) | copy-start | bytes 786436
  241.0 14.1 %copy-start.14 = (bf16[1024,8,16]{0,2,1:T(8,128)(2,1)}, bf16[1024,8,16]{0,2,1:T(8,128)(2,1)S(1)}, u32[]{:S(2)}) copy-start(bf16[1024,8,16]{0,2,1:T(8,128)(2,1)S(1)} %get-tuple-element.104) | copy-start | bytes 786436
  241.0 14.1 %copy-start.15 = (bf16[1024,8,16]{0,2,1:T(8,128)(2,1)}, bf16[1024,8,16]{0,2,1:T(8,128)(2,1)S(1)}, u32[]{:S(2)}) copy-start(bf16[1024,8,16]{0,2,1:T(8,128)(2,1)S(1)} %get-tuple-element.105) | copy-start | bytes 786436
  255.1 14.0 %copy-start.6 = (bf16[1024,512]{1,0:T(8,128)(2,1)S(1)}, bf16[1024,512]{1,0:T(8,128)(2,1)}, u32[]{:S(2)}) copy-start(bf16[1024,512]{1,0:T(8,128)(2,1)} %slice.101) | copy-start | bytes 3145732
  268.5 0.6 copy-start.20
  269.7 22.6 %copy-start.3 = (bf16[1024,512]{0,1:T(8,128)(2,1)}, bf16[1024,512]{0,1:T(8,128)(2,1)S(1)}, u32[]{:S(2)}) copy-start(bf16[1024,512]{0,1:T(8,128)(2,1)S(1)} %copy.41) | copy-start | bytes 3145732
  333.9 10.1 copy-start.17
  343.1 2.1 copy-start.4
  343.1 2.1 copy-start.21
  345.2 15.0 %copy-start.34 = (bf16[1024,2048]{1,0:T(8,128)(2,1)S(1)}, bf16[1024,2048]{1,0:T(8,128)(2,1)}, u32[]{:S(2)}) copy-start(bf16[1024,2048]{1,0:T(8,128)(2,1)} %all-gather.17.cloned.1.call-done) | copy-start | bytes 12582916
  359.2 1.0 copy-start.7
  378.5 169.6 %reduce-scatter.9.cloned.1.call-start = ((), (), s32[]{:S(2)}) async-start(), calls=%async_computation.13 | async-start | bytes 10485760 | tf_op jit(solution)/shard_map/reduce_scatter | solution.py:224
  380.3 93.1 %copy-start.5 = (bf16[1024,8,64]{0,2,1:T(8,128)(2,1)}, bf16[1024,8,64]{0,2,1:T(8,128)(2,1)S(1)}, u32[]{:S(2)}) copy-start(bf16[1024,8,64]{0,2,1:T(8,128)(2,1)S(1)} %get-tuple-element.122) | copy-start | bytes 3145732
  380.3 15.1 %copy-start.35 = (f32[2048]{0:T(1024)S(1)}, f32[2048]{0:T(1024)}, u32[]{:S(2)}) copy-start(f32[2048]{0:T(1024)} %param.21) | copy-start | bytes 24580
  395.4 19.0 %copy-start.33 = (bf16[2048,2048]{1,0:T(8,128)(2,1)S(1)}, bf16[2048,2048]{1,0:T(8,128)(2,1)}, u32[]{:S(2)}) copy-start(bf16[2048,2048]{1,0:T(8,128)(2,1)} %all-gather.13.cloned.1.call-done) | copy-start | bytes 25165828
  414.3 8.9 copy-start.36
  434.3 176.8 %reduce-scatter.7.cloned.1.call-start = ((), (), s32[]{:S(2)}) async-start(), calls=%async_computation.11 | async-start | bytes 10485760 | tf_op jit(solution)/shard_map/reduce_scatter | solution.py:181
  434.3 15.8 %copy-start.8 = (bf16[8,64,1024]{2,1,0:T(8,128)(2,1)S(1)}, bf16[8,64,1024]{2,1,0:T(8,128)(2,1)}, u32[]{:S(2)}) copy-start(bf16[8,64,1024]{2,1,0:T(8,128)(2,1)} %copy-done.7) | copy-start | bytes 3145732
  434.3 15.8 %copy-start.9 = (bf16[2048,512]{1,0:T(8,128)(2,1)S(1)}, bf16[2048,512]{1,0:T(8,128)(2,1)}, u32[]{:S(2)}) copy-start(bf16[2048,512]{1,0:T(8,128)(2,1)} %all-gather.11.cloned.1.call-done) | copy-start | bytes 6291460
  455.8 326.7 %reduce-scatter.17.cloned.1.call-start = ((), (), s32[]{:S(2)}) async-start(), calls=%async_computation.17 | async-start | bytes 18874368 | tf_op jit(solution)/shard_map/reduce_scatter | solution.py:238
  473.3 439.7 %reduce-scatter.11.cloned.1.call-start = ((), (), s32[]{:S(2)}) async-start(), calls=%async_computation.14 | async-start | bytes 14155776 | tf_op jit(solution)/shard_map/reduce_scatter | solution.py:235
  500.4 582.0 %reduce-scatter.15.cloned.1.call-start = ((), (), s32[]{:S(2)}) async-start(), calls=%async_computation.16 | async-start | bytes 18874368 | tf_op jit(solution)/shard_map/reduce_scatter | solution.py:237
  516.1 32.0 %copy-start.1 = (bf16[256,2048]{1,0:T(8,128)(2,1)S(1)}, bf16[256,2048]{1,0:T(8,128)(2,1)}, u32[]{:S(2)}) copy-start(bf16[256,2048]{1,0:T(8,128)(2,1)} %param.13) | copy-start | bytes 3145732
  516.1 32.0 %copy-start.19 = (f32[2048]{0:T(1024)S(1)}, f32[2048]{0:T(1024)}, u32[]{:S(2)}) copy-start(f32[2048]{0:T(1024)} %param.14) | copy-start | bytes 24580
  516.1 32.0 %copy-start.23 = (f32[256]{0:T(256)S(1)}, f32[256]{0:T(256)}, u32[]{:S(2)}) copy-start(f32[256]{0:T(256)} %copy-done.22) | copy-start | bytes 3076
  516.2 34.5 %copy-start.27 = (f32[256]{0:T(256)S(1)}, f32[256]{0:T(256)}, u32[]{:S(2)}) copy-start(f32[256]{0:T(256)} %copy-done.26) | copy-start | bytes 3076
  516.2 34.5 %copy-start.25 = (f32[256]{0:T(256)S(1)}, f32[256]{0:T(256)}, u32[]{:S(2)}) copy-start(f32[256]{0:T(256)} %copy-done.24) | copy-start | bytes 3076
  517.9 93.1 %copy-start.31 = (f32[2048]{0:T(1024)S(1)}, f32[2048]{0:T(1024)}, u32[]{:S(2)}) copy-start(f32[2048]{0:T(1024)} %param.23) | copy-start | bytes 24580
  517.9 93.1 %copy-start.32 = (f32[2048]{0:T(1024)S(1)}, f32[2048]{0:T(1024)}, u32[]{:S(2)}) copy-start(f32[2048]{0:T(1024)} %param.19) | copy-start | bytes 24580
  548.1 2.5 copy-start.2
  656.9 426.1 %copy-start.30 = (f32[2048]{0:T(1024)}, f32[2048]{0:T(1024)S(1)}, u32[]{:S(2)}) copy-start(f32[2048]{0:T(1024)S(1)} %get-tuple-element.146) | copy-start | bytes 24580
  (1 other events, 0.6 us)
Sparse Core Ops, SparseCore 0:
  10.2 31.8 all-gather.10
  43.9 51.9 all-gather.16
  98.4 52.5 all-gather.6
  153.0 65.1 all-gather.8
  220.2 80.2 all-gather.12
  302.5 80.5 all-gather.14
  385.3 48.4 reduce-scatter.12
  436.8 84.7 reduce-scatter.8
  524.7 86.2 reduce-scatter.6
  613.2 169.1 reduce-scatter.16
  785.4 127.6 reduce-scatter.10
  915.8 166.6 reduce-scatter.14
where the time goes:
time: 1100 us; the launch traced here: 1090 us
  waiting for transfers between devices  670 us (61%)
  matrix products  228 us (21%)
  other arithmetic  70.5 us (6%)
  blocking collectives  69.2 us (6%)
  local copies, waits for them, and re-layouts  36.4 us (3%)
  between operations  15.9 us (1%)
    reduce_scatter x1, waiting for transfers between devices, body(): lax.psum_scatter(up_grad, 'dp', scatter_dimension=0, tiled=True)  169 us
    reduce_scatter x1, waiting for transfers between devices, body(): lax.psum_scatter(qkv_grad, 'dp', scatter_dimension=0, tiled=True)  128 us
    reduce_scatter x1, waiting for transfers between devices, body(): lax.psum_scatter(down_grad, 'dp', scatter_dimension=0, tiled=True)  126 us
    all_gather x1, waiting for transfers between devices, body(): lax.all_gather(masters[0], 'dp', axis=0, tiled=True)  67.2 us
    reduce_scatter x1, waiting for transfers between devices, body(): lax.psum_scatter(attn_part + mlp_part, 'mp', scatter_dimension=0, tiled=T...  59.4 us
    all_gather x1, waiting for transfers between devices, body(): out_rows = lax.all_gather(cotangent, 'mp', axis=0, tiled=True)  53.8 us
    dot_general x4, matrix products, rows_product(): lax.dot_general(left_side, right_side, (((0,), (0,)), ((), ())), preferre...  51.8 us
    all_gather x1, waiting for transfers between devices, body(): gathered = lax.all_gather(normed_low, 'mp', axis=0, tiled=True)  49.8 us
  transfers between devices with their start and end apart: 12, of which 8 were waited for; matrix products, arithmetic and copies ran while one was open for 30% of the time, Pallas kernels for 0%

commit v1 on v0

--- a/solution.py
+++ b/solution.py
@@ -114,6 +114,12 @@
     return lax.dot_general(
         left_side, right_side, (((0,), (0,)), ((), ())), preferred_element_type=jnp.float32
     )
+
+
+def low_scatter(partial_sums, axis):
+    return lax.psum_scatter(
+        partial_sums.astype(jnp.bfloat16), axis, scatter_dimension=0, tiled=True
+    ).astype(jnp.float32)
 
 
 def body(
@@ -178,7 +184,7 @@
     hidden_pre = jnp.dot(gathered, up_full, preferred_element_type=jnp.float32) + fc1_bias
     hidden_low = jax.nn.gelu(hidden_pre, approximate=True).astype(jnp.bfloat16)
     mlp_part = right_product(hidden_low, down_full)
-    mixed_sum = lax.psum_scatter(attn_part + mlp_part, "mp", scatter_dimension=0, tiled=True)
+    mixed_sum = low_scatter(attn_part + mlp_part, "mp")
     output = (token_float + mixed_sum + dense_bias + fc2_bias).astype(jnp.bfloat16)
     out_rows = lax.all_gather(cotangent, "mp", axis=0, tiled=True)
     qkv_full, dense_full, up_full, down_full = (
@@ -221,7 +227,7 @@
     qkv_bias_grad = jnp.sum(projected_grad.astype(jnp.float32), axis=0).reshape(3, local_width)
     attn_input = right_product(projected_grad, qkv_full.reshape(model_width, 3 * local_width))
     mlp_input = right_product(pre_grad, up_full)
-    normed_grad = lax.psum_scatter(attn_input + mlp_input, "mp", scatter_dimension=0, tiled=True)
+    normed_grad = low_scatter(attn_input + mlp_input, "mp")
     norm_value, norm_back = jax.vjp(normalize, token_float, ln_gain, ln_bias)
     token_grad, gain_grad, shift_grad = norm_back(normed_grad)
     cot_float = cotangent.astype(jnp.float32)
@@ -232,10 +238,10 @@
     )
     qkv_bias_total, up_bias_total = lax.psum((qkv_bias_grad, up_bias_grad), "dp")
     qkv_share, dense_share, up_share, down_share = (
-        lax.psum_scatter(qkv_grad, "dp", scatter_dimension=0, tiled=True),
-        lax.psum_scatter(dense_grad, "dp", scatter_dimension=0, tiled=True),
-        lax.psum_scatter(up_grad, "dp", scatter_dimension=0, tiled=True),
-        lax.psum_scatter(down_grad, "dp", scatter_dimension=0, tiled=True),
+        low_scatter(qkv_grad, "dp"),
+        low_scatter(dense_grad, "dp"),
+        low_scatter(up_grad, "dp"),
+        low_scatter(down_grad, "dp"),
     )
     return (
         output,

time: 1100 us -> 810 us (0.74)
  waiting for transfers between devices: 670 us -> 391 us
    reduce_scatter x6, waiting for transfers between devices: 482 us -> 203 us  [low_scatter(): lax.psum_scatter(partial_sums.astype(jnp.bfloat16), axis, scatter_dimensi...]
    reshape x1 -> x0, local copies, waits for them, and re-layouts: 12.6 us -> none  [body(): rows_product(gathered, projected_grad).reshape(model_width, 3, local_width)]
  transfers between devices with their start and end apart: 12 -> 12, of which waited for: 8 -> 7; matrix products, arithmetic and copies ran while one was open for 30% -> 40% of each run, Pallas kernels for 0% -> 0%
where the time goes in v1:
time: 810 us; the launch traced here: 805 us
  waiting for transfers between devices  391 us (48%)
  matrix products  222 us (27%)
  other arithmetic  76.1 us (9%)
  blocking collectives  67.5 us (8%)
  local copies, waits for them, and re-layouts  31.7 us (4%)
  between operations  16 us (2%)
    reduce_scatter x6, waiting for transfers between devices, low_scatter(): lax.psum_scatter(partial_sums.astype(jnp.bfloat16), axis, scatter_dimensi...  203 us
    all_gather x1, waiting for transfers between devices, body(): lax.all_gather(masters[0], 'dp', axis=0, tiled=True)  67.2 us
    all_gather x1, waiting for transfers between devices, body(): out_rows = lax.all_gather(cotangent, 'mp', axis=0, tiled=True)  53.8 us
    all_gather x1, waiting for transfers between devices, body(): gathered = lax.all_gather(normed_low, 'mp', axis=0, tiled=True)  49.8 us
    dot_general x4, matrix products, rows_product(): lax.dot_general(left_side, right_side, (((0,), (0,)), ((), ())), preferre...  47.5 us
    dot_general x4, matrix products, right_product(): lax.dot_general(left_side, right_side, (((1,), (1,)), ((), ())), preferre...  40.3 us
    psum x1, blocking collectives, body(): lax.psum((gain_grad, shift_grad, out_bias_grad), ('dp', 'mp'))  39.2 us
    convert_element_type x1, other arithmetic, attend_backward(): score_grad = (prob_values * (prob_grad - inner_sum)).astype(jnp.bfloat16)  29.3 us
  transfers between devices with their start and end apart: 12, of which 7 were waited for; matrix products, arithmetic and copies ran while one was open for 40% of the time, Pallas kernels for 0%

profile of v1, /device:TPU:0, one launch (start us, length us, event | category | flops | bytes accessed | tf_op | source)
XLA Modules:
  0.0 804.7 jit_solution(14406205368883967676)
XLA Ops:
  7.3 1.9 convert_element_type.196
  11.5 1.6 fusion.24
  15.8 2.6 copy.40
  19.7 2.8 convert_element_type.199
  23.3 1.6 fusion.13
  25.8 16.3 %all-gather.11.cloned.1.call-done = bf16[2048,512]{1,0:T(8,128)(2,1)} async-done(((bf16[256,512]{1,0:T(8,128)(2,1)}), bf16[2048,512]{1,0:T(8,128)(2,1)}) %all-gather.11.cloned.1.call-update) | async-done | bytes 2097168 | tf_op jit(solution)/shard_map/all_gather | solution.py:152
  42.1 53.8 %all-gather.17.cloned.1.call-done = bf16[1024,2048]{1,0:T(8,128)(2,1)} async-done(((bf16[256,2048]{1,0:T(8,128)(2,1)}), bf16[1024,2048]{1,0:T(8,128)(2,1)}) %all-gather.17.cloned.1.call-update) | async-done | bytes 4194320 | tf_op jit(solution)/shard_map/all_gather | solution.py:189
  95.9 5.2 convolution_convert_fusion.3
  101.2 49.8 %all-gather.7.cloned.1.call-done = bf16[1024,2048]{1,0:T(8,128)(2,1)} async-done(((bf16[256,2048]{1,0:T(8,128)(2,1)}), bf16[1024,2048]{1,0:T(8,128)(2,1)}) %all-gather.7.cloned.1.call-update) | async-done | bytes 4194320 | tf_op jit(solution)/shard_map/all_gather | solution.py:142
  151.0 67.2 %all-gather.9.cloned.1.call-done = bf16[2048,3,512]{0,2,1:T(8,128)(2,1)} async-done(((bf16[256,3,512]{0,2,1:T(8,128)(2,1)}), bf16[2048,3,512]{0,2,1:T(8,128)(2,1)}) %all-gather.9.cloned.1.call-update) | async-done | bytes 6291472 | tf_op jit(solution)/shard_map/all_gather | solution.py:151
  218.2 10.2 %convolution_add_fusion = f32[1024,1536]{1,0:T(8,128)S(1)} fusion(bf16[1024,2048]{1,0:T(8,128)(2,1)} %all-gather.7.cloned.1.call-done, bf16[2048,1536]{0,1:T(8,128)(2,1)} %bitcast.69, f32[1536]{0:T(1024)S(1)} %add.171), kind=kOutput, calls=%fused_computation.28 | convolution fusion | flops 6444023808 | bytes 16783360 | tf_op jit(solution)/shard_map/dot_general | solution.py:167
  228.4 1.8 fusion.46
  231.3 2.9 copy.42
  234.2 1.8 copy.43
  238.9 2.1 subtract_convert_fusion.3
  241.0 14.0 %fusion.47 = (f32[8,1024]{1,0:T(8,128)S(1)}, f32[8,1024,1024]{1,2,0:T(8,128)}) fusion(bf16[1024,8,32]{0,2,1:T(8,128)(2,1)S(1)} %slice.104, bf16[1024,8,16]{0,2,1:T(8,128)(2,1)S(1)} %get-tuple-element.113, bf16[1024,8,16]{0,2,1:T(8,128)(2,1)S(1)} %get-tuple-element.114, bf16[1024,8,32]{0,2,1:T(8,128)(2,1)S(1)} %slice.105, ...), kind=kOutput, calls=%fused_computation.104 | convolution fusion | flops 1105190912 | bytes 36732928 | tf_op jit(solution)/shard_map/while/body/eval_jaxpr/qhd,khd->hqk/dot_general | solution.py:72
  255.1 13.4 %fusion = f32[8,1024]{1,0:T(8,128)S(1)} fusion(f32[8,1024,1024]{1,2,0:T(8,128)} %get-tuple-element.118, f32[8,1024]{1,0:T(8,128)S(1)} %get-tuple-element.117), kind=kLoop, calls=%fused_computation.6 | loop fusion | flops 16769024 | bytes 33619968 | tf_op jit(solution)/shard_map/while/body/eval_jaxpr/reduce_sum | solution.py:83
  269.7 22.6 %multiply_reduce_fusion = (f32[8,1024]{1,0:T(8,128)S(1)}, f32[8,1024,1024]{1,2,0:T(8,128)}) fusion(f32[8,1024,1024]{1,2,0:T(8,128)} %get-tuple-element.118, f32[8,1024]{1,0:T(8,128)S(1)} %log_add_fusion, bf16[1024,8,64]{0,2,1:T(8,128)(2,1)S(1)} %bitcast.56, bf16[1024,8,64]{0,2,1:T(8,128)(2,1)S(1)} %bitcast.58), kind=kOutput, calls=%fused_computation.1 | convolution fusion | flops 1098899456 | bytes 69271552 | tf_op jit(solution)/shard_map/while/body/eval_jaxpr/qhd,khd->hqk/dot_general | solution.py:95
  292.3 29.3 %multiply_convert_fusion = bf16[8,1024,1024]{1,2,0:T(8,128)(2,1)} fusion(f32[8,1024,1024]{1,2,0:T(8,128)} %get-tuple-element.120, f32[8,1024,1024]{1,2,0:T(8,128)} %get-tuple-element.118, f32[8,1024]{1,0:T(8,128)S(1)} %get-tuple-element.119, f32[8,1024]{1,0:T(8,128)S(1)} %log_add_fusion), kind=kLoop, calls=%fused_computation | loop fusion | flops 33554432 | bytes 83951616 | tf_op jit(solution)/shard_map/while/body/eval_jaxpr/convert_element_type | solution.py:97
  321.6 11.4 %multiply_bitcast_fusion = f32[1024,8,64]{0,2,1:T(8,128)S(1)} fusion(bf16[8,1024,1024]{1,2,0:T(8,128)(2,1)} %multiply_convert_fusion, bf16[1024,8,32]{0,2,1:T(8,128)(2,1)} %copy-done.9, bf16[1024,8,16]{0,2,1:T(8,128)(2,1)} %copy-done.13, bf16[1024,8,16]{0,2,1:T(8,128)(2,1)} %copy-done.12), kind=kOutput, calls=%fused_computation.59 | convolution fusion | flops 1077411840 | bytes 19922944 | tf_op jit(solution)/shard_map/while/body/eval_jaxpr/hqk,qhd->khd/dot_general | solution.py:101
  333.9 9.2 %multiply_bitcast_fusion.1 = f32[1024,8,64]{0,2,1:T(8,128)S(1)} fusion(bf16[8,1024,1024]{1,2,0:T(8,128)(2,1)} %multiply_convert_fusion, bf16[1024,8,32]{0,2,1:T(8,128)(2,1)} %copy-done.8, bf16[1024,8,16]{0,2,1:T(8,128)(2,1)S(1)} %get-tuple-element.113, bf16[1024,8,16]{0,2,1:T(8,128)(2,1)} %copy-done.11), kind=kOutput, calls=%fused_computation.60 | convolution fusion | flops 1077411840 | bytes 19922944 | tf_op jit(solution)/shard_map/while/body/eval_jaxpr/hqk,khd->qhd/dot_general | solution.py:98
  345.2 14.0 %fusion.33 = bf16[8,64,1024]{2,1,0:T(8,128)(2,1)S(1)} fusion(bf16[1024,8,64]{0,2,1:T(8,128)(2,1)S(1)} %bitcast.59, f32[8,1024,1024]{1,2,0:T(8,128)} %get-tuple-element.118, f32[8,1024]{1,0:T(8,128)S(1)} %copy-done.19, f32[8,1024]{1,0:T(8,128)S(1)} %get-tuple-element.117), kind=kOutput, calls=%fused_computation.63 | convolution fusion | flops 1099431936 | bytes 35717120 | tf_op jit(solution)/shard_map/while/body/eval_jaxpr/hqk,khd->qhd/dot_general | solution.py:85
  360.2 3.7 fusion.18
  363.9 13.9 %fusion.30 = bf16[8,64,1024]{2,1,0:T(8,128)(2,1)S(1)} fusion(bf16[1024,8,64]{0,2,1:T(8,128)(2,1)S(1)} %bitcast.57, f32[8,1024,1024]{1,2,0:T(8,128)} %get-tuple-element.118, f32[8,1024]{1,0:T(8,128)S(1)} %log_add_fusion), kind=kOutput, calls=%fused_computation.61 | convolution fusion | flops 1091043328 | bytes 35684352 | tf_op jit(solution)/shard_map/while/body/eval_jaxpr/hqk,qhd->khd/dot_general | solution.py:94
  377.9 1.7 pad_maximum_fusion.3
  379.7 14.8 %fusion.48 = f32[1024,2048]{1,0:T(8,128)} fusion(bf16[1024,2048]{1,0:T(8,128)(2,1)} %all-gather.7.cloned.1.call-done, bf16[2048,2048]{1,0:T(8,128)(2,1)} %all-gather.13.cloned.1.call-done), kind=kOutput, calls=%fused_computation.105 | convolution fusion | flops 8589934592 | bytes 20971520 | tf_op jit(solution)/shard_map/dot_general | solution.py:184
  394.5 18.9 %convert_reduce_fusion = (f32[2048]{0:T(1024)S(1)}, bf16[1024,2048]{1,0:T(8,128)(2,1)S(1)}) fusion(f32[1024,2048]{1,0:T(8,128)} %fusion.48, f32[2048]{0:T(1024)S(1)} %copy-done.34, bf16[1024,2048]{1,0:T(8,128)(2,1)} %all-gather.17.cloned.1.call-done, bf16[2048,2048]{1,0:T(8,128)(2,1)} %all-gather.15.cloned.1.call-done), kind=kOutput, calls=%fused_computation.21 | convolution fusion | flops 8638167040 | bytes 25182208 | tf_op jit(solution)/shard_map/dot_general | solution.py:201
  413.5 8.8 %fusion.49 = f32[1024,2048]{1,0:T(8,128)S(1)} fusion(bf16[1024,2048]{1,0:T(8,128)(2,1)S(1)} %get-tuple-element.97, bf16[2048,2048]{1,0:T(8,128)(2,1)S(1)} %copy-done.31), kind=kOutput, calls=%fused_computation.106 | convolution fusion | flops 8589934592 | bytes 20971520 | tf_op jit(solution)/shard_map/dot_general | solution.py:108
  422.3 11.2 %add_convert_fusion = bf16[1024,2048]{1,0:T(8,128)(2,1)} fusion(f32[1024,2048]{1,0:T(8,128)S(1)} %fusion.49, bf16[2048,1536]{0,1:T(8,128)(2,1)} %bitcast.70, bf16[1024,512]{0,1:T(8,128)(2,1)S(1)} %bitcast.60, bf16[1024,512]{0,1:T(8,128)(2,1)S(1)} %bitcast.66, bf16[1024,512]{0,1:T(8,128)(2,1)S(1)} %bitcast.63), kind=kOutput, calls=%fused_computation.22 | convolution fusion | flops 6456082432 | bytes 22020096 | tf_op jit(solution)/shard_map/dot_general | solution.py:108
  433.6 15.8 %fusion.44 = f32[1024,2048]{1,0:T(8,128)S(1)} fusion(bf16[2048,2048]{1,0:T(8,128)(2,1)} %all-gather.15.cloned.1.call-done, f32[1024,2048]{1,0:T(8,128)} %fusion.48, f32[2048]{0:T(1024)S(1)} %copy-done.34), kind=kOutput, calls=%fused_computation.102 | convolution fusion | flops 8610906112 | bytes 25174016 | tf_op jit(solution)/shard_map/dot_general | solution.py:108
  449.5 4.4 add_convert_fusion.1
  454.0 13.6 %convolution_convert_fusion = bf16[2048,1536]{0,1:T(8,128)(2,1)} fusion(bf16[1024,2048]{1,0:T(8,128)(2,1)} %all-gather.7.cloned.1.call-done, bf16[1024,512]{0,1:T(8,128)(2,1)S(1)} %bitcast.61, bf16[1024,512]{0,1:T(8,128)(2,1)S(1)} %bitcast.67, bf16[1024,512]{0,1:T(8,128)(2,1)S(1)} %bitcast.64), kind=kOutput, calls=%fused_computation.25 | convolution fusion | flops 6455033856 | bytes 13631488 | tf_op jit(solution)/shard_map/dot_general | solution.py:114
  467.6 8.4 %copy.48 = bf16[2048,3,512]{2,0,1:T(8,128)(2,1)} copy(bf16[2048,3,512]{0,2,1:T(8,128)(2,1)} %bitcast.55) | data formatting | bytes 12582912 | tf_op jit(solution)/shard_map/convert_element_type | solution.py:121
  476.1 14.3 %convolution_convert_fusion.1 = bf16[2048,2048]{1,0:T(8,128)(2,1)} fusion(bf16[1024,2048]{1,0:T(8,128)(2,1)} %all-gather.7.cloned.1.call-done, bf16[1024,2048]{1,0:T(8,128)(2,1)} %copy-done.37), kind=kOutput, calls=%fused_computation.26 | convolution fusion | flops 8594128896 | bytes 16777216 | tf_op jit(solution)/shard_map/dot_general | solution.py:114
  490.5 15.9 %convert_bitcast_fusion = bf16[2048,2048]{0,1:T(8,128)(2,1)} fusion(bf16[1024,2048]{1,0:T(8,128)(2,1)} %all-gather.17.cloned.1.call-done, f32[1024,2048]{1,0:T(8,128)} %fusion.48, f32[2048]{0:T(1024)S(1)} %copy-done.34), kind=kOutput, calls=%fused_computation.20 | convolution fusion | flops 8615100416 | bytes 20979712 | tf_op jit(solution)/shard_map/dot_general | solution.py:114
  506.5 1.8 convert_reduce_fusion.1
  508.3 28.3 %all-reduce.1 = (f32[3,512]{1,0:T(4,128)}, f32[2048]{0:T(1024)}) all-reduce(f32[3,512]{1,0:T(4,128)S(1)} %reshape.253, f32[2048]{0:T(1024)S(1)} %get-tuple-element.96), channel_id=1, replica_groups=mesh['dp'=8,'mp'=4] {'dp'}, use_global_device_ids=true, to_apply=%region_15.16 | all-reduce | flops 3584 | bytes 28672 | tf_op jit(solution)/shard_map/psum | solution.py:239
  536.6 1.9 copy.49
  538.5 2.0 convert_reduce_fusion.2
  540.6 2.3 fusion.29
  542.9 4.1 convert_reduce_fusion.4
  547.1 39.2 %all-reduce = (f32[2048]{0:T(1024)}, f32[2048]{0:T(1024)}, f32[2048]{0:T(1024)S(1)}) all-reduce(f32[2048]{0:T(1024)S(1)} %get-tuple-element.87, f32[2048]{0:T(1024)S(1)} %get-tuple-element.89, f32[2048]{0:T(1024)S(1)} %get-tuple-element.108), channel_id=1, replica_groups=mesh['dp'=8,'mp'=4] {'dp','mp'}, use_global_device_ids=true, to_apply=%region_10.11 | all-reduce | flops 6144 | bytes 49152 | tf_op jit(solution)/shard_map/psum | solution.py:236
  586.3 27.4 %reduce-scatter.11.cloned.1.call-done = bf16[256,3,512]{2,0,1:T(8,128)(2,1)} async-done(((bf16[2048,3,512]{2,0,1:T(8,128)(2,1)}), bf16[256,3,512]{2,0,1:T(8,128)(2,1)}) %reduce-scatter.11.cloned.1.call-update) | async-done | bytes 786448 | tf_op jit(solution)/shard_map/reduce_scatter | solution.py:120
  613.7 2.5 convert_element_type.213
  616.2 87.8 %reduce-scatter.15.cloned.1.call-done = bf16[256,2048]{1,0:T(8,128)(2,1)} async-done(((bf16[2048,2048]{1,0:T(8,128)(2,1)}), bf16[256,2048]{1,0:T(8,128)(2,1)}) %reduce-scatter.15.cloned.1.call-update) | async-done | bytes 1048592 | tf_op jit(solution)/shard_map/reduce_scatter | solution.py:120
  704.0 2.8 convert_element_type.219
  706.8 87.4 %reduce-scatter.17.cloned.1.call-done = bf16[256,2048]{0,1:T(8,128)(2,1)} async-done(((bf16[2048,2048]{0,1:T(8,128)(2,1)}), bf16[256,2048]{0,1:T(8,128)(2,1)}) %reduce-scatter.17.cloned.1.call-update) | async-done | bytes 1048592 | tf_op jit(solution)/shard_map/reduce_scatter | solution.py:120
  794.2 2.6 copy.50
  (127 shorter events, 17.5 us)
Async XLA Ops:
  7.2 7.2 copy-start
  7.2 7.1 copy-start.16
  7.2 7.1 copy-start.26
  7.2 34.9 %all-gather.11.cloned.1.call-start = ((), (), s32[]{:S(2)}) async-start(), calls=%async_computation.8 | async-start | bytes 2359296 | tf_op jit(solution)/shard_map/all_gather | solution.py:152
  9.1 86.8 %all-gather.17.cloned.1.call-start = ((), (), s32[]{:S(2)}) async-start(), calls=%async_computation.12 | async-start | bytes 5242880 | tf_op jit(solution)/shard_map/all_gather | solution.py:189
  9.9 8.6 %copy-start.10 = (f32[256,2048]{1,0:T(8,128)S(1)}, f32[256,2048]{1,0:T(8,128)}, u32[]{:S(2)}) copy-start(f32[256,2048]{1,0:T(8,128)} %param.20) | copy-start | bytes 6291460
  9.9 141.1 %all-gather.7.cloned.1.call-start = ((), (), s32[]{:S(2)}) async-start(), calls=%async_computation.6 | async-start | bytes 5242880 | tf_op jit(solution)/shard_map/all_gather | solution.py:142
  11.5 2.2 copy-start.20
  15.8 202.4 %all-gather.9.cloned.1.call-start = ((), (), s32[]{:S(2)}) async-start(), calls=%async_computation.7 | async-start | bytes 7077888 | tf_op jit(solution)/shard_map/all_gather | solution.py:151
  18.4 4.1 copy-start.29
  18.4 361.2 %all-gather.13.cloned.1.call-start = ((), (), s32[]{:S(2)}) async-start(), calls=%async_computation.9 | async-start | bytes 9437184 | tf_op jit(solution)/shard_map/all_gather | solution.py:153
  19.6 374.9 %all-gather.15.cloned.1.call-start = ((), (), s32[]{:S(2)}) async-start(), calls=%async_computation.10 | async-start | bytes 9437184 | tf_op jit(solution)/shard_map/all_gather | solution.py:154
  22.5 514.1 %reduce-scatter.13.cloned.1.call-start = ((), (), s32[]{:S(2)}) async-start(), calls=%async_computation.15 | async-start | bytes 2359296 | tf_op jit(solution)/shard_map/reduce_scatter | solution.py:120
  236.0 5.1 copy-start.14
  237.4 17.7 %copy-start.8 = (bf16[1024,8,32]{0,2,1:T(8,128)(2,1)}, bf16[1024,8,32]{0,2,1:T(8,128)(2,1)S(1)}, u32[]{:S(2)}) copy-start(bf16[1024,8,32]{0,2,1:T(8,128)(2,1)S(1)} %slice.104) | copy-start | bytes 1572868
  238.9 16.1 %copy-start.9 = (bf16[1024,8,32]{0,2,1:T(8,128)(2,1)}, bf16[1024,8,32]{0,2,1:T(8,128)(2,1)S(1)}, u32[]{:S(2)}) copy-start(bf16[1024,8,32]{0,2,1:T(8,128)(2,1)S(1)} %slice.105) | copy-start | bytes 1572868
  241.0 14.1 %copy-start.11 = (bf16[1024,8,16]{0,2,1:T(8,128)(2,1)}, bf16[1024,8,16]{0,2,1:T(8,128)(2,1)S(1)}, u32[]{:S(2)}) copy-start(bf16[1024,8,16]{0,2,1:T(8,128)(2,1)S(1)} %get-tuple-element.114) | copy-start | bytes 786436
  241.0 14.1 %copy-start.12 = (bf16[1024,8,16]{0,2,1:T(8,128)(2,1)}, bf16[1024,8,16]{0,2,1:T(8,128)(2,1)S(1)}, u32[]{:S(2)}) copy-start(bf16[1024,8,16]{0,2,1:T(8,128)(2,1)S(1)} %get-tuple-element.104) | copy-start | bytes 786436
  241.0 14.1 %copy-start.13 = (bf16[1024,8,16]{0,2,1:T(8,128)(2,1)}, bf16[1024,8,16]{0,2,1:T(8,128)(2,1)S(1)}, u32[]{:S(2)}) copy-start(bf16[1024,8,16]{0,2,1:T(8,128)(2,1)S(1)} %get-tuple-element.105) | copy-start | bytes 786436
  255.1 14.0 %copy-start.6 = (bf16[1024,512]{1,0:T(8,128)(2,1)S(1)}, bf16[1024,512]{1,0:T(8,128)(2,1)}, u32[]{:S(2)}) copy-start(bf16[1024,512]{1,0:T(8,128)(2,1)} %slice.101) | copy-start | bytes 3145732
  268.5 0.6 copy-start.18
  269.7 22.6 %copy-start.3 = (bf16[1024,512]{0,1:T(8,128)(2,1)}, bf16[1024,512]{0,1:T(8,128)(2,1)S(1)}, u32[]{:S(2)}) copy-start(bf16[1024,512]{0,1:T(8,128)(2,1)S(1)} %copy.41) | copy-start | bytes 3145732
  333.9 10.1 %copy-start.15 = (f32[1024,16]{0,1:T(8,128)S(1)}, f32[1024,16]{0,1:T(8,128)}, u32[]{:S(2)}) copy-start(f32[1024,16]{0,1:T(8,128)} %get-tuple-element.116) | copy-start | bytes 196612
  343.1 2.1 copy-start.4
  343.1 2.0 copy-start.19
  345.2 15.0 %copy-start.32 = (bf16[1024,2048]{1,0:T(8,128)(2,1)S(1)}, bf16[1024,2048]{1,0:T(8,128)(2,1)}, u32[]{:S(2)}) copy-start(bf16[1024,2048]{1,0:T(8,128)(2,1)} %all-gather.17.cloned.1.call-done) | copy-start | bytes 12582916
  359.2 1.0 copy-start.35
  377.9 160.7 %reduce-scatter.9.cloned.1.call-start = ((), (), s32[]{:S(2)}) async-start(), calls=%async_computation.13 | async-start | bytes 5242880 | tf_op jit(solution)/shard_map/reduce_scatter | solution.py:120
  379.6 74.4 %copy-start.5 = (bf16[1024,8,64]{0,2,1:T(8,128)(2,1)}, bf16[1024,8,64]{0,2,1:T(8,128)(2,1)S(1)}, u32[]{:S(2)}) copy-start(bf16[1024,8,64]{0,2,1:T(8,128)(2,1)S(1)} %get-tuple-element.122) | copy-start | bytes 3145732
  379.6 14.9 %copy-start.34 = (f32[2048]{0:T(1024)S(1)}, f32[2048]{0:T(1024)}, u32[]{:S(2)}) copy-start(f32[2048]{0:T(1024)} %param.21) | copy-start | bytes 24580
  394.5 19.0 %copy-start.31 = (bf16[2048,2048]{1,0:T(8,128)(2,1)S(1)}, bf16[2048,2048]{1,0:T(8,128)(2,1)}, u32[]{:S(2)}) copy-start(bf16[2048,2048]{1,0:T(8,128)(2,1)} %all-gather.13.cloned.1.call-done) | copy-start | bytes 25165828
  413.5 8.9 %copy-start.37 = (bf16[1024,2048]{1,0:T(8,128)(2,1)}, bf16[1024,2048]{1,0:T(8,128)(2,1)S(1)}, u32[]{:S(2)}) copy-start(bf16[1024,2048]{1,0:T(8,128)(2,1)S(1)} %get-tuple-element.97) | copy-start | bytes 12582916
  433.6 109.3 %reduce-scatter.7.cloned.1.call-start = ((), (), s32[]{:S(2)}) async-start(), calls=%async_computation.11 | async-start | bytes 5242880 | tf_op jit(solution)/shard_map/reduce_scatter | solution.py:120
  433.6 15.8 %copy-start.33 = (bf16[2048,512]{1,0:T(8,128)(2,1)S(1)}, bf16[2048,512]{1,0:T(8,128)(2,1)}, u32[]{:S(2)}) copy-start(bf16[2048,512]{1,0:T(8,128)(2,1)} %all-gather.11.cloned.1.call-done) | copy-start | bytes 6291460
  433.6 15.8 %copy-start.36 = (bf16[8,64,1024]{2,1,0:T(8,128)(2,1)S(1)}, bf16[8,64,1024]{2,1,0:T(8,128)(2,1)}, u32[]{:S(2)}) copy-start(bf16[8,64,1024]{2,1,0:T(8,128)(2,1)} %copy-done.35) | copy-start | bytes 3145732
  453.9 159.8 %reduce-scatter.11.cloned.1.call-start = ((), (), s32[]{:S(2)}) async-start(), calls=%async_computation.14 | async-start | bytes 7077888 | tf_op jit(solution)/shard_map/reduce_scatter | solution.py:120
  476.0 228.0 %reduce-scatter.15.cloned.1.call-start = ((), (), s32[]{:S(2)}) async-start(), calls=%async_computation.16 | async-start | bytes 9437184 | tf_op jit(solution)/shard_map/reduce_scatter | solution.py:120
  490.4 303.8 %reduce-scatter.17.cloned.1.call-start = ((), (), s32[]{:S(2)}) async-start(), calls=%async_computation.17 | async-start | bytes 9437184 | tf_op jit(solution)/shard_map/reduce_scatter | solution.py:120
  506.4 32.1 %copy-start.1 = (bf16[256,2048]{1,0:T(8,128)(2,1)S(1)}, bf16[256,2048]{1,0:T(8,128)(2,1)}, u32[]{:S(2)}) copy-start(bf16[256,2048]{1,0:T(8,128)(2,1)} %param.13) | copy-start | bytes 3145732
  506.4 32.1 %copy-start.17 = (f32[2048]{0:T(1024)S(1)}, f32[2048]{0:T(1024)}, u32[]{:S(2)}) copy-start(f32[2048]{0:T(1024)} %param.14) | copy-start | bytes 24580
  506.4 32.1 %copy-start.21 = (f32[256]{0:T(256)S(1)}, f32[256]{0:T(256)}, u32[]{:S(2)}) copy-start(f32[256]{0:T(256)} %copy-done.20) | copy-start | bytes 3076
  506.4 34.1 %copy-start.25 = (f32[256]{0:T(256)S(1)}, f32[256]{0:T(256)}, u32[]{:S(2)}) copy-start(f32[256]{0:T(256)} %copy-done.24) | copy-start | bytes 3076
  506.4 34.1 %copy-start.23 = (f32[256]{0:T(256)S(1)}, f32[256]{0:T(256)}, u32[]{:S(2)}) copy-start(f32[256]{0:T(256)} %copy-done.22) | copy-start | bytes 3076
  506.4 36.4 %copy-start.27 = (f32[2048]{0:T(1024)S(1)}, f32[2048]{0:T(1024)}, u32[]{:S(2)}) copy-start(f32[2048]{0:T(1024)} %param.23) | copy-start | bytes 24580
  506.5 36.4 %copy-start.28 = (f32[2048]{0:T(1024)S(1)}, f32[2048]{0:T(1024)}, u32[]{:S(2)}) copy-start(f32[2048]{0:T(1024)} %param.19) | copy-start | bytes 24580
  508.3 34.6 %copy-start.7 = (bf16[256,2048]{1,0:T(8,128)(2,1)S(1)}, bf16[256,2048]{1,0:T(8,128)(2,1)}, u32[]{:S(2)}) copy-start(bf16[256,2048]{1,0:T(8,128)(2,1)} %param.25) | copy-start | bytes 3145732
  538.5 4.4 copy-start.2
  586.3 210.5 %copy-start.30 = (f32[2048]{0:T(1024)}, f32[2048]{0:T(1024)S(1)}, u32[]{:S(2)}) copy-start(f32[2048]{0:T(1024)S(1)} %get-tuple-element.146) | copy-start | bytes 24580
  (2 other events, 1.1 us)
Sparse Core Ops, SparseCore 0:
  10.2 31.8 all-gather.10
  43.9 51.9 all-gather.16
  98.4 52.5 all-gather.6
  153.0 65.1 all-gather.8
  220.2 80.2 all-gather.12
  302.5 80.5 all-gather.14
  385.9 34.5 reduce-scatter.12
  433.7 51.4 reduce-scatter.8
  488.2 52.5 reduce-scatter.6
  542.9 70.7 reduce-scatter.10
  616.0 87.9 reduce-scatter.14
  706.2 87.9 reduce-scatter.16

commit v2 on v1

--- a/solution.py
+++ b/solution.py
@@ -3,16 +3,354 @@
 import jax
 import jax.numpy as jnp
 from jax import lax
+from jax.experimental import pallas as pl
+from jax.experimental.pallas import tpu as pltpu
 from jax.sharding import PartitionSpec as P
 
 HEAD_DIM = 64
 ROT_DIM = 32
 LENGTH = 1024
 PIECE = 256
-
-
 EPSILON = 1e-05
 NEGATIVE = -1e30
+MESH = pl.DeviceIdType.MESH
+BF = jnp.bfloat16
+F32 = jnp.float32
+ANY = pl.BlockSpec(memory_space=pl.ANY)
+VM = pl.BlockSpec(memory_space=pltpu.VMEM)
+
+
+def dot(a, b, ca=1, cb=0):
+    return lax.dot_general(a, b, (((ca,), (cb,)), ((), ())), preferred_element_type=F32)
+
+
+def remote(src, dst, send, recv, dp_index, mp_index):
+    return pltpu.make_async_remote_copy(
+        src_ref=src,
+        dst_ref=dst,
+        send_sem=send,
+        recv_sem=recv,
+        device_id=(dp_index, mp_index),
+        device_id_type=MESH,
+    )
+
+
+def place():
+    me = lax.axis_index("dp")
+    return me, me // 2, lax.rem(me, 2), lax.axis_index("mp")
+
+
+def greet(chips, mp_size):
+    me, z, c, mp = place()
+    bar = pltpu.get_barrier_semaphore()
+    pl.semaphore_signal(bar, 1, device_id=(2 * z + 1 - c, mp), device_id_type=MESH)
+
+    @pl.when(z > 0)
+    def _():
+        pl.semaphore_signal(bar, 1, device_id=(me - 2, mp), device_id_type=MESH)
+
+    @pl.when(z < chips - 1)
+    def _():
+        pl.semaphore_signal(bar, 1, device_id=(me + 2, mp), device_id_type=MESH)
+
+    for k in range(1, mp_size):
+        pl.semaphore_signal(
+            bar, 1, device_id=(me, lax.rem(mp + k, mp_size)), device_id_type=MESH
+        )
+    count = mp_size + jnp.where(z > 0, 1, 0) + jnp.where(z < chips - 1, 1, 0)
+    pl.semaphore_wait(bar, count)
+
+
+class RowGather:
+    def __init__(self, chips, own, full, sems):
+        self.chips, self.own, self.full = chips, own, full
+        self.recv, self.left, self.right, self.side = sems
+
+    def copies(self, oz):
+        me, z, c, mp = place()
+        b = 2 * oz + c
+        dst = self.full.at[b]
+
+        def make(src, send, target):
+            return remote(src, dst, send.at[oz], self.recv.at[b], target, mp)
+
+        return (
+            lambda src: make(src, self.left, me - 2),
+            lambda src: make(src, self.right, me + 2),
+            lambda src: make(src, self.side, 2 * z + 1 - c),
+        )
+
+    def start(self):
+        me, z, c, mp = place()
+        left, right, side = self.copies(z)
+
+        @pl.when(z > 0)
+        def _():
+            left(self.own).start()
+
+        @pl.when(z < self.chips - 1)
+        def _():
+            right(self.own).start()
+
+        side(self.own).start()
+
+    def wait_block(self, b):
+        me, z, c, mp = place()
+        remote(self.full.at[b], self.full.at[b], self.side.at[0], self.recv.at[b], me, mp).wait_recv()
+
+    def stage(self, k):
+        me, z, c, mp = place()
+
+        @pl.when(z + k < self.chips)
+        def _():
+            oz = z + k
+            self.wait_block(2 * oz + c)
+            left, right, side = self.copies(oz)
+
+            @pl.when(z > 0)
+            def _():
+                left(self.full.at[2 * oz + c]).start()
+
+            side(self.full.at[2 * oz + c]).start()
+
+        @pl.when(z - k >= 0)
+        def _():
+            oz = z - k
+            self.wait_block(2 * oz + c)
+            left, right, side = self.copies(oz)
+
+            @pl.when(z < self.chips - 1)
+            def _():
+                right(self.full.at[2 * oz + c]).start()
+
+            side(self.full.at[2 * oz + c]).start()
+
+    def drain(self):
+        me, z, c, mp = place()
+        for oz in range(self.chips):
+            left, right, side = self.copies(oz)
+
+            @pl.when((z > 0) & (oz >= z))
+            def _():
+                left(self.full.at[2 * oz + c]).wait_send()
+
+            @pl.when((z < self.chips - 1) & (oz <= z))
+            def _():
+                right(self.full.at[2 * oz + c]).wait_send()
+
+            side(self.full.at[2 * oz + c]).wait_send()
+
+
+class GroupGather:
+    def __init__(self, size, own, full, sems):
+        self.size, self.own, self.full = size, own, full
+        self.send, self.recv = sems
+        self.half = full.shape[1] // 2
+
+    def to(self, src, origin, part, slot, target):
+        me, z, c, mp = place()
+        rows = self.full.at[origin] if part is None else self.full.at[origin, pl.ds(part * self.half, self.half)]
+        sem = self.recv.at[origin, 0 if part is None else part]
+        return remote(src, rows, self.send.at[slot], sem, me, target)
+
+    def start(self):
+        me, z, c, mp = place()
+        for slot, peer in self.peers():
+            self.to(self.own, mp, None, slot, peer).start()
+
+    def peers(self):
+        me, z, c, mp = place()
+        if self.size == 4:
+            x_peer = mp + 1 - 2 * lax.rem(mp, 2)
+            return ((0, x_peer), (1, lax.rem(mp + 2, 4)))
+        return tuple((k - 1, lax.rem(mp + k, self.size)) for k in range(1, self.size))
+
+    def relays(self):
+        (_, x_peer), (_, y_peer) = self.peers()
+        return (
+            self.to(self.full.at[x_peer, pl.ds(0, self.half)], x_peer, 0, 2, y_peer),
+            self.to(self.full.at[y_peer, pl.ds(self.half, self.half)], y_peer, 1, 3, x_peer),
+        )
+
+    def relay(self):
+        for slot, peer in self.peers():
+            self.to(self.full.at[peer], peer, None, slot, peer).wait_recv()
+        if self.size == 4:
+            for copy in self.relays():
+                copy.start()
+
+    def finish(self):
+        me, z, c, mp = place()
+        if self.size == 4:
+            far = 3 - mp
+            for part in (0, 1):
+                rows = self.full.at[far, pl.ds(part * self.half, self.half)]
+                self.to(rows, far, part, 0, mp).wait_recv()
+
+    def drain(self):
+        me, z, c, mp = place()
+        for slot, peer in self.peers():
+            self.to(self.own, mp, None, slot, peer).wait_send()
+        if self.size == 4:
+            for copy in self.relays():
+                copy.wait_send()
+
+
+def row_gather_sems(dp_size):
+    chips = dp_size // 2
+    return [pltpu.SemaphoreType.DMA((n,)) for n in (dp_size, chips, chips, chips)]
+
+
+def group_gather_sems(mp_size):
+    return [pltpu.SemaphoreType.DMA((max(4, mp_size - 1),)), pltpu.SemaphoreType.DMA((mp_size, 2))]
+
+
+def gelu_pair(v):
+    k0, k1 = 0.7978845608028654, 0.044715
+    square = v * v
+    t = jnp.tanh(k0 * (v + k1 * v * square))
+    half = 0.5 * (1.0 + t)
+    slope = half + 0.5 * v * (1.0 - t * t) * (k0 + 3.0 * k0 * k1 * square)
+    return v * half, slope
+
+
+def up_kernel(
+    dp_size,
+    mp_size,
+    tokens,
+    gain,
+    shift,
+    cot,
+    up_master,
+    up_bias,
+    x_out,
+    cot_out,
+    up_out,
+    hidden_out,
+    slope_out,
+    x_all,
+    up_all,
+    acc,
+    hidden,
+    slope,
+    *sems,
+):
+    chips = dp_size // 2
+    row_sems, x_sems, cot_sems = sems[0:4], sems[4:6], sems[6:8]
+    out_sem = sems[8]
+    me, z, c, mp = place()
+    rows = tokens.shape[0]
+    length = rows * mp_size
+    depth, width = up_all.shape[1], up_all.shape[2]
+
+    values = tokens[...].astype(F32)
+    centre = values - jnp.mean(values, axis=-1, keepdims=True)
+    spread = jnp.mean(centre * centre, axis=-1, keepdims=True)
+    x_all[mp] = (centre * lax.rsqrt(spread + EPSILON) * gain[...] + shift[...]).astype(BF)
+    up_all[me] = up_master[...].astype(BF)
+
+    greet(chips, mp_size)
+    weights = RowGather(chips, up_all.at[me], up_all, row_sems)
+    x_gather = GroupGather(mp_size, x_all.at[mp], x_all, x_sems)
+    cot_gather = GroupGather(mp_size, cot, cot_out, cot_sems)
+    x_gather.start()
+    weights.start()
+    own_cot = pltpu.make_async_copy(cot, cot_out.at[mp], out_sem.at[0])
+    own_cot.start()
+
+    def product(oz, first=False):
+        cols = pl.ds(pl.multiple_of(oz * (2 * depth), 2 * depth), 2 * depth)
+
+        def tile(i, carry):
+            r, n = i // (width // 512), lax.rem(i, width // 512)
+            n0 = pl.ds(pl.multiple_of(n * 512, 512), 512)
+            left = x_all[r, :, cols]
+            right = up_all[pl.ds(2 * oz, 2), :, n0].reshape(2 * depth, 512)
+            term = dot(left, right)
+            if first:
+                acc[r, :, n0] = term + up_bias[:, n0]
+            else:
+                acc[r, :, n0] += term
+            return carry
+
+        lax.fori_loop(0, mp_size * (width // 512), tile, 0)
+
+    x_gather.relay()
+    x_gather.finish()
+    weights.stage(1)
+    cot_gather.start()
+    x_copy = pltpu.make_async_copy(x_all, x_out, out_sem.at[1])
+    x_copy.start()
+    weights.wait_block(2 * z + 1 - c)
+    product(z, True)
+    for k in range(1, chips):
+        if k > 1:
+            weights.stage(k)
+        for oz, valid in ((z + k, z + k < chips), (z - k, z - k >= 0)):
+
+            @pl.when(valid)
+            def _():
+                weights.wait_block(2 * oz + 1 - c)
+                product(oz)
+
+        if k == min(2, chips - 1):
+            cot_gather.relay()
+    up_copy = pltpu.make_async_copy(up_all, up_out, out_sem.at[2])
+    up_copy.start()
+
+    def finish(i, carry):
+        r, n = i // (width // 512), lax.rem(i, width // 512)
+        n0 = pl.ds(pl.multiple_of(n * 512, 512), 512)
+        high, grad = gelu_pair(acc[r, :, n0])
+        hidden[r, :, n0] = high.astype(BF)
+        slope[r, :, n0] = grad.astype(BF)
+        return carry
+
+    lax.fori_loop(0, mp_size * (width // 512), finish, 0)
+    hidden_copy = pltpu.make_async_copy(hidden, hidden_out, out_sem.at[3])
+    slope_copy = pltpu.make_async_copy(slope, slope_out, out_sem.at[4])
+    hidden_copy.start()
+    slope_copy.start()
+    cot_gather.finish()
+    weights.drain()
+    x_gather.drain()
+    cot_gather.drain()
+    for copy in (own_cot, x_copy, up_copy, hidden_copy, slope_copy):
+        copy.wait()
+
+
+def up_stage(dp_size, mp_size, tokens, gain, shift, cot, up_master, up_bias):
+    rows, model = tokens.shape
+    depth, width = up_master.shape
+    shape = jax.ShapeDtypeStruct
+    outs = (
+        shape((mp_size, rows, model), BF),
+        shape((mp_size, rows, model), BF),
+        shape((dp_size, depth, width), BF),
+        shape((mp_size, rows, width), BF),
+        shape((mp_size, rows, width), BF),
+    )
+    return pl.pallas_call(
+        partial(up_kernel, dp_size, mp_size),
+        out_shape=outs,
+        in_specs=[VM] * 6,
+        out_specs=[ANY] * 5,
+        scratch_shapes=[
+            pltpu.VMEM((mp_size, rows, model), BF),
+            pltpu.VMEM((dp_size, depth, width), BF),
+            pltpu.VMEM((mp_size, rows, width), F32),
+            pltpu.VMEM((mp_size, rows, width), BF),
+            pltpu.VMEM((mp_size, rows, width), BF),
+            *row_gather_sems(dp_size),
+            *group_gather_sems(mp_size),
+            *group_gather_sems(mp_size),
+            pltpu.SemaphoreType.DMA((5,)),
+        ],
+        compiler_params=pltpu.CompilerParams(
+            collective_id=1, has_side_effects=True, vmem_limit_bytes=58 << 20
+        ),
+        name="up_stage",
+    )(tokens, gain.reshape(1, -1), shift.reshape(1, -1), cot, up_master, up_bias.reshape(1, -1))
 
 
 def normalize(values, gain_vec, shift_vec):
@@ -138,20 +476,25 @@
     cotangent,
 ):
     token_float = tokens.astype(jnp.float32)
-    normed_low = normalize(token_float, ln_gain, ln_bias).astype(jnp.bfloat16)
-    gathered = lax.all_gather(normed_low, "mp", axis=0, tiled=True)
+    dp_size, mp_size = lax.axis_size("dp"), lax.axis_size("mp")
+    x_all, cot_all, up_all, hidden_all, slope_all = up_stage(
+        dp_size, mp_size, tokens, ln_gain, ln_bias, cotangent, fc1_weight, fc1_bias
+    )
+    gathered = x_all.reshape(-1, x_all.shape[-1])
+    out_rows = cot_all.reshape(gathered.shape)
+    up_full = up_all.reshape(-1, up_all.shape[-1])
+    hidden_low = hidden_all.reshape(-1, up_all.shape[-1])
+    slope = slope_all.reshape(hidden_low.shape)
     group_rows = gathered.shape[0]
     masters = (
         qkv_weight.astype(jnp.bfloat16),
         dense_weight.astype(jnp.bfloat16),
-        fc1_weight.astype(jnp.bfloat16),
         fc2_weight.astype(jnp.bfloat16),
     )
-    qkv_full, dense_full, up_full, down_full = (
+    qkv_full, dense_full, down_full = (
         lax.all_gather(masters[0], "dp", axis=0, tiled=True),
         lax.all_gather(masters[1], "dp", axis=0, tiled=True),
         lax.all_gather(masters[2], "dp", axis=0, tiled=True),
-        lax.all_gather(masters[3], "dp", axis=0, tiled=True),
     )
     model_width = qkv_full.shape[0]
     local_width = qkv_full.shape[2]
@@ -181,26 +524,16 @@
     )
     attended = attended.reshape(group_rows, local_width)
     attn_part = right_product(attended, dense_full)
-    hidden_pre = jnp.dot(gathered, up_full, preferred_element_type=jnp.float32) + fc1_bias
-    hidden_low = jax.nn.gelu(hidden_pre, approximate=True).astype(jnp.bfloat16)
     mlp_part = right_product(hidden_low, down_full)
     mixed_sum = low_scatter(attn_part + mlp_part, "mp")
     output = (token_float + mixed_sum + dense_bias + fc2_bias).astype(jnp.bfloat16)
-    out_rows = lax.all_gather(cotangent, "mp", axis=0, tiled=True)
-    qkv_full, dense_full, up_full, down_full = (
-        lax.all_gather(masters[0], "dp", axis=0, tiled=True),
-        lax.all_gather(masters[1], "dp", axis=0, tiled=True),
-        lax.all_gather(masters[2], "dp", axis=0, tiled=True),
-        lax.all_gather(masters[3], "dp", axis=0, tiled=True),
-    )
     attended_grad = jnp.dot(out_rows, dense_full, preferred_element_type=jnp.float32).astype(
         jnp.bfloat16
     )
     dense_grad = rows_product(out_rows, attended)
     down_grad = rows_product(out_rows, hidden_low)
     hidden_grad = jnp.dot(out_rows, down_full, preferred_element_type=jnp.float32)
-    gelu_value, gelu_back = jax.vjp(partial(jax.nn.gelu, approximate=True), hidden_pre)
-    pre_grad = gelu_back(hidden_grad)[0].astype(jnp.bfloat16)
+    pre_grad = (hidden_grad * slope).astype(jnp.bfloat16)
     up_grad = rows_product(gathered, pre_grad)
     up_bias_grad = jnp.sum(pre_grad.astype(jnp.float32), axis=0)
     query_grad, key_grad, value_grad = lax.map(

time: 810 us -> 683 us (0.84)
  waiting for transfers between devices: 391 us -> 141 us
  Pallas kernels: 0 us -> 160 us
  matrix products: 222 us -> 198 us
  local copies, waits for them, and re-layouts: 31.7 us -> 20.9 us
    pallas_call x0 -> x1, Pallas kernels: none -> 160 us  [up_stage(): pl.pallas_call(partial(up_kernel, dp_size, mp_size), out_shape=outs, in_s...]
    all_gather x3 -> x0, waiting for transfers between devices: 104 us -> none  [the longest x1 53.8 us: body(): out_rows = lax.all_gather(cotangent, 'mp', axis=0, tiled=True)]
    all_gather x1, waiting for transfers between devices: 67.2 us -> 0.01 us  [body(): lax.all_gather(masters[0], 'dp', axis=0, tiled=True)]
    reduce_scatter x6, waiting for transfers between devices: 203 us -> 140 us  [low_scatter(): lax.psum_scatter(partial_sums.astype(jnp.bfloat16), axis, scatter_dimensi...]
    all_gather x1, waiting for transfers between devices: 16.3 us -> 0.02 us  [body(): lax.all_gather(masters[1], 'dp', axis=0, tiled=True)]
    dot_general x1 -> x0, matrix products: 14.8 us -> none  [body(): jnp.dot(gathered, up_full, preferred_element_type=jnp.float32) + fc1_bias]
    convert_element_type x1 -> x0, local copies, waits for them, and re-layouts: 8.44 us -> none  [low_scatter(): partial_sums.astype(jnp.bfloat16)]
  transfers between devices with their start and end apart: 12 -> 9, of which waited for: 7 -> 3; matrix products, arithmetic and copies ran while one was open for 40% -> 42% of each run, Pallas kernels for 0% -> 24%
where the time goes in v2:
time: 683 us; the launch traced here: 679 us
  matrix products  198 us (29%)
  Pallas kernels  160 us (23%)
  waiting for transfers between devices  141 us (21%)
  other arithmetic  73.9 us (11%)
  blocking collectives  70.3 us (10%)
  local copies, waits for them, and re-layouts  20.9 us (3%)
  between operations  15.2 us (2%)
    pallas_call x1, Pallas kernels, up_stage(): pl.pallas_call(partial(up_kernel, dp_size, mp_size), out_shape=outs, in_s...  160 us
    reduce_scatter x6, waiting for transfers between devices, low_scatter(): lax.psum_scatter(partial_sums.astype(jnp.bfloat16), axis, scatter_dimensi...  140 us
    dot_general x4, matrix products, rows_product(): lax.dot_general(left_side, right_side, (((0,), (0,)), ((), ())), preferre...  43.4 us
    psum x1, blocking collectives, body(): lax.psum((gain_grad, shift_grad, out_bias_grad), ('dp', 'mp'))  41.1 us
    dot_general x4, matrix products, right_product(): lax.dot_general(left_side, right_side, (((1,), (1,)), ((), ())), preferre...  38.9 us
    psum x1, blocking collectives, body(): lax.psum((qkv_bias_grad, up_bias_grad), 'dp')  29.2 us
    convert_element_type x1, other arithmetic, attend_backward(): score_grad = (prob_values * (prob_grad - inner_sum)).astype(jnp.bfloat16)  29 us
    dot_general x1, matrix products, attend_backward(): jnp.einsum('qhd,khd->hqk', out_grad, values_in, preferred_element_type=jn...  22.3 us
  transfers between devices with their start and end apart: 9, of which 3 were waited for; matrix products, arithmetic and copies ran while one was open for 42% of the time, Pallas kernels for 24%

profile of v2, /device:TPU:0, one launch (start us, length us, event | category | flops | bytes accessed | tf_op | source)
XLA Modules:
  0.0 678.8 jit_solution(4075139663898133024)
XLA Ops:
  7.2 2.7 copy.39
  10.0 1.8 convert_element_type.183
  11.9 1.1 convert_element_type.184
  13.7 159.9 %up_stage.1 = (bf16[4,256,2048]{2,1,0:T(8,128)(2,1)}, bf16[4,256,2048]{2,1,0:T(8,128)(2,1)}, bf16[8,256,2048]{2,1,0:T(8,128)(2,1)}, bf16[4,256,2048]{2,1,0:T(8,128)(2,1)}, bf16[4,256,2048]{2,1,0:T(8,128)(2,1)}) custom-call(bf16[256,2048]{1,0:T(8,128)(2,1)} %tokens.1, f32[1,2048]{1,0:T(1,128)} %bitcast.76, f32[1,2048]{1,0:T(1,128)} %bitcast.77, ...), custom_call_target="tpu_custom_call" | custom-call | tf_op jit(solution)/shard_map/up_stage/pallas_call | solution.py:333
  174.0 1.6 fusion.7
  175.6 10.2 %convolution_add_fusion = f32[1024,1536]{1,0:T(8,128)S(1)} fusion(bf16[1024,2048]{1,0:T(8,128)(2,1)} %bitcast.84, bf16[2048,1536]{0,1:T(8,128)(2,1)} %bitcast.80, f32[1536]{0:T(1024)S(1)} %add.145), kind=kOutput, calls=%fused_computation.20 | convolution fusion | flops 6444023808 | bytes 16783360 | tf_op jit(solution)/shard_map/dot_general | solution.py:510
  186.9 1.8 fusion.34
  188.6 2.9 copy.41
  191.6 1.5 copy.40
  193.1 2.5 slice.105
  195.6 1.8 copy.42
  197.4 1.4 slice.104
  198.9 2.1 subtract_convert_fusion.3
  201.0 14.0 %fusion.35 = (f32[8,1024]{1,0:T(8,128)S(1)}, f32[8,1024,1024]{1,2,0:T(8,128)}) fusion(bf16[1024,8,32]{0,2,1:T(8,128)(2,1)S(1)} %slice.104, bf16[1024,8,16]{0,2,1:T(8,128)(2,1)S(1)} %get-tuple-element.100, bf16[1024,8,16]{0,2,1:T(8,128)(2,1)S(1)} %get-tuple-element.101, bf16[1024,8,32]{0,2,1:T(8,128)(2,1)S(1)} %copy-done.6, ...), kind=kOutput, calls=%fused_computation.91 | convolution fusion | flops 1105190912 | bytes 36732928 | tf_op jit(solution)/shard_map/while/body/eval_jaxpr/qhd,khd->hqk/dot_general | solution.py:410
  215.0 13.2 %fusion = f32[8,1024]{1,0:T(8,128)S(1)} fusion(f32[8,1024,1024]{1,2,0:T(8,128)} %get-tuple-element.107, f32[8,1024]{1,0:T(8,128)S(1)} %get-tuple-element.106), kind=kLoop, calls=%fused_computation.6 | loop fusion | flops 16769024 | bytes 33619968 | tf_op jit(solution)/shard_map/while/body/eval_jaxpr/reduce_sum | solution.py:421
  228.2 14.5 %fusion.23 = bf16[8,64,1024]{2,1,0:T(8,128)(2,1)S(1)} fusion(bf16[1024,8,64]{0,2,1:T(8,128)(2,1)S(1)} %bitcast.70, f32[8,1024,1024]{1,2,0:T(8,128)} %get-tuple-element.107, f32[8,1024]{1,0:T(8,128)S(1)} %fusion, f32[8,1024]{1,0:T(8,128)S(1)} %get-tuple-element.106), kind=kOutput, calls=%fused_computation.51 | convolution fusion | flops 1099431936 | bytes 35717120 | tf_op jit(solution)/shard_map/while/body/eval_jaxpr/hqk,khd->qhd/dot_general | solution.py:423
  243.7 3.8 convolution_convert_fusion.2
  247.6 14.0 %bitcast_convert_fusion = bf16[2048,2048]{1,0:T(8,128)(2,1)} fusion(bf16[4,256,2048]{2,1,0:T(8,128)(2,1)} %get-tuple-element.70, bf16[4,256,2048]{2,1,0:T(8,128)(2,1)} %get-tuple-element.69), kind=kOutput, calls=%fused_computation.9 | convolution fusion | flops 8594128896 | bytes 16777216 | tf_op jit(solution)/shard_map/dot_general | solution.py:452
  261.7 5.4 convolution_convert_fusion.3
  267.1 22.3 %multiply_reduce_fusion = (f32[8,1024]{1,0:T(8,128)S(1)}, f32[8,1024,1024]{1,2,0:T(8,128)}) fusion(f32[8,1024,1024]{1,2,0:T(8,128)} %get-tuple-element.107, f32[8,1024]{1,0:T(8,128)S(1)} %log_add_fusion, bf16[1024,8,64]{0,2,1:T(8,128)(2,1)S(1)} %bitcast.68, bf16[1024,8,64]{0,2,1:T(8,128)(2,1)S(1)} %bitcast.71), kind=kOutput, calls=%fused_computation.1 | convolution fusion | flops 1098899456 | bytes 69271552 | tf_op jit(solution)/shard_map/while/body/eval_jaxpr/qhd,khd->hqk/dot_general | solution.py:433
  289.4 29.0 %multiply_convert_fusion = bf16[8,1024,1024]{1,2,0:T(8,128)(2,1)} fusion(f32[8,1024,1024]{1,2,0:T(8,128)} %get-tuple-element.109, f32[8,1024,1024]{1,2,0:T(8,128)} %get-tuple-element.107, f32[8,1024]{1,0:T(8,128)S(1)} %get-tuple-element.108, f32[8,1024]{1,0:T(8,128)S(1)} %log_add_fusion), kind=kLoop, calls=%fused_computation | loop fusion | flops 33554432 | bytes 83951616 | tf_op jit(solution)/shard_map/while/body/eval_jaxpr/convert_element_type | solution.py:435
  318.4 9.3 %multiply_bitcast_fusion.1 = f32[1024,8,64]{0,2,1:T(8,128)S(1)} fusion(bf16[8,1024,1024]{1,2,0:T(8,128)(2,1)} %multiply_convert_fusion, bf16[1024,8,32]{0,2,1:T(8,128)(2,1)} %copy-done.7, bf16[1024,8,16]{0,2,1:T(8,128)(2,1)} %copy-done.13, bf16[1024,8,16]{0,2,1:T(8,128)(2,1)} %copy-done.14), kind=kOutput, calls=%fused_computation.48 | convolution fusion | flops 1077411840 | bytes 19922944 | tf_op jit(solution)/shard_map/while/body/eval_jaxpr/hqk,khd->qhd/dot_general | solution.py:436
  328.7 12.7 %multiply_bitcast_fusion = f32[1024,8,64]{0,2,1:T(8,128)} fusion(bf16[8,1024,1024]{1,2,0:T(8,128)(2,1)} %multiply_convert_fusion, bf16[1024,8,32]{0,2,1:T(8,128)(2,1)} %slice.105, bf16[1024,8,16]{0,2,1:T(8,128)(2,1)} %copy-done.12, bf16[1024,8,16]{0,2,1:T(8,128)(2,1)S(1)} %copy-done.11), kind=kOutput, calls=%fused_computation.47 | convolution fusion | flops 1077411840 | bytes 19922944 | tf_op jit(solution)/shard_map/while/body/eval_jaxpr/hqk,qhd->khd/dot_general | solution.py:439
  341.4 1.3 slice.102
  342.8 1.5 add_convert_fusion.3
  344.3 1.2 pad_maximum_fusion.3
  345.5 13.6 %fusion.20 = bf16[8,64,1024]{2,1,0:T(8,128)(2,1)S(1)} fusion(bf16[1024,8,64]{0,2,1:T(8,128)(2,1)S(1)} %bitcast.69, f32[8,1024,1024]{1,2,0:T(8,128)} %get-tuple-element.107, f32[8,1024]{1,0:T(8,128)S(1)} %log_add_fusion), kind=kOutput, calls=%fused_computation.49 | convolution fusion | flops 1091043328 | bytes 35684352 | tf_op jit(solution)/shard_map/while/body/eval_jaxpr/hqk,qhd->khd/dot_general | solution.py:432
  359.1 3.2 convert_reduce_fusion.1
  362.4 13.4 %convert_reduce_fusion = (f32[2048]{0:T(1024)S(1)}, bf16[1024,2048]{1,0:T(8,128)(2,1)S(1)}) fusion(bf16[1024,2048]{1,0:T(8,128)(2,1)} %bitcast.91, bf16[1024,2048]{1,0:T(8,128)(2,1)} %bitcast.89, bf16[2048,2048]{1,0:T(8,128)(2,1)} %all-gather.8.cloned.1.call-done), kind=kOutput, calls=%fused_computation.14 | convolution fusion | flops 8600418304 | bytes 20979712 | tf_op jit(solution)/shard_map/dot_general | solution.py:535
  375.7 12.8 %fusion.37 = f32[1024,2048]{1,0:T(8,128)S(1)} fusion(bf16[1024,2048]{1,0:T(8,128)(2,1)S(1)} %get-tuple-element.111, bf16[2048,2048]{1,0:T(8,128)(2,1)} %bitcast.79), kind=kOutput, calls=%fused_computation.93 | convolution fusion | flops 8589934592 | bytes 20971520 | tf_op jit(solution)/shard_map/dot_general | solution.py:446
  388.6 8.4 %add_convert_fusion = bf16[1024,2048]{1,0:T(8,128)(2,1)} fusion(f32[1024,2048]{1,0:T(8,128)S(1)} %fusion.37, bf16[1024,1536]{0,1:T(8,128)(2,1)S(1)} %copy-done.5, bf16[2048,1536]{0,1:T(8,128)(2,1)S(1)} %bitcast.83), kind=kOutput, calls=%fused_computation.15 | convolution fusion | flops 6446645248 | bytes 22020096 | tf_op jit(solution)/shard_map/dot_general | solution.py:446
  397.1 13.2 %fusion.36 = f32[1024,2048]{1,0:T(8,128)S(1)} fusion(bf16[1024,2048]{1,0:T(8,128)(2,1)} %bitcast.87, bf16[2048,2048]{1,0:T(8,128)(2,1)} %all-gather.8.cloned.1.call-done), kind=kOutput, calls=%fused_computation.92 | convolution fusion | flops 8589934592 | bytes 20971520 | tf_op jit(solution)/shard_map/dot_general | solution.py:446
  410.3 4.5 add_convert_fusion.1
  414.9 11.3 %convolution_convert_fusion.1 = bf16[2048,3,512]{2,0,1:T(8,128)(2,1)} fusion(bf16[1024,2048,1]{1,0,2:T(8,128)(2,1)} %bitcast.85, bf16[3,512,1024]{2,1,0:T(8,128)(2,1)S(1)} %bitcast.75), kind=kOutput, calls=%fused_computation.19 | convolution fusion | flops 6445596672 | bytes 13631488 | tf_op jit(solution)/shard_map/dot_general | solution.py:452
  426.2 14.3 %convolution_convert_fusion = bf16[2048,2048]{1,0:T(8,128)(2,1)} fusion(bf16[1024,2048]{1,0:T(8,128)(2,1)} %bitcast.86, bf16[1024,2048]{1,0:T(8,128)(2,1)} %copy-done.28), kind=kOutput, calls=%fused_computation.17 | convolution fusion | flops 8594128896 | bytes 16777216 | tf_op jit(solution)/shard_map/dot_general | solution.py:452
  440.5 1.2 copy-done
  442.0 29.2 %all-reduce.1 = (f32[3,512]{1,0:T(4,128)}, f32[2048]{0:T(1024)}) all-reduce(f32[3,512]{1,0:T(4,128)S(1)} %reshape.282, f32[2048]{0:T(1024)S(1)} %get-tuple-element.110), channel_id=1, replica_groups=mesh['dp'=8,'mp'=4] {'dp'}, use_global_device_ids=true, to_apply=%region_15.16 | all-reduce | flops 3584 | bytes 28672 | tf_op jit(solution)/shard_map/psum | solution.py:572
  471.2 1.8 convert_element_type.202
  473.0 2.8 convert_element_type.207
  475.9 2.3 fusion.14
  478.1 2.3 fusion.19
  480.4 24.8 %reduce-scatter.7.cloned.1.call-done = bf16[256,2048]{1,0:T(8,128)(2,1)} async-done(((bf16[1024,2048]{1,0:T(8,128)(2,1)}), bf16[256,2048]{1,0:T(8,128)(2,1)}) %reduce-scatter.7.cloned.1.call-update) | async-done | bytes 1048592 | tf_op jit(solution)/shard_map/reduce_scatter | solution.py:458
  505.2 4.1 convert_reduce_fusion.4
  509.4 41.1 %all-reduce = (f32[2048]{0:T(1024)}, f32[2048]{0:T(1024)}, f32[2048]{0:T(1024)S(1)}) all-reduce(f32[2048]{0:T(1024)S(1)} %get-tuple-element.73, f32[2048]{0:T(1024)S(1)} %get-tuple-element.77, f32[2048]{0:T(1024)S(1)} %get-tuple-element.95), channel_id=1, replica_groups=mesh['dp'=8,'mp'=4] {'dp','mp'}, use_global_device_ids=true, to_apply=%region_10.11 | all-reduce | flops 6144 | bytes 49152 | tf_op jit(solution)/shard_map/psum | solution.py:569
  550.5 27.8 %reduce-scatter.11.cloned.1.call-done = bf16[256,3,512]{2,0,1:T(8,128)(2,1)} async-done(((bf16[2048,3,512]{2,0,1:T(8,128)(2,1)}), bf16[256,3,512]{2,0,1:T(8,128)(2,1)}) %reduce-scatter.11.cloned.1.call-update) | async-done | bytes 786448 | tf_op jit(solution)/shard_map/reduce_scatter | solution.py:458
  578.3 2.5 convert_element_type.199
  580.8 87.9 %reduce-scatter.15.cloned.1.call-done = bf16[256,2048]{1,0:T(8,128)(2,1)} async-done(((bf16[2048,2048]{1,0:T(8,128)(2,1)}), bf16[256,2048]{1,0:T(8,128)(2,1)}) %reduce-scatter.15.cloned.1.call-update) | async-done | bytes 1048592 | tf_op jit(solution)/shard_map/reduce_scatter | solution.py:458
  668.6 2.8 convert_element_type.204
  (100 shorter events, 4.9 us)
Async XLA Ops:
  7.2 4.7 copy-start.8
  7.2 6.5 copy-start.22
  7.2 168.4 %all-gather.4.cloned.1.call-start = ((), (), s32[]{:S(2)}) async-start(), calls=%async_computation.6 | async-start | bytes 7077888 | tf_op jit(solution)/shard_map/all_gather | solution.py:495
  10.0 251.8 %all-gather.6.cloned.1.call-start = ((), (), s32[]{:S(2)}) async-start(), calls=%async_computation.7 | async-start | bytes 2359296 | tf_op jit(solution)/shard_map/all_gather | solution.py:496
  11.8 350.5 %all-gather.8.cloned.1.call-start = ((), (), s32[]{:S(2)}) async-start(), calls=%async_computation.8 | async-start | bytes 9437184 | tf_op jit(solution)/shard_map/all_gather | solution.py:497
  13.0 458.2 %reduce-scatter.13.cloned.1.call-start = ((), (), s32[]{:S(2)}) async-start(), calls=%async_computation.12 | async-start | bytes 2359296 | tf_op jit(solution)/shard_map/reduce_scatter | solution.py:458
  174.0 24.8 %copy-start.16 = (f32[1024,16]{0,1:T(8,128)}, f32[1024,16]{0,1:T(8,128)S(1)}, u32[]{:S(2)}) copy-start(f32[1024,16]{0,1:T(8,128)S(1)} %get-tuple-element.102) | copy-start | bytes 196612
  174.0 24.8 %copy-start.18 = (f32[1024,16]{0,1:T(8,128)}, f32[1024,16]{0,1:T(8,128)S(1)}, u32[]{:S(2)}) copy-start(f32[1024,16]{0,1:T(8,128)S(1)} %get-tuple-element.103) | copy-start | bytes 196612
  193.0 35.1 %copy-start.2 = (bf16[1024,512]{0,1:T(8,128)(2,1)}, bf16[1024,512]{0,1:T(8,128)(2,1)S(1)}, u32[]{:S(2)}) copy-start(bf16[1024,512]{0,1:T(8,128)(2,1)S(1)} %copy.40) | copy-start | bytes 3145732
  197.4 3.6 copy-start.6
  197.4 3.6 copy-start.15
  198.8 16.1 %copy-start.7 = (bf16[1024,8,32]{0,2,1:T(8,128)(2,1)}, bf16[1024,8,32]{0,2,1:T(8,128)(2,1)S(1)}, u32[]{:S(2)}) copy-start(bf16[1024,8,32]{0,2,1:T(8,128)(2,1)S(1)} %slice.104) | copy-start | bytes 1572868
  200.9 14.0 %copy-start.10 = (bf16[1024,8,16]{0,2,1:T(8,128)(2,1)}, bf16[1024,8,16]{0,2,1:T(8,128)(2,1)S(1)}, u32[]{:S(2)}) copy-start(bf16[1024,8,16]{0,2,1:T(8,128)(2,1)S(1)} %get-tuple-element.91) | copy-start | bytes 786436
  200.9 14.0 %copy-start.12 = (bf16[1024,8,16]{0,2,1:T(8,128)(2,1)}, bf16[1024,8,16]{0,2,1:T(8,128)(2,1)S(1)}, u32[]{:S(2)}) copy-start(bf16[1024,8,16]{0,2,1:T(8,128)(2,1)S(1)} %get-tuple-element.92) | copy-start | bytes 786436
  200.9 14.0 %copy-start.13 = (bf16[1024,8,16]{0,2,1:T(8,128)(2,1)}, bf16[1024,8,16]{0,2,1:T(8,128)(2,1)S(1)}, u32[]{:S(2)}) copy-start(bf16[1024,8,16]{0,2,1:T(8,128)(2,1)S(1)} %get-tuple-element.100) | copy-start | bytes 786436
  201.0 14.0 %copy-start.14 = (bf16[1024,8,16]{0,2,1:T(8,128)(2,1)}, bf16[1024,8,16]{0,2,1:T(8,128)(2,1)S(1)}, u32[]{:S(2)}) copy-start(bf16[1024,8,16]{0,2,1:T(8,128)(2,1)S(1)} %get-tuple-element.101) | copy-start | bytes 786436
  228.2 15.5 %copy-start.24 = (bf16[4,256,2048]{2,1,0:T(8,128)(2,1)S(1)}, bf16[4,256,2048]{2,1,0:T(8,128)(2,1)}, u32[]{:S(2)}) copy-start(bf16[4,256,2048]{2,1,0:T(8,128)(2,1)} %get-tuple-element.70) | copy-start | bytes 12582916
  242.7 1.0 copy-start.26
  247.5 225.5 %reduce-scatter.17.cloned.1.call-start = ((), (), s32[]{:S(2)}) async-start(), calls=%async_computation.14 | async-start | bytes 9437184 | tf_op jit(solution)/shard_map/reduce_scatter | solution.py:458
  261.6 5.5 copy-start.3
  261.7 214.2 %reduce-scatter.9.cloned.1.call-start = ((), (), s32[]{:S(2)}) async-start(), calls=%async_computation.10 | async-start | bytes 5242880 | tf_op jit(solution)/shard_map/reduce_scatter | solution.py:458
  318.4 10.2 %copy-start.11 = (bf16[1024,8,16]{0,2,1:T(8,128)(2,1)S(1)}, bf16[1024,8,16]{0,2,1:T(8,128)(2,1)}, u32[]{:S(2)}) copy-start(bf16[1024,8,16]{0,2,1:T(8,128)(2,1)} %copy-done.10) | copy-start | bytes 786436
  328.7 14.1 %copy-start.17 = (f32[1024,16]{0,1:T(8,128)S(1)}, f32[1024,16]{0,1:T(8,128)}, u32[]{:S(2)}) copy-start(f32[1024,16]{0,1:T(8,128)} %copy-done.16) | copy-start | bytes 196612
  341.4 2.9 copy-start.9
  362.4 26.2 %slice-start = ((s8[6291456]{0:T(1024)(128)(4,1)}), s8[4194304]{0:T(1024)(128)(4,1)S(1)}, s32[]{:S(2)}) async-start(s8[6291456]{0:T(1024)(128)(4,1)} %bitcast.81), calls=%async_computation.15 | async-start | bytes 8388608
  375.7 12.9 %copy-start.28 = (bf16[1024,2048]{1,0:T(8,128)(2,1)}, bf16[1024,2048]{1,0:T(8,128)(2,1)S(1)}, u32[]{:S(2)}) copy-start(bf16[1024,2048]{1,0:T(8,128)(2,1)S(1)} %get-tuple-element.111) | copy-start | bytes 12582916
  375.7 12.9 %copy-start.5 = (bf16[1024,1536]{0,1:T(8,128)(2,1)S(1)}, bf16[1024,1536]{0,1:T(8,128)(2,1)}, u32[]{:S(2)}) copy-start(bf16[1024,1536]{0,1:T(8,128)(2,1)} %get-tuple-element.84) | copy-start | bytes 9437188
  375.7 12.9 %slice-start.1 = ((s8[6291456]{0:T(1024)(128)(4,1)}), s8[2097152]{0:T(1024)(128)(4,1)S(1)}, s32[]{:S(2)}) async-start(s8[6291456]{0:T(1024)(128)(4,1)} %bitcast.81), calls=%async_computation.16 | async-start | bytes 4194304
  397.1 108.1 %reduce-scatter.7.cloned.1.call-start = ((), (), s32[]{:S(2)}) async-start(), calls=%async_computation.9 | async-start | bytes 5242880 | tf_op jit(solution)/shard_map/reduce_scatter | solution.py:458
  397.1 13.2 %copy-start.25 = (bf16[2048,512]{1,0:T(8,128)(2,1)S(1)}, bf16[2048,512]{1,0:T(8,128)(2,1)}, u32[]{:S(2)}) copy-start(bf16[2048,512]{1,0:T(8,128)(2,1)} %all-gather.6.cloned.1.call-done) | copy-start | bytes 6291460
  397.1 13.2 %copy-start.27 = (bf16[8,64,1024]{2,1,0:T(8,128)(2,1)S(1)}, bf16[8,64,1024]{2,1,0:T(8,128)(2,1)}, u32[]{:S(2)}) copy-start(bf16[8,64,1024]{2,1,0:T(8,128)(2,1)} %copy-done.26) | copy-start | bytes 3145732
  414.8 163.5 %reduce-scatter.11.cloned.1.call-start = ((), (), s32[]{:S(2)}) async-start(), calls=%async_computation.11 | async-start | bytes 7077888 | tf_op jit(solution)/shard_map/reduce_scatter | solution.py:458
  426.2 242.5 %reduce-scatter.15.cloned.1.call-start = ((), (), s32[]{:S(2)}) async-start(), calls=%async_computation.13 | async-start | bytes 9437184 | tf_op jit(solution)/shard_map/reduce_scatter | solution.py:458
  440.5 1.3 copy-start
  441.8 34.1 %copy-start.19 = (f32[2048]{0:T(1024)S(1)}, f32[2048]{0:T(1024)}, u32[]{:S(2)}) copy-start(f32[2048]{0:T(1024)} %param.14) | copy-start | bytes 24580
  442.0 63.2 %copy-start.4 = (bf16[256,2048]{1,0:T(8,128)(2,1)S(1)}, bf16[256,2048]{1,0:T(8,128)(2,1)}, u32[]{:S(2)}) copy-start(bf16[256,2048]{1,0:T(8,128)(2,1)} %cot.1) | copy-start | bytes 3145732
  442.0 63.2 %copy-start.20 = (f32[2048]{0:T(1024)S(1)}, f32[2048]{0:T(1024)}, u32[]{:S(2)}) copy-start(f32[2048]{0:T(1024)} %param.23) | copy-start | bytes 24580
  442.0 63.2 %copy-start.21 = (f32[2048]{0:T(1024)S(1)}, f32[2048]{0:T(1024)}, u32[]{:S(2)}) copy-start(f32[2048]{0:T(1024)} %param.19) | copy-start | bytes 24580
  475.9 29.4 %copy-start.1 = (bf16[256,2048]{1,0:T(8,128)(2,1)S(1)}, bf16[256,2048]{1,0:T(8,128)(2,1)}, u32[]{:S(2)}) copy-start(bf16[256,2048]{1,0:T(8,128)(2,1)} %reduce-scatter.9.cloned.1.call-done) | copy-start | bytes 3145732
  550.5 121.6 %copy-start.23 = (f32[2048]{0:T(1024)}, f32[2048]{0:T(1024)S(1)}, u32[]{:S(2)}) copy-start(f32[2048]{0:T(1024)S(1)} %get-tuple-element.137) | copy-start | bytes 24580
Sparse Core Ops, SparseCore 0:
  10.2 102.5 all-gather.3
  114.4 35.1 all-gather.5
  151.8 81.9 all-gather.7
  247.6 35.5 reduce-scatter.12
  285.4 88.0 reduce-scatter.16
  397.2 52.3 reduce-scatter.8
  452.6 52.5 reduce-scatter.6
  507.5 70.7 reduce-scatter.10
  580.6 88.0 reduce-scatter.14

commit v3 on v2

--- a/solution.py
+++ b/solution.py
@@ -360,86 +360,225 @@
     return scaled * gain_vec + shift_vec
 
 
-def rotary_tables(row_count):
+def attention_kernel(start, q_in, k_in, v_in, out_grad, rot, out, q_grad, k_grad, v_grad, q_sum, k_sum, v_sum, bias, k_acc, v_acc):
+    length = q_in.shape[0]
+    block = 256
+    blocks = length // block
+
+    @pl.when(pl.program_id(0) == 0)
+    def _():
+        first = start[0]
+        for i in range(blocks):
+            high = min(length, block * (i + 2)) - block * i
+            keys = block * i + lax.broadcasted_iota(jnp.int32, (high, block), 0)
+            places = block * i + lax.broadcasted_iota(jnp.int32, (high, block), 1)
+            inside = (keys >= first) & (keys < first + PIECE) & (places >= first) & (places < first + PIECE)
+            bias[i, :high] = jnp.where((keys <= places) | inside, 0.0, NEGATIVE)
+
+    def turn(values, sign):
+        return (
+            values * rot[0]
+            + sign * (pltpu.roll(values, 128 - ROT_DIM // 2, 1) * rot[1] + pltpu.roll(values, ROT_DIM // 2, 1) * rot[2])
+        )
+
+    scale = HEAD_DIM ** (-0.5)
+    q_low = (turn(q_in[...], 1.0).astype(BF).astype(F32) * scale).astype(BF)
+    k_low = turn(k_in[...], 1.0).astype(BF)
+    v_low = v_in[...].astype(BF)
+    grad = out_grad[...]
+    k_flip, v_flip = k_low.T, v_low.T
+    lane = lax.broadcasted_iota(jnp.int32, (length, 128), 1) < HEAD_DIM
+    row = lax.broadcasted_iota(jnp.int32, (128, length), 0) < HEAD_DIM
+    zero = jnp.zeros((), BF)
+    k_acc[...] = jnp.zeros_like(k_acc)
+    v_acc[...] = jnp.zeros_like(v_acc)
+    heads = []
+    for h in range(2):
+        lanes, rows = (lane, row) if h == 0 else (~lane, ~row)
+        heads.append(
+            (
+                jnp.where(lanes, q_low, zero),
+                jnp.where(lanes, k_low, zero),
+                jnp.where(lanes, v_low, zero),
+                jnp.where(lanes, grad, zero),
+                jnp.where(rows, k_flip, zero),
+                jnp.where(rows, v_flip, zero),
+            )
+        )
+    for i in range(blocks):
+        here = slice(block * i, block * (i + 1))
+        stop = min(length, block * (i + 2))
+        parts = [(0, block * i)] if i else []
+        parts.append((block * i, stop))
+        out_flip = jnp.zeros((128, block), F32)
+        q_flip = jnp.zeros((128, block), F32)
+        for q_h, k_h, v_h, grad_h, kt_h, vt_h in heads:
+            scores = [dot(k_h[a:b], q_low[here], 1, 1) for a, b in parts]
+            scores[-1] = scores[-1] + bias[i, : stop - block * i]
+            top = scores[-1].max(0, keepdims=True)
+            for s in scores[:-1]:
+                top = jnp.maximum(top, s.max(0, keepdims=True))
+            expo = [jnp.exp(s - top) for s in scores]
+            total = expo[0].sum(0, keepdims=True)
+            for e in expo[1:]:
+                total = total + e.sum(0, keepdims=True)
+            share = 1.0 / total
+            probs = [e * share for e in expo]
+            grads = [dot(v_h[a:b], grad[here], 1, 1) for a, b in parts]
+            inner = (probs[0] * grads[0]).sum(0, keepdims=True)
+            for p, g in zip(probs[1:], grads[1:]):
+                inner = inner + (p * g).sum(0, keepdims=True)
+            for (a, b), p, g in zip(parts, probs, grads):
+                p_low = p.astype(BF)
+                s_grad = (p * (g - inner)).astype(BF)
+                out_flip = out_flip + dot(vt_h[:, a:b], p_low)
+                q_flip = q_flip + dot(kt_h[:, a:b], s_grad)
+                v_acc[a:b] += dot(p_low, grad_h[here])
+                k_acc[a:b] += dot(s_grad, q_h[here])
+        out[here] = out_flip.T.astype(BF)
+        q_rows = q_flip.T * scale
+        q_back = (
+            q_rows * rot[0, here]
+            - pltpu.roll(q_rows, 128 - ROT_DIM // 2, 1) * rot[1, here]
+            - pltpu.roll(q_rows, ROT_DIM // 2, 1) * rot[2, here]
+        )
+        q_grad[here] = q_back.astype(BF)
+    k_grad[...] = turn(k_acc[...], -1.0).astype(BF)
+    v_grad[...] = v_acc[...].astype(BF)
+    for total_out, rows_out in ((q_sum, q_grad), (k_sum, k_grad), (v_sum, v_grad)):
+        total_out[...] = jnp.sum(rows_out[...].astype(F32), axis=0, keepdims=True)
+
+
+def rotary_lanes(length):
     half_dim = ROT_DIM // 2
-    places = (jnp.arange(row_count) % LENGTH).astype(jnp.float32)
-    frequency = 10000.0 ** (-jnp.arange(half_dim).astype(jnp.float32) * 2.0 / ROT_DIM)
-    angles = places[:, None] * frequency[None, :]
-    return (jnp.cos(angles), jnp.sin(angles))
-
-
-def rotate(values, cosine_table, sine_table):
-    half_dim = ROT_DIM // 2
-    first_part = values[..., :half_dim]
-    second_part = values[..., half_dim:ROT_DIM]
-    cosine_row = cosine_table[:, None, :]
-    sine_row = sine_table[:, None, :]
-    return jnp.concatenate(
+    lane = jnp.arange(128) % HEAD_DIM
+    frequency = 10000.0 ** (-jnp.arange(half_dim).astype(F32) * 2.0 / ROT_DIM)
+    angles = jnp.arange(length).astype(F32)[:, None] * frequency[None, :]
+    cosine = jnp.tile(jnp.cos(angles), (1, 128 // half_dim))
+    sine = jnp.tile(jnp.sin(angles), (1, 128 // half_dim))
+    turned = lane[None, :] < ROT_DIM
+    first = lane[None, :] < half_dim
+    return jnp.stack(
         [
-            first_part * cosine_row - second_part * sine_row,
-            second_part * cosine_row + first_part * sine_row,
-            values[..., ROT_DIM:],
+            jnp.where(turned, cosine, 1.0),
+            jnp.where(first, -sine, 0.0),
+            jnp.where(turned & ~first, sine, 0.0),
+        ]
+    )
+
+
+def attention(projected, out_grad, start):
+    length, width = out_grad.shape
+    pairs = width // 128
+    shape = jax.ShapeDtypeStruct
+
+    def rows(shift):
+        return pl.BlockSpec((length, 128), lambda i: (0, i + shift))
+
+    total = pl.BlockSpec((1, 128), lambda i: (0, i))
+    return pl.pallas_call(
+        attention_kernel,
+        grid=(pairs,),
+        in_specs=[
+            pl.BlockSpec(memory_space=pltpu.SMEM),
+            rows(0),
+            rows(pairs),
+            rows(2 * pairs),
+            rows(0),
+            pl.BlockSpec((3, length, 128), lambda i: (0, 0, 0)),
         ],
-        axis=-1,
-    )
-
-
-def unrotate(gradient, cosine_table, sine_table):
-    half_dim = ROT_DIM // 2
-    first_part = gradient[..., :half_dim]
-    second_part = gradient[..., half_dim:ROT_DIM]
-    cosine_row = cosine_table[:, None, :]
-    sine_row = sine_table[:, None, :]
-    return jnp.concatenate(
-        [
-            first_part * cosine_row + second_part * sine_row,
-            second_part * cosine_row - first_part * sine_row,
-            gradient[..., ROT_DIM:],
+        out_specs=[rows(0)] * 4 + [total] * 3,
+        out_shape=[shape((length, width), BF)] * 4 + [shape((1, width), F32)] * 3,
+        scratch_shapes=[
+            pltpu.VMEM((length // 256, 512, 256), F32),
+            pltpu.VMEM((length, 128), F32),
+            pltpu.VMEM((length, 128), F32),
         ],
-        axis=-1,
-    )
-
-
-def allowed_mask(piece_start):
-    places = jnp.arange(LENGTH)
-    inside = (places >= piece_start) & (places < piece_start + PIECE)
-    return (places[None, :] <= places[:, None]) | inside[:, None] & inside[None, :]
-
-
-def masked_scores(queries, key_rows, piece_start):
-    scores = jnp.einsum(
-        "qhd,khd->hqk", queries, key_rows, preferred_element_type=jnp.float32
-    ) * HEAD_DIM ** (-0.5)
-    return jnp.where(allowed_mask(piece_start)[None], scores, NEGATIVE)
-
-
-def attend_forward(members):
-    queries, key_rows, values_in, piece_start = members
-    masked = masked_scores(queries, key_rows, piece_start)
-    row_max = jnp.max(masked, axis=-1, keepdims=True)
-    expo_values = jnp.exp(masked - row_max)
-    row_total = jnp.sum(expo_values, axis=-1, keepdims=True)
-    prob_low = (expo_values / row_total).astype(jnp.bfloat16)
-    attended = jnp.einsum("hqk,khd->qhd", prob_low, values_in, preferred_element_type=jnp.float32)
-    return (attended.astype(jnp.bfloat16), (row_max + jnp.log(row_total))[..., 0])
-
-
-def attend_backward(members):
-    queries, key_rows, values_in, piece_start, logsum, out_grad = members
-    masked = masked_scores(queries, key_rows, piece_start)
-    prob_values = jnp.exp(masked - logsum[..., None])
-    prob_low = prob_values.astype(jnp.bfloat16)
-    value_grad = jnp.einsum("hqk,qhd->khd", prob_low, out_grad, preferred_element_type=jnp.float32)
-    prob_grad = jnp.einsum("qhd,khd->hqk", out_grad, values_in, preferred_element_type=jnp.float32)
-    inner_sum = jnp.sum(prob_values * prob_grad, axis=-1, keepdims=True)
-    score_grad = (prob_values * (prob_grad - inner_sum)).astype(jnp.bfloat16)
-    query_grad = jnp.einsum(
-        "hqk,khd->qhd", score_grad, key_rows, preferred_element_type=jnp.float32
-    ) * HEAD_DIM ** (-0.5)
-    key_grad = jnp.einsum(
-        "hqk,qhd->khd", score_grad, queries, preferred_element_type=jnp.float32
-    ) * HEAD_DIM ** (-0.5)
-    return (query_grad, key_grad, value_grad)
+        compiler_params=pltpu.CompilerParams(vmem_limit_bytes=50 << 20),
+        cost_estimate=pl.CostEstimate(
+            flops=16 * length * length * width, bytes_accessed=16 * length * width, transcendentals=length * length * width // 64
+        ),
+        name="attention",
+    )(start, projected, projected, projected, out_grad, rotary_lanes(length))
+
+
+def sums_kernel(dp_size, mp_size, every, group, every_out, group_out, first, second, send_1, recv_1, send_2, recv_2):
+    me, z, c, mp = place()
+    split = every.shape[0]
+    bar = pltpu.get_barrier_semaphore()
+    for k in range(1, mp_size):
+        pl.semaphore_signal(bar, 1, device_id=(me, lax.rem(mp + k, mp_size)), device_id_type=MESH)
+    for k in range(1, dp_size):
+        pl.semaphore_signal(bar, 1, device_id=(lax.rem(me + k, dp_size), mp), device_id_type=MESH)
+    pl.semaphore_wait(bar, mp_size + dp_size - 2)
+
+    def copy_1(k):
+        return remote(
+            every, first.at[mp], send_1.at[k], recv_1.at[mp], me, lax.rem(mp + k, mp_size)
+        )
+
+    def copy_2(k):
+        return remote(
+            second.at[me], second.at[me], send_2.at[k], recv_2.at[me], lax.rem(me + k, dp_size), mp
+        )
+
+    for k in range(1, mp_size):
+        copy_1(k).start()
+    first[mp] = every[...]
+    second[me, split:] = group[...]
+    for k in range(1, mp_size):
+        origin = lax.rem(mp + k, mp_size)
+        remote(every, first.at[origin], send_1.at[0], recv_1.at[origin], me, origin).wait_recv()
+    total = first[0]
+    for k in range(1, mp_size):
+        total = total + first[k]
+    second[me, :split] = total
+    for k in range(1, dp_size):
+        copy_2(k).start()
+    for k in range(1, dp_size):
+        origin = lax.rem(me + k, dp_size)
+        remote(second.at[origin], second.at[origin], send_2.at[0], recv_2.at[origin], origin, mp).wait_recv()
+    total = second[0]
+    for k in range(1, dp_size):
+        total = total + second[k]
+    every_out[...] = total[:split]
+    group_out[...] = total[split:]
+    for k in range(1, mp_size):
+        copy_1(k).wait_send()
+    for k in range(1, dp_size):
+        copy_2(k).wait_send()
+
+
+def tiled(vectors):
+    flat = jnp.concatenate([v.reshape(-1) for v in vectors])
+    return jnp.pad(flat, (0, -flat.shape[0] % 1024)).reshape(-1, 128)
+
+
+def untiled(table, vectors):
+    flat, place_at, parts = table.reshape(-1), 0, []
+    for v in vectors:
+        parts.append(flat[place_at : place_at + v.size].reshape(v.shape))
+        place_at += v.size
+    return parts
+
+
+def all_sums(dp_size, mp_size, every, group):
+    one, two = tiled(every), tiled(group)
+    shape = jax.ShapeDtypeStruct
+    totals = pl.pallas_call(
+        partial(sums_kernel, dp_size, mp_size),
+        out_shape=(shape(one.shape, F32), shape(two.shape, F32)),
+        in_specs=[VM] * 2,
+        out_specs=[VM] * 2,
+        scratch_shapes=[
+            pltpu.VMEM((mp_size, *one.shape), F32),
+            pltpu.VMEM((dp_size, one.shape[0] + two.shape[0], 128), F32),
+            *[pltpu.SemaphoreType.DMA((n,)) for n in (mp_size, mp_size, dp_size, dp_size)],
+        ],
+        compiler_params=pltpu.CompilerParams(collective_id=2, has_side_effects=True),
+        name="all_sums",
+    )(one, two)
+    return untiled(totals[0], every), untiled(totals[1], group)
 
 
 def right_product(left_side, right_side):
@@ -485,7 +624,6 @@
     up_full = up_all.reshape(-1, up_all.shape[-1])
     hidden_low = hidden_all.reshape(-1, up_all.shape[-1])
     slope = slope_all.reshape(hidden_low.shape)
-    group_rows = gathered.shape[0]
     masters = (
         qkv_weight.astype(jnp.bfloat16),
         dense_weight.astype(jnp.bfloat16),
@@ -498,66 +636,28 @@
     )
     model_width = qkv_full.shape[0]
     local_width = qkv_full.shape[2]
-    heads_local = local_width // HEAD_DIM
-    seq_count = group_rows // LENGTH
-
-    def to_sequences(tensor):
-        return tensor.reshape(seq_count, LENGTH, heads_local, HEAD_DIM)
-
-    def to_heads(tensor):
-        return tensor.reshape(group_rows, heads_local, HEAD_DIM)
-
     projected = jnp.dot(
         gathered, qkv_full.reshape(model_width, 3 * local_width), preferred_element_type=jnp.float32
     ) + qkv_bias.reshape(3 * local_width)
-    cosine_table, sine_table = rotary_tables(group_rows)
-    queries = rotate(to_heads(projected[:, :local_width]), cosine_table, sine_table).astype(
+    attended_grad = jnp.dot(out_rows, dense_full, preferred_element_type=jnp.float32).astype(
         jnp.bfloat16
     )
-    key_rows = rotate(
-        to_heads(projected[:, local_width : 2 * local_width]), cosine_table, sine_table
-    ).astype(jnp.bfloat16)
-    values_in = to_heads(projected[:, 2 * local_width :]).astype(jnp.bfloat16)
-    attended, logsum = lax.map(
-        attend_forward,
-        (to_sequences(queries), to_sequences(key_rows), to_sequences(values_in), starts),
-    )
-    attended = attended.reshape(group_rows, local_width)
+    attended, query_grad, key_grad, value_grad, query_sum, key_sum, value_sum = attention(
+        projected, attended_grad, starts
+    )
     attn_part = right_product(attended, dense_full)
     mlp_part = right_product(hidden_low, down_full)
     mixed_sum = low_scatter(attn_part + mlp_part, "mp")
     output = (token_float + mixed_sum + dense_bias + fc2_bias).astype(jnp.bfloat16)
-    attended_grad = jnp.dot(out_rows, dense_full, preferred_element_type=jnp.float32).astype(
-        jnp.bfloat16
-    )
     dense_grad = rows_product(out_rows, attended)
     down_grad = rows_product(out_rows, hidden_low)
     hidden_grad = jnp.dot(out_rows, down_full, preferred_element_type=jnp.float32)
     pre_grad = (hidden_grad * slope).astype(jnp.bfloat16)
     up_grad = rows_product(gathered, pre_grad)
     up_bias_grad = jnp.sum(pre_grad.astype(jnp.float32), axis=0)
-    query_grad, key_grad, value_grad = lax.map(
-        attend_backward,
-        (
-            to_sequences(queries),
-            to_sequences(key_rows),
-            to_sequences(values_in),
-            starts,
-            logsum,
-            to_sequences(attended_grad),
-        ),
-    )
-    query_grad = unrotate(to_heads(query_grad), cosine_table, sine_table).reshape(
-        group_rows, local_width
-    )
-    key_grad = unrotate(to_heads(key_grad), cosine_table, sine_table).reshape(
-        group_rows, local_width
-    )
-    projected_grad = jnp.concatenate(
-        [query_grad, key_grad, value_grad.reshape(group_rows, local_width)], axis=1
-    ).astype(jnp.bfloat16)
+    projected_grad = jnp.concatenate([query_grad, key_grad, value_grad], axis=1)
     qkv_grad = rows_product(gathered, projected_grad).reshape(model_width, 3, local_width)
-    qkv_bias_grad = jnp.sum(projected_grad.astype(jnp.float32), axis=0).reshape(3, local_width)
+    qkv_bias_grad = jnp.concatenate([query_sum, key_sum, value_sum], axis=0)
     attn_input = right_product(projected_grad, qkv_full.reshape(model_width, 3 * local_width))
     mlp_input = right_product(pre_grad, up_full)
     normed_grad = low_scatter(attn_input + mlp_input, "mp")
@@ -566,10 +666,9 @@
     cot_float = cotangent.astype(jnp.float32)
     input_grad = (cot_float + token_grad).astype(jnp.bfloat16)
     out_bias_grad = jnp.sum(cot_float, axis=0)
-    gain_total, shift_total, bias_total = lax.psum(
-        (gain_grad, shift_grad, out_bias_grad), ("dp", "mp")
-    )
-    qkv_bias_total, up_bias_total = lax.psum((qkv_bias_grad, up_bias_grad), "dp")
+    (gain_total, shift_total, bias_total), (qkv_bias_total, up_bias_total) = all_sums(
+        dp_size, mp_size, (gain_grad, shift_grad, out_bias_grad), (qkv_bias_grad, up_bias_grad)
+    )
     qkv_share, dense_share, up_share, down_share = (
         low_scatter(qkv_grad, "dp"),
         low_scatter(dense_grad, "dp"),

time: 683 us -> 659 us (0.965)
  waiting for transfers between devices: 141 us -> 262 us
  matrix products: 198 us -> 115 us
  blocking collectives: 70.3 us -> 0 us
  Pallas kernels: 160 us -> 219 us
  other arithmetic: 73.9 us -> 24.8 us
    reduce_scatter x6, waiting for transfers between devices: 140 us -> 262 us  [low_scatter(): lax.psum_scatter(partial_sums.astype(jnp.bfloat16), axis, scatter_dimensi...]
    dot_general x6 -> x0, matrix products: 86.4 us -> none  [the longest x1 22.3 us: attend_backward(): jnp.einsum('qhd,khd->hqk', out_grad, values_in, preferred_element_type=jn...]
    psum x2 -> x0, blocking collectives: 70.3 us -> none  [the longest x1 41.1 us: body(): lax.psum((gain_grad, shift_grad, out_bias_grad), ('dp', 'mp'))]
    pallas_call x0 -> x2, Pallas kernels: none -> 58 us  [the longest x1 38.3 us: attention(): pl.pallas_call(attention_kernel, grid=(pairs,), in_specs=[pl.BlockSpec(me...]
    convert_element_type x2 -> x1, other arithmetic: 29 us -> 0.01 us  [rotary_lanes(): angles = jnp.arange(length).astype(F32)[:, None] * frequency[None, :]]
    reduce_sum x2 -> x0, other arithmetic: 16.4 us -> none  [the longest x1 13.2 us: attend_forward(): row_total = jnp.sum(expo_values, axis=-1, keepdims=True)]
    slice x9 -> x3, local copies, waits for them, and re-layouts: 15.2 us -> 3.35 us  [untiled(): parts.append(flat[place_at:place_at + v.size].reshape(v.shape))]
  transfers between devices with their start and end apart: 9 -> 9, of which waited for: 3 -> 5; matrix products, arithmetic and copies ran while one was open for 42% -> 23% of each run, Pallas kernels for 24% -> 34%
where the time goes in v3:
time: 659 us; the launch traced here: 652 us
  waiting for transfers between devices  262 us (40%)
  Pallas kernels  219 us (33%)
  matrix products  115 us (17%)
  other arithmetic  24.8 us (4%)
  local copies, waits for them, and re-layouts  15.3 us (2%)
  between operations  15.2 us (2%)
    reduce_scatter x6, waiting for transfers between devices, low_scatter(): lax.psum_scatter(partial_sums.astype(jnp.bfloat16), axis, scatter_dimensi...  262 us
    pallas_call x1, Pallas kernels, up_stage(): pl.pallas_call(partial(up_kernel, dp_size, mp_size), out_shape=outs, in_s...  162 us
    dot_general x4, matrix products, rows_product(): lax.dot_general(left_side, right_side, (((0,), (0,)), ((), ())), preferre...  43.5 us
    dot_general x4, matrix products, right_product(): lax.dot_general(left_side, right_side, (((1,), (1,)), ((), ())), preferre...  40.5 us
    pallas_call x1, Pallas kernels, attention(): pl.pallas_call(attention_kernel, grid=(pairs,), in_specs=[pl.BlockSpec(me...  38.3 us
    pallas_call x1, Pallas kernels, all_sums(): pl.pallas_call(partial(sums_kernel, dp_size, mp_size), out_shape=(shape(o...  19.7 us
    dot_general x1, matrix products, body(): jnp.dot(out_rows, down_full, preferred_element_type=jnp.float32)  13.4 us
  transfers between devices with their start and end apart: 9, of which 5 were waited for; matrix products, arithmetic and copies ran while one was open for 23% of the time, Pallas kernels for 34%

profile of v3, /device:TPU:0, one launch (start us, length us, event | category | flops | bytes accessed | tf_op | source)
XLA Modules:
  0.0 652.5 jit_solution(18069008570398505302)
XLA Ops:
  7.2 1.9 convert_element_type.98
  9.2 2.6 copy.28
  11.9 1.1 convert_element_type.102
  13.0 0.0 reduce-scatter.13.cloned.1.call-start
  13.8 0.3 multiply_cosine_fusion
  14.1 0.2 copy.29
  14.4 0.2 copy.30
  14.6 161.5 %up_stage.1 = (bf16[4,256,2048]{2,1,0:T(8,128)(2,1)}, bf16[4,256,2048]{2,1,0:T(8,128)(2,1)}, bf16[8,256,2048]{2,1,0:T(8,128)(2,1)}, bf16[4,256,2048]{2,1,0:T(8,128)(2,1)}, bf16[4,256,2048]{2,1,0:T(8,128)(2,1)}) custom-call(bf16[256,2048]{1,0:T(8,128)(2,1)} %tokens.1, f32[1,2048]{1,0:T(1,128)} %bitcast.56, f32[1,2048]{1,0:T(1,128)} %bitcast.60, ...), custom_call_target="tpu_custom_call" | custom-call | tf_op jit(solution)/shard_map/up_stage/pallas_call | solution.py:333
  176.2 0.1 negate_select_fusion
  176.3 1.2 pad_maximum_fusion.rot
  177.5 6.2 convolution_convert_fusion.3.out_grad
  183.7 11.8 %convolution_add_fusion.q_in.k_in.v_in = f32[1024,1536]{1,0:T(8,128)} fusion(bf16[1024,2048]{1,0:T(8,128)(2,1)} %bitcast.67, bf16[2048,1536]{0,1:T(8,128)(2,1)} %bitcast.63, f32[1536]{0:T(1024)S(1)} %add.85), kind=kOutput, calls=%fused_computation.8 | convolution fusion | flops 6444023808 | bytes 16783360 | tf_op jit(solution)/shard_map/dot_general | solution.py:639
  195.5 38.3 %attention.1 = (bf16[1024,512]{1,0:T(8,128)(2,1)S(1)}, bf16[1024,512]{1,0:T(8,128)(2,1)S(1)}, bf16[1024,512]{1,0:T(8,128)(2,1)S(1)}, bf16[1024,512]{1,0:T(8,128)...) custom-call(s32[1]{0:T(128)S(6)} %copy.41.start, ...), custom_call_target="tpu_custom_call" | custom-call | flops 8589934592 | bytes 8388608 | tf_op jit(solution)/shard_map/attention/pallas_call | solution.py:479
  233.8 3.7 convolution_convert_fusion.2
  237.6 14.2 %bitcast_convert_fusion = bf16[2048,2048]{1,0:T(8,128)(2,1)} fusion(bf16[4,256,2048]{2,1,0:T(8,128)(2,1)} %get-tuple-element.27, bf16[4,256,2048]{2,1,0:T(8,128)(2,1)} %get-tuple-element.29), kind=kOutput, calls=%fused_computation | convolution fusion | flops 8594128896 | bytes 16777216 | tf_op jit(solution)/shard_map/dot_general | solution.py:591
  251.9 1.1 constant_dynamic-update-slice_fusion.2
  252.9 1.1 constant_dynamic-update-slice_fusion.1
  254.1 1.1 constant_dynamic-update-slice_fusion
  255.1 13.4 %convert_reduce_fusion = (f32[2048]{0:T(1024)S(1)}, bf16[1024,2048]{1,0:T(8,128)(2,1)S(1)}) fusion(bf16[1024,2048]{1,0:T(8,128)(2,1)} %bitcast.74, bf16[1024,2048]{1,0:T(8,128)(2,1)} %bitcast.72, bf16[2048,2048]{1,0:T(8,128)(2,1)} %all-gather.8.cloned.1.call-done), kind=kOutput, calls=%fused_computation.3 | convolution fusion | flops 8600418304 | bytes 20979712 | tf_op jit(solution)/shard_map/dot_general | solution.py:654
  268.5 12.9 %fusion.17 = f32[1024,2048]{1,0:T(8,128)S(1)} fusion(bf16[1024,2048]{1,0:T(8,128)(2,1)S(1)} %get-tuple-element.58, bf16[2048,2048]{1,0:T(8,128)(2,1)} %bitcast.62), kind=kOutput, calls=%fused_computation.63 | convolution fusion | flops 8589934592 | bytes 20971520 | tf_op jit(solution)/shard_map/dot_general | solution.py:585
  281.4 10.1 %add_convert_fusion = bf16[1024,2048]{1,0:T(8,128)(2,1)} fusion(f32[1024,2048]{1,0:T(8,128)S(1)} %fusion.17, bf16[1024,1536]{1,0:T(8,128)(2,1)} %constant_dynamic-update-slice_fusion, bf16[2048,1536]{0,1:T(8,128)(2,1)S(1)} %bitcast.66), kind=kOutput, calls=%fused_computation.4 | convolution fusion | flops 6446645248 | bytes 22020096 | tf_op jit(solution)/shard_map/dot_general | solution.py:585
  291.6 13.0 %fusion.16 = f32[1024,2048]{1,0:T(8,128)S(1)} fusion(bf16[1024,2048]{1,0:T(8,128)(2,1)} %bitcast.70, bf16[2048,2048]{1,0:T(8,128)(2,1)} %all-gather.8.cloned.1.call-done), kind=kOutput, calls=%fused_computation.62 | convolution fusion | flops 8589934592 | bytes 20971520 | tf_op jit(solution)/shard_map/dot_general | solution.py:585
  304.6 4.5 add_convert_fusion.1
  309.2 3.2 copy.32
  312.4 11.2 %convolution_convert_fusion.1 = bf16[2048,3,512]{2,0,1:T(8,128)(2,1)} fusion(bf16[1024,2048,1]{1,0,2:T(8,128)(2,1)} %bitcast.68, bf16[3,512,1024]{2,1,0:T(8,128)(2,1)S(1)} %bitcast.53), kind=kOutput, calls=%fused_computation.7 | convolution fusion | flops 6445596672 | bytes 13631488 | tf_op jit(solution)/shard_map/dot_general | solution.py:591
  323.6 14.4 %convolution_convert_fusion = bf16[2048,2048]{1,0:T(8,128)(2,1)} fusion(bf16[1024,2048]{1,0:T(8,128)(2,1)} %bitcast.69, bf16[1024,2048]{1,0:T(8,128)(2,1)} %copy-done.12), kind=kOutput, calls=%fused_computation.6 | convolution fusion | flops 8594128896 | bytes 16777216 | tf_op jit(solution)/shard_map/dot_general | solution.py:591
  338.0 1.2 copy-done
  339.2 0.2 convert_reduce_fusion.2
  339.5 0.6 fusion.14.group
  340.2 1.8 convert_element_type.117
  342.0 22.2 %reduce-scatter.17.cloned.1.call-done = bf16[256,2048]{1,0:T(8,128)(2,1)} async-done(((bf16[2048,2048]{1,0:T(8,128)(2,1)}), bf16[256,2048]{1,0:T(8,128)(2,1)}) %reduce-scatter.17.cloned.1.call-update) | async-done | bytes 1048592 | tf_op jit(solution)/shard_map/reduce_scatter | solution.py:597
  364.2 2.8 convert_element_type.121
  366.9 51.1 %reduce-scatter.9.cloned.1.call-done = bf16[256,2048]{1,0:T(8,128)(2,1)} async-done(((bf16[1024,2048]{1,0:T(8,128)(2,1)}), bf16[256,2048]{1,0:T(8,128)(2,1)}) %reduce-scatter.9.cloned.1.call-update) | async-done | bytes 1048592 | tf_op jit(solution)/shard_map/reduce_scatter | solution.py:597
  418.1 2.2 fusion.7
  420.3 2.3 fusion.12
  422.6 51.0 %reduce-scatter.7.cloned.1.call-done = bf16[256,2048]{1,0:T(8,128)(2,1)} async-done(((bf16[1024,2048]{1,0:T(8,128)(2,1)}), bf16[256,2048]{1,0:T(8,128)(2,1)}) %reduce-scatter.7.cloned.1.call-update) | async-done | bytes 1048592 | tf_op jit(solution)/shard_map/reduce_scatter | solution.py:597
  473.7 4.2 convert_reduce_fusion.3
  477.8 0.6 pad_maximum_fusion.1.every
  478.4 19.7 %all_sums.1 = (f32[48,128]{1,0:T(8,128)}, f32[32,128]{1,0:T(8,128)}) custom-call(f32[48,128]{1,0:T(8,128)} %pad_maximum_fusion.1.every, f32[32,128]{1,0:T(8,128)} %fusion.14.group), custom_call_target="tpu_custom_call" | custom-call | tf_op jit(solution)/shard_map/all_sums/pallas_call | solution.py:568
  498.1 1.3 slice_bitcast_fusion.1
  499.5 0.7 slice.32
  500.2 0.6 reshape.315
  500.8 1.3 slice_bitcast_fusion
  502.1 48.9 %reduce-scatter.11.cloned.1.call-done = bf16[256,3,512]{2,0,1:T(8,128)(2,1)} async-done(((bf16[2048,3,512]{2,0,1:T(8,128)(2,1)}), bf16[256,3,512]{2,0,1:T(8,128)(2,1)}) %reduce-scatter.11.cloned.1.call-update) | async-done | bytes 786448 | tf_op jit(solution)/shard_map/reduce_scatter | solution.py:597
  551.0 2.5 convert_element_type.115
  553.5 88.7 %reduce-scatter.15.cloned.1.call-done = bf16[256,2048]{1,0:T(8,128)(2,1)} async-done(((bf16[2048,2048]{1,0:T(8,128)(2,1)}), bf16[256,2048]{1,0:T(8,128)(2,1)}) %reduce-scatter.15.cloned.1.call-update) | async-done | bytes 1048592 | tf_op jit(solution)/shard_map/reduce_scatter | solution.py:597
  642.1 2.8 convert_element_type.119
  644.9 0.6 copy.42
  (64 shorter events, 0.8 us)
Async XLA Ops:
  7.2 4.7 copy-start.3
  7.2 6.5 %copy-start.9 = (f32[3,512]{1,0:T(4,128)S(1)}, f32[3,512]{1,0:T(4,128)}, u32[]{:S(2)}) copy-start(f32[3,512]{1,0:T(4,128)} %param.17) | copy-start | bytes 18436
  7.2 170.3 %all-gather.6.cloned.1.call-start = ((), (), s32[]{:S(2)}) async-start(), calls=%async_computation.7 | async-start | bytes 2359296 | tf_op jit(solution)/shard_map/all_gather | solution.py:634
  9.2 174.5 %all-gather.4.cloned.1.call-start = ((), (), s32[]{:S(2)}) async-start(), calls=%async_computation.6 | async-start | bytes 7077888 | tf_op jit(solution)/shard_map/all_gather | solution.py:633
  11.8 243.3 %all-gather.8.cloned.1.call-start = ((), (), s32[]{:S(2)}) async-start(), calls=%async_computation.8 | async-start | bytes 9437184 | tf_op jit(solution)/shard_map/all_gather | solution.py:635
  13.0 327.1 %reduce-scatter.13.cloned.1.call-start = ((), (), s32[]{:S(2)}) async-start(), calls=%async_computation.12 | async-start | bytes 2359296 | tf_op jit(solution)/shard_map/reduce_scatter | solution.py:597
  195.5 38.3 %copy-start.10 = (bf16[4,256,2048]{2,1,0:T(8,128)(2,1)S(1)}, bf16[4,256,2048]{2,1,0:T(8,128)(2,1)}, u32[]{:S(2)}) copy-start(bf16[4,256,2048]{2,1,0:T(8,128)(2,1)} %get-tuple-element.27) | copy-start | bytes 12582916
  237.5 126.6 %reduce-scatter.17.cloned.1.call-start = ((), (), s32[]{:S(2)}) async-start(), calls=%async_computation.14 | async-start | bytes 9437184 | tf_op jit(solution)/shard_map/reduce_scatter | solution.py:597
  251.8 166.3 %reduce-scatter.9.cloned.1.call-start = ((), (), s32[]{:S(2)}) async-start(), calls=%async_computation.10 | async-start | bytes 5242880 | tf_op jit(solution)/shard_map/reduce_scatter | solution.py:597
  251.9 2.2 copy-start.4
  255.1 26.3 %slice-start = ((s8[6291456]{0:T(1024)(128)(4,1)}), s8[4194304]{0:T(1024)(128)(4,1)S(1)}, s32[]{:S(2)}) async-start(s8[6291456]{0:T(1024)(128)(4,1)} %bitcast.64), calls=%async_computation.15 | async-start | bytes 8388608
  268.5 12.9 %copy-start.12 = (bf16[1024,2048]{1,0:T(8,128)(2,1)}, bf16[1024,2048]{1,0:T(8,128)(2,1)S(1)}, u32[]{:S(2)}) copy-start(bf16[1024,2048]{1,0:T(8,128)(2,1)S(1)} %get-tuple-element.58) | copy-start | bytes 12582916
  268.5 12.9 %slice-start.1 = ((s8[6291456]{0:T(1024)(128)(4,1)}), s8[2097152]{0:T(1024)(128)(4,1)S(1)}, s32[]{:S(2)}) async-start(s8[6291456]{0:T(1024)(128)(4,1)} %bitcast.64), calls=%async_computation.16 | async-start | bytes 4194304
  291.6 182.1 %reduce-scatter.7.cloned.1.call-start = ((), (), s32[]{:S(2)}) async-start(), calls=%async_computation.9 | async-start | bytes 5242880 | tf_op jit(solution)/shard_map/reduce_scatter | solution.py:597
  291.6 13.0 %copy-start.11 = (bf16[2048,512]{1,0:T(8,128)(2,1)S(1)}, bf16[2048,512]{1,0:T(8,128)(2,1)}, u32[]{:S(2)}) copy-start(bf16[2048,512]{1,0:T(8,128)(2,1)} %all-gather.6.cloned.1.call-done) | copy-start | bytes 6291460
  309.1 241.8 %reduce-scatter.11.cloned.1.call-start = ((), (), s32[]{:S(2)}) async-start(), calls=%async_computation.11 | async-start | bytes 7077888 | tf_op jit(solution)/shard_map/reduce_scatter | solution.py:597
  323.6 318.6 %reduce-scatter.15.cloned.1.call-start = ((), (), s32[]{:S(2)}) async-start(), calls=%async_computation.13 | async-start | bytes 9437184 | tf_op jit(solution)/shard_map/reduce_scatter | solution.py:597
  338.0 1.3 copy-start
  339.2 78.8 %copy-start.5 = (f32[2048]{0:T(1024)S(1)}, f32[2048]{0:T(1024)}, u32[]{:S(2)}) copy-start(f32[2048]{0:T(1024)} %param.14) | copy-start | bytes 24580
  339.5 134.2 %copy-start.2 = (bf16[256,2048]{1,0:T(8,128)(2,1)S(1)}, bf16[256,2048]{1,0:T(8,128)(2,1)}, u32[]{:S(2)}) copy-start(bf16[256,2048]{1,0:T(8,128)(2,1)} %cot.1) | copy-start | bytes 3145732
  339.5 134.2 %copy-start.7 = (f32[2048]{0:T(1024)S(1)}, f32[2048]{0:T(1024)}, u32[]{:S(2)}) copy-start(f32[2048]{0:T(1024)} %param.23) | copy-start | bytes 24580
  339.5 134.2 %copy-start.8 = (f32[2048]{0:T(1024)S(1)}, f32[2048]{0:T(1024)}, u32[]{:S(2)}) copy-start(f32[2048]{0:T(1024)} %param.19) | copy-start | bytes 24580
  418.1 55.6 %copy-start.1 = (bf16[256,2048]{1,0:T(8,128)(2,1)S(1)}, bf16[256,2048]{1,0:T(8,128)(2,1)}, u32[]{:S(2)}) copy-start(bf16[256,2048]{1,0:T(8,128)(2,1)} %reduce-scatter.9.cloned.1.call-done) | copy-start | bytes 3145732
  499.5 146.0 %copy-start.6 = (f32[2048]{0:T(1024)}, f32[2048]{0:T(1024)S(1)}, u32[]{:S(2)}) copy-start(f32[2048]{0:T(1024)S(1)} %get-tuple-element.84) | copy-start | bytes 24580
Sparse Core Ops, SparseCore 0:
  10.2 43.8 all-gather.5
  56.2 92.2 all-gather.3
  150.7 80.7 all-gather.7
  237.6 36.1 reduce-scatter.12
  275.9 88.1 reduce-scatter.16
  367.0 51.0 reduce-scatter.8
  421.0 52.5 reduce-scatter.6
  476.0 74.9 reduce-scatter.10
  553.3 88.8 reduce-scatter.14

commit v4 on v3

--- a/solution.py
+++ b/solution.py
@@ -581,6 +581,304 @@
     return untiled(totals[0], every), untiled(totals[1], group)
 
 
+class RowScatter:
+    pieces = 2
+
+    def __init__(self, chips, left, rights, flip, give, part, land, sems):
+        self.chips, self.left, self.rights, self.flip = chips, left, rights, flip
+        self.give, self.part, self.land = give, part, land
+        self.sib_send, self.sib_recv, self.send_l, self.send_r, self.recv = sems
+        self.depth = part.shape[1]
+
+    def target(self, p):
+        me, z, c, mp = place()
+        s, side = p // 2, lax.rem(p, 2)
+        far = self.chips - 1
+        t = jnp.where(side == 0, z + s - far, z - s + far)
+        return t, (t >= 0) & (t < self.chips)
+
+    def block(self, t, core, store):
+        b = 2 * t + core
+        cols = pl.ds(pl.multiple_of(b * self.depth, self.depth), self.depth)
+        self.flip[...] = self.left[:, cols].T
+        place_at = 0
+        for right in self.rights:
+            tile = min(512, right.shape[1])
+            for n in range(0, right.shape[1], tile):
+                store(slice(place_at + n, place_at + n + tile), dot(self.flip[...], right[:, n : n + tile]))
+            place_at += right.shape[1]
+
+    def sibling(self, t):
+        me, z, c, mp = place()
+        return remote(
+            self.give.at[t], self.part.at[t], self.sib_send.at[t], self.sib_recv.at[t], 2 * z + 1 - c, mp
+        )
+
+    def rows(self, q):
+        return pl.ds(q * (self.depth // self.pieces), self.depth // self.pieces)
+
+    def to_left(self, t, q):
+        me, z, c, mp = place()
+        r = self.rows(q)
+        return remote(
+            self.part.at[t, r], self.land.at[t, r], self.send_l.at[t, q], self.recv.at[t, q], me - 2, mp
+        )
+
+    def to_right(self, t, q):
+        me, z, c, mp = place()
+        r = self.rows(q)
+        slot = jnp.where(t > z + 1, t, self.chips)
+        return remote(
+            self.part.at[t, r], self.land.at[slot, r], self.send_r.at[t, q], self.recv.at[slot, q], me + 2, mp
+        )
+
+    def landed(self, slot, q):
+        me, z, c, mp = place()
+        here = self.land.at[slot, self.rows(q)]
+        remote(here, here, self.send_l.at[0, 0], self.recv.at[slot, q], me, mp).wait_recv()
+
+    def swap(self):
+        me, z, c, mp = place()
+
+        def step(p, carry):
+            t, valid = self.target(p)
+
+            @pl.when(valid)
+            def _():
+                def store(cols, values):
+                    self.give[t, :, cols] = values.astype(BF)
+
+                self.block(t, 1 - c, store)
+                self.sibling(t).start()
+
+            return carry
+
+        lax.fori_loop(0, 2 * self.chips - 1, step, 0)
+
+    def collect(self):
+        me, z, c, mp = place()
+        last = self.chips - 1
+
+        def step(p, carry):
+            t, valid = self.target(p)
+
+            @pl.when(valid)
+            def _():
+                self.sibling(t).wait_recv()
+
+                def store(cols, values):
+                    self.part[t, :, cols] = (values + self.part[t, :, cols].astype(F32)).astype(BF)
+
+                self.block(t, c, store)
+
+                @pl.when((t < z) & (z == last))
+                def _():
+                    for q in range(self.pieces):
+                        self.to_left(t, q).start()
+
+                @pl.when((t > z) & (z == 0))
+                def _():
+                    for q in range(self.pieces):
+                        self.to_right(t, q).start()
+
+            return carry
+
+        lax.fori_loop(0, 2 * self.chips - 1, step, 0)
+
+    def add(self, t, slot, q):
+        r = self.rows(q)
+        self.landed(slot, q)
+        self.part[t, r] = (self.part[t, r].astype(F32) + self.land[slot, r].astype(F32)).astype(BF)
+
+    def relay(self, s):
+        me, z, c, mp = place()
+        last = self.chips - 1
+        for q in range(self.pieces):
+            t = z + s - last
+
+            @pl.when((t >= 0) & (z < last))
+            def _():
+                self.add(t, t, q)
+                self.to_left(t, q).start()
+
+            u = z - s + last
+
+            @pl.when((u <= last) & (z > 0))
+            def _():
+                self.add(u, u, q)
+                self.to_right(u, q).start()
+
+    def finish(self, result):
+        me, z, c, mp = place()
+        for q in range(self.pieces):
+            r = self.rows(q)
+            result[r] = self.part[z, r].astype(F32)
+
+            @pl.when(z < self.chips - 1)
+            def _():
+                self.landed(z, q)
+                result[r] += self.land[z, r].astype(F32)
+
+            @pl.when(z > 0)
+            def _():
+                self.landed(self.chips, q)
+                result[r] += self.land[self.chips, r].astype(F32)
+
+    def drain(self):
+        me, z, c, mp = place()
+
+        def step(t, carry):
+            self.sibling(t).wait_send()
+            for q in range(self.pieces):
+
+                @pl.when(t < z)
+                def _():
+                    self.to_left(t, q).wait_send()
+
+                @pl.when(t > z)
+                def _():
+                    self.to_right(t, q).wait_send()
+
+            return carry
+
+        lax.fori_loop(0, self.chips, step, 0)
+
+
+def row_scatter_scratch(chips, depth, width):
+    return [
+        pltpu.VMEM((chips, depth, width), BF),
+        pltpu.VMEM((chips, depth, width), BF),
+        pltpu.VMEM((chips + 1, depth, width), BF),
+        pltpu.SemaphoreType.DMA((chips,)),
+        pltpu.SemaphoreType.DMA((chips,)),
+        pltpu.SemaphoreType.DMA((chips, RowScatter.pieces)),
+        pltpu.SemaphoreType.DMA((chips, RowScatter.pieces)),
+        pltpu.SemaphoreType.DMA((chips + 1, RowScatter.pieces)),
+    ]
+
+
+class GroupScatter:
+    def __init__(self, size, parts, land, send, recv):
+        self.size, self.parts, self.land, self.send, self.recv = size, parts, land, send, recv
+
+    def copy(self, k):
+        me, z, c, mp = place()
+        peer = lax.rem(mp + k, self.size)
+        return remote(
+            self.parts.at[peer], self.land.at[mp], self.send.at[k], self.recv.at[mp], me, peer
+        )
+
+    def start(self):
+        me, z, c, mp = place()
+        for k in range(1, self.size):
+            self.copy(k).start()
+
+    def finish(self, result):
+        me, z, c, mp = place()
+        own = pltpu.make_async_copy(self.parts.at[mp], self.land.at[mp], self.send.at[0])
+        own.start()
+        own.wait()
+        for k in range(1, self.size):
+            origin = lax.rem(mp + k, self.size)
+            here = self.land.at[origin]
+            remote(here, here, self.send.at[0], self.recv.at[origin], me, origin).wait_recv()
+        total = self.land[0].astype(F32)
+        for k in range(1, self.size):
+            total = total + self.land[k].astype(F32)
+        result[...] = total
+
+    def drain(self):
+        for k in range(1, self.size):
+            self.copy(k).wait_send()
+
+
+def grad_kernel(
+    dp_size,
+    mp_size,
+    x_all,
+    query_grad,
+    key_grad,
+    value_grad,
+    pre_grad,
+    mixed,
+    normed,
+    qkv_share,
+    up_share,
+    mixed_sum,
+    normed_sum,
+    flip,
+    *scratch,
+):
+    chips = dp_size // 2
+    qkv_scratch, up_scratch, rest = scratch[:8], scratch[8:16], scratch[16:]
+    qkv = RowScatter(chips, x_all, (query_grad, key_grad, value_grad), flip, *qkv_scratch[:3], qkv_scratch[3:])
+    up = RowScatter(chips, x_all, (pre_grad,), flip, *up_scratch[:3], up_scratch[3:])
+    normed_group = GroupScatter(mp_size, normed, *rest[:3])
+    mixed_group = GroupScatter(mp_size, mixed, *rest[3:6])
+    greet(chips, mp_size)
+    normed_group.start()
+    mixed_group.start()
+    qkv.swap()
+    qkv.collect()
+    up.swap()
+    if chips > 2:
+        qkv.relay(1)
+    up.collect()
+    for s in range(2, chips - 1):
+        qkv.relay(s)
+    qkv.finish(qkv_share)
+    for s in range(1, chips - 1):
+        up.relay(s)
+    normed_group.finish(normed_sum)
+    mixed_group.finish(mixed_sum)
+    up.finish(up_share)
+    for stream in (qkv, up, normed_group, mixed_group):
+        stream.drain()
+
+
+def grad_stage(dp_size, mp_size, x_all, query_grad, key_grad, value_grad, pre_grad, mixed, normed):
+    length, model = x_all.shape
+    rows = length // mp_size
+    depth, chips = model // dp_size, dp_size // 2
+    width, hidden = query_grad.shape[1], pre_grad.shape[1]
+    shape = jax.ShapeDtypeStruct
+    group = [
+        pltpu.VMEM((mp_size, rows, model), BF),
+        pltpu.SemaphoreType.DMA((mp_size,)),
+        pltpu.SemaphoreType.DMA((mp_size,)),
+    ]
+    return pl.pallas_call(
+        partial(grad_kernel, dp_size, mp_size),
+        out_shape=(
+            shape((depth, 3 * width), F32),
+            shape((depth, hidden), F32),
+            shape((rows, model), F32),
+            shape((rows, model), F32),
+        ),
+        in_specs=[VM] * 5 + [ANY] * 2,
+        out_specs=[VM] * 4,
+        scratch_shapes=[
+            pltpu.VMEM((depth, length), BF),
+            *row_scatter_scratch(chips, depth, 3 * width),
+            *row_scatter_scratch(chips, depth, hidden),
+            *group,
+            *group,
+        ],
+        compiler_params=pltpu.CompilerParams(
+            collective_id=3, has_side_effects=True, vmem_limit_bytes=60 << 20
+        ),
+        name="grad_stage",
+    )(
+        x_all,
+        query_grad,
+        key_grad,
+        value_grad,
+        pre_grad,
+        mixed.astype(BF).reshape(mp_size, rows, model),
+        normed.astype(BF).reshape(mp_size, rows, model),
+    )
+
+
 def right_product(left_side, right_side):
     return lax.dot_general(
         left_side, right_side, (((1,), (1,)), ((), ())), preferred_element_type=jnp.float32
@@ -647,20 +945,28 @@
     )
     attn_part = right_product(attended, dense_full)
     mlp_part = right_product(hidden_low, down_full)
-    mixed_sum = low_scatter(attn_part + mlp_part, "mp")
-    output = (token_float + mixed_sum + dense_bias + fc2_bias).astype(jnp.bfloat16)
     dense_grad = rows_product(out_rows, attended)
     down_grad = rows_product(out_rows, hidden_low)
     hidden_grad = jnp.dot(out_rows, down_full, preferred_element_type=jnp.float32)
     pre_grad = (hidden_grad * slope).astype(jnp.bfloat16)
-    up_grad = rows_product(gathered, pre_grad)
     up_bias_grad = jnp.sum(pre_grad.astype(jnp.float32), axis=0)
     projected_grad = jnp.concatenate([query_grad, key_grad, value_grad], axis=1)
-    qkv_grad = rows_product(gathered, projected_grad).reshape(model_width, 3, local_width)
     qkv_bias_grad = jnp.concatenate([query_sum, key_sum, value_sum], axis=0)
     attn_input = right_product(projected_grad, qkv_full.reshape(model_width, 3 * local_width))
     mlp_input = right_product(pre_grad, up_full)
-    normed_grad = low_scatter(attn_input + mlp_input, "mp")
+    qkv_share, up_share, mixed_sum, normed_grad = grad_stage(
+        dp_size,
+        mp_size,
+        gathered,
+        query_grad,
+        key_grad,
+        value_grad,
+        pre_grad,
+        attn_part + mlp_part,
+        attn_input + mlp_input,
+    )
+    qkv_share = qkv_share.reshape(-1, 3, local_width)
+    output = (token_float + mixed_sum + dense_bias + fc2_bias).astype(jnp.bfloat16)
     norm_value, norm_back = jax.vjp(normalize, token_float, ln_gain, ln_bias)
     token_grad, gain_grad, shift_grad = norm_back(normed_grad)
     cot_float = cotangent.astype(jnp.float32)
@@ -669,12 +975,8 @@
     (gain_total, shift_total, bias_total), (qkv_bias_total, up_bias_total) = all_sums(
         dp_size, mp_size, (gain_grad, shift_grad, out_bias_grad), (qkv_bias_grad, up_bias_grad)
     )
-    qkv_share, dense_share, up_share, down_share = (
-        low_scatter(qkv_grad, "dp"),
-        low_scatter(dense_grad, "dp"),
-        low_scatter(up_grad, "dp"),
-        low_scatter(down_grad, "dp"),
-    )
+    dense_share = low_scatter(dense_grad, "dp")
+    down_share = low_scatter(down_grad, "dp")
     return (
         output,
         input_grad,

time: 659 us -> 534 us (0.81)
  waiting for transfers between devices: 262 us -> 0.11 us
  Pallas kernels: 219 us -> 390 us
  matrix products: 115 us -> 90.3 us
  other arithmetic: 24.8 us -> 16.6 us
    reduce_scatter x6 -> x2, waiting for transfers between devices: 262 us -> 0.01 us  [low_scatter(): lax.psum_scatter(partial_sums.astype(jnp.bfloat16), axis, scatter_dimensi...]
    pallas_call x0 -> x1, Pallas kernels: none -> 173 us  [grad_stage(): pl.pallas_call(partial(grad_kernel, dp_size, mp_size), out_shape=(shape((...]
    dot_general x4 -> x2, matrix products: 43.5 us -> 17.9 us  [rows_product(): lax.dot_general(left_side, right_side, (((0,), (0,)), ((), ())), preferre...]
  transfers between devices with their start and end apart: 9 -> 5, of which waited for: 5 -> 0; matrix products, arithmetic and copies ran while one was open for 23% -> 22% of each run, Pallas kernels for 34% -> 74%
where the time goes in v4:
time: 534 us; the launch traced here: 528 us
  Pallas kernels  390 us (73%)
  matrix products  90.3 us (17%)
  other arithmetic  16.6 us (3%)
  between operations  15.3 us (3%)
  local copies, waits for them, and re-layouts  15.2 us (3%)
    pallas_call x1, Pallas kernels, grad_stage(): pl.pallas_call(partial(grad_kernel, dp_size, mp_size), out_shape=(shape((...  173 us
    pallas_call x1, Pallas kernels, up_stage(): pl.pallas_call(partial(up_kernel, dp_size, mp_size), out_shape=outs, in_s...  161 us
    dot_general x4, matrix products, right_product(): lax.dot_general(left_side, right_side, (((1,), (1,)), ((), ())), preferre...  42.8 us
    pallas_call x1, Pallas kernels, attention(): pl.pallas_call(attention_kernel, grid=(pairs,), in_specs=[pl.BlockSpec(me...  38.4 us
    dot_general x2, matrix products, rows_product(): lax.dot_general(left_side, right_side, (((0,), (0,)), ((), ())), preferre...  17.9 us
    pallas_call x1, Pallas kernels, all_sums(): pl.pallas_call(partial(sums_kernel, dp_size, mp_size), out_shape=(shape(o...  17 us
    dot_general x1, matrix products, body(): jnp.dot(gathered, qkv_full.reshape(model_width, 3 * local_width), preferr...  11.8 us
    dot_general x1, matrix products, body(): jnp.dot(out_rows, down_full, preferred_element_type=jnp.float32)  11.6 us
  transfers between devices with their start and end apart: 5, of which 0 were waited for; matrix products, arithmetic and copies ran while one was open for 22% of the time, Pallas kernels for 74%

profile of v4, /device:TPU:0, one launch (start us, length us, event | category | flops | bytes accessed | tf_op | source)
XLA Modules:
  0.0 527.7 jit_solution(9568786197077194454)
XLA Ops:
  7.2 0.0 all-gather.6.cloned.1.call-start
  7.2 1.9 convert_element_type.80
  9.1 0.0 all-gather.6.cloned.1.call-update
  9.2 0.0 all-gather.4.cloned.1.call-start
  9.2 2.6 copy.27
  11.8 0.0 all-gather.4.cloned.1.call-update
  11.8 0.0 all-gather.8.cloned.1.call-start
  11.9 1.1 convert_element_type.84
  13.0 0.0 all-gather.8.cloned.1.call-update
  13.0 0.0 reduce-scatter.3.cloned.1.call-start
  13.1 0.3 multiply_cosine_fusion
  13.4 0.2 copy.29
  13.7 0.2 copy.28
  14.6 161.4 %up_stage.1 = (bf16[4,256,2048]{2,1,0:T(8,128)(2,1)}, bf16[4,256,2048]{2,1,0:T(8,128)(2,1)}, bf16[8,256,2048]{2,1,0:T(8,128)(2,1)}, bf16[4,256,2048]{2,1,0:T(8,128)(2,1)}, bf16[4,256,2048]{2,1,0:T(8,128)(2,1)}) custom-call(bf16[256,2048]{1,0:T(8,128)(2,1)} %tokens.1, f32[1,2048]{1,0:T(1,128)} %bitcast.54, f32[1,2048]{1,0:T(1,128)} %bitcast.58, ...), custom_call_target="tpu_custom_call" | custom-call | tf_op jit(solution)/shard_map/up_stage/pallas_call | solution.py:333
  176.0 0.1 negate_select_fusion
  176.1 1.2 pad_maximum_fusion.rot
  177.3 6.2 %convolution_convert_fusion.1.out_grad = bf16[1024,512]{1,0:T(8,128)(2,1)} fusion(bf16[1024,2048]{1,0:T(8,128)(2,1)} %bitcast.65, bf16[2048,512]{1,0:T(8,128)(2,1)} %all-gather.6.cloned.1.call-done), kind=kOutput, calls=%fused_computation.32 | convolution fusion | flops 2148007936 | bytes 7340032 | tf_op jit(solution)/shard_map/dot_general | solution.py:940
  183.5 11.8 %convolution_add_fusion.q_in.k_in.v_in = f32[1024,1536]{1,0:T(8,128)} fusion(bf16[1024,2048]{1,0:T(8,128)(2,1)} %bitcast.48, bf16[2048,1536]{0,1:T(8,128)(2,1)} %bitcast.63, f32[1536]{0:T(1024)S(1)} %add.77), kind=kOutput, calls=%fused_computation.6 | convolution fusion | flops 6444023808 | bytes 16783360 | tf_op jit(solution)/shard_map/dot_general | solution.py:937
  195.3 38.4 %attention.1 = (bf16[1024,512]{1,0:T(8,128)(2,1)S(1)}, bf16[1024,512]{1,0:T(8,128)(2,1)S(1)}, bf16[1024,512]{1,0:T(8,128)(2,1)S(1)}, bf16[1024,512]{1,0:T(8,128)...) custom-call(s32[1]{0:T(128)S(6)} %copy.37.start, ...), custom_call_target="tpu_custom_call" | custom-call | flops 8589934592 | bytes 8388608 | tf_op jit(solution)/shard_map/attention/pallas_call | solution.py:479
  233.7 3.7 convolution_convert_fusion
  237.4 0.0 reduce-scatter.3.cloned.1.call-update
  237.4 0.0 reduce-scatter.5.cloned.1.call-start
  237.5 14.2 %bitcast_convert_fusion = bf16[2048,2048]{1,0:T(8,128)(2,1)} fusion(bf16[4,256,2048]{2,1,0:T(8,128)(2,1)} %get-tuple-element.31, bf16[4,256,2048]{2,1,0:T(8,128)(2,1)} %get-tuple-element.37), kind=kOutput, calls=%fused_computation | convolution fusion | flops 8594128896 | bytes 16777216 | tf_op jit(solution)/shard_map/dot_general | solution.py:889
  251.7 0.0 reduce-scatter.5.cloned.1.call-update
  251.7 1.5 convert_reduce_fusion.1
  253.2 0.0 all-gather.8.cloned.1.call-done
  253.3 14.8 %fusion.22 = f32[1024,2048]{1,0:T(8,128)} fusion(bf16[1024,2048]{1,0:T(8,128)(2,1)} %bitcast.69, bf16[2048,2048]{1,0:T(8,128)(2,1)} %all-gather.8.cloned.1.call-done), kind=kOutput, calls=%fused_computation.60 | convolution fusion | flops 8589934592 | bytes 20971520 | tf_op jit(solution)/shard_map/dot_general | solution.py:883
  268.1 7.9 %add_convert_fusion.1 = bf16[1024,2048]{1,0:T(8,128)(2,1)} fusion(f32[1024,2048]{1,0:T(8,128)} %fusion.22, bf16[1024,512]{1,0:T(8,128)(2,1)S(1)} %get-tuple-element.36, bf16[2048,512]{1,0:T(8,128)(2,1)S(1)} %copy-done.17), kind=kOutput, calls=%fused_computation.5 | convolution fusion | flops 2151677952 | bytes 15728640 | tf_op jit(solution)/shard_map/dot_general | solution.py:883
  276.0 11.6 %convert_reduce_fusion = (f32[2048]{0:T(1024)S(1)}, bf16[1024,2048]{1,0:T(8,128)(2,1)S(1)}) fusion(bf16[1024,2048]{1,0:T(8,128)(2,1)} %bitcast.68, bf16[1024,2048]{1,0:T(8,128)(2,1)} %bitcast.66, bf16[2048,2048]{1,0:T(8,128)(2,1)S(1)} %copy-done.15), kind=kOutput, calls=%fused_computation.3 | convolution fusion | flops 8600418304 | bytes 20979712 | tf_op jit(solution)/shard_map/dot_general | solution.py:950
  287.7 8.8 %fusion.23 = f32[1024,2048]{1,0:T(8,128)S(1)} fusion(bf16[1024,2048]{1,0:T(8,128)(2,1)S(1)} %get-tuple-element.90.pre_grad, bf16[2048,2048]{1,0:T(8,128)(2,1)S(1)} %bitcast.62), kind=kOutput, calls=%fused_computation.61 | convolution fusion | flops 8589934592 | bytes 20971520 | tf_op jit(solution)/shard_map/dot_general | solution.py:883
  296.6 11.2 %add_convert_fusion = bf16[1024,2048]{1,0:T(8,128)(2,1)} fusion(f32[1024,2048]{1,0:T(8,128)S(1)} %fusion.23, bf16[2048,1536]{0,1:T(8,128)(2,1)} %bitcast.64, bf16[1024,512]{1,0:T(8,128)(2,1)S(1)} %copy-done.9, bf16[1024,512]{1,0:T(8,128)(2,1)S(1)} %get-tuple-element.33.key_grad, bf16[1024,512]{1,0:T(8,128)(2,1)S(1)} %get-tuple-element.32.query_grad), kind=kOutput, calls=%fused_computation.4 | convolution fusion | flops 6456082432 | bytes 22020096 | tf_op jit(solution)/shard_map/dot_general | solution.py:883
  307.8 173.2 %grad_stage.1 = (f32[256,1536]{1,0:T(8,128)}, f32[256,2048]{1,0:T(8,128)}, f32[256,2048]{1,0:T(8,128)}, f32[256,2048]{1,0:T(8,128)}) custom-call(bf16[1024,2048]{1,0:T(8,128)(2,1)} %bitcast.49, bf16[1024,512]{1,0:T(8,128)(2,1)} %copy-done, bf16[1024,512]{1,0:T(8,128)(2,1)} %copy-done.1, bf16[1024,512]{1,0:T(8,128)(2,1)} %get-tuple-element.34.value_grad, ...), custom_call_target="tpu_custom_call" | custom-call | tf_op jit(solution)/shard_map/grad_stage/pallas_call | solution.py:850
  481.1 3.2 copy.31
  484.3 3.0 copy.33
  487.3 0.6 fusion.18.group
  488.0 0.6 fusion.11
  488.6 1.0 fusion.14
  489.7 2.9 convert_reduce_fusion.2
  492.6 0.6 pad_maximum_fusion.1.every
  493.2 17.0 %all_sums.1 = (f32[48,128]{1,0:T(8,128)}, f32[32,128]{1,0:T(8,128)}) custom-call(f32[48,128]{1,0:T(8,128)} %pad_maximum_fusion.1.every, f32[32,128]{1,0:T(8,128)} %fusion.18.group), custom_call_target="tpu_custom_call" | custom-call | tf_op jit(solution)/shard_map/all_sums/pallas_call | solution.py:568
  510.2 1.3 slice_bitcast_fusion.1
  511.5 0.7 slice.32
  512.2 0.6 reshape.325
  512.8 1.3 slice_bitcast_fusion
  514.1 1.8 convert_element_type.95
  515.9 2.8 convert_element_type.97
  518.7 0.6 copy.38
  519.3 1.3 copy.39
  (58 shorter events, 0.3 us)
Async XLA Ops:
  7.2 4.7 copy-start.6
  7.2 170.2 %all-gather.6.cloned.1.call-start = ((), (), s32[]{:S(2)}) async-start(), calls=%async_computation.3 | async-start | bytes 2359296 | tf_op jit(solution)/shard_map/all_gather | solution.py:932
  9.2 174.3 %all-gather.4.cloned.1.call-start = ((), (), s32[]{:S(2)}) async-start(), calls=%async_computation.2 | async-start | bytes 7077888 | tf_op jit(solution)/shard_map/all_gather | solution.py:931
  11.8 2.1 copy-start.12
  11.8 241.4 %all-gather.8.cloned.1.call-start = ((), (), s32[]{:S(2)}) async-start(), calls=%async_computation.4 | async-start | bytes 9437184 | tf_op jit(solution)/shard_map/all_gather | solution.py:933
  13.0 501.1 %reduce-scatter.3.cloned.1.call-start = ((), (), s32[]{:S(2)}) async-start(), calls=%async_computation.5 | async-start | bytes 2359296 | tf_op jit(solution)/shard_map/reduce_scatter | solution.py:895
  195.3 38.4 %copy-start.16 = (bf16[4,256,2048]{2,1,0:T(8,128)(2,1)S(1)}, bf16[4,256,2048]{2,1,0:T(8,128)(2,1)}, u32[]{:S(2)}) copy-start(bf16[4,256,2048]{2,1,0:T(8,128)(2,1)} %get-tuple-element.31) | copy-start | bytes 12582916
  233.7 62.9 %copy-start = (bf16[1024,512]{1,0:T(8,128)(2,1)}, bf16[1024,512]{1,0:T(8,128)(2,1)S(1)}, u32[]{:S(2)}) copy-start(bf16[1024,512]{1,0:T(8,128)(2,1)S(1)} %get-tuple-element.32.query_grad) | copy-start | bytes 3145732
  233.7 62.9 %copy-start.1 = (bf16[1024,512]{1,0:T(8,128)(2,1)}, bf16[1024,512]{1,0:T(8,128)(2,1)S(1)}, u32[]{:S(2)}) copy-start(bf16[1024,512]{1,0:T(8,128)(2,1)S(1)} %get-tuple-element.33.key_grad) | copy-start | bytes 3145732
  237.4 278.5 %reduce-scatter.5.cloned.1.call-start = ((), (), s32[]{:S(2)}) async-start(), calls=%async_computation.6 | async-start | bytes 9437184 | tf_op jit(solution)/shard_map/reduce_scatter | solution.py:895
  253.3 14.8 %copy-start.17 = (bf16[2048,512]{1,0:T(8,128)(2,1)S(1)}, bf16[2048,512]{1,0:T(8,128)(2,1)}, u32[]{:S(2)}) copy-start(bf16[2048,512]{1,0:T(8,128)(2,1)} %all-gather.6.cloned.1.call-done) | copy-start | bytes 6291460
  268.1 7.9 %copy-start.15 = (bf16[2048,2048]{1,0:T(8,128)(2,1)S(1)}, bf16[2048,2048]{1,0:T(8,128)(2,1)}, u32[]{:S(2)}) copy-start(bf16[2048,2048]{1,0:T(8,128)(2,1)} %all-gather.8.cloned.1.call-done) | copy-start | bytes 25165828
  268.1 19.6 %slice-start = ((s8[8388608]{0:T(1024)(128)(4,1)}), s8[4194304]{0:T(1024)(128)(4,1)S(1)}, s32[]{:S(2)}) async-start(s8[8388608]{0:T(1024)(128)(4,1)} %bitcast.60), calls=%async_computation.7 | async-start | bytes 8388608
  276.0 11.7 %slice-start.1 = ((s8[8388608]{0:T(1024)(128)(4,1)}), s8[4194304]{0:T(1024)(128)(4,1)S(1)}, s32[]{:S(2)}) async-start(s8[8388608]{0:T(1024)(128)(4,1)} %bitcast.60), calls=%async_computation.8 | async-start | bytes 8388608
  287.6 8.9 %copy-start.4 = (bf16[1024,2048]{1,0:T(8,128)(2,1)}, bf16[1024,2048]{1,0:T(8,128)(2,1)S(1)}, u32[]{:S(2)}) copy-start(bf16[1024,2048]{1,0:T(8,128)(2,1)S(1)} %get-tuple-element.90.pre_grad) | copy-start | bytes 12582916
  287.7 8.9 %copy-start.9 = (bf16[1024,512]{1,0:T(8,128)(2,1)S(1)}, bf16[1024,512]{1,0:T(8,128)(2,1)}, u32[]{:S(2)}) copy-start(bf16[1024,512]{1,0:T(8,128)(2,1)} %get-tuple-element.34.value_grad) | copy-start | bytes 3145732
  481.1 6.9 %copy-start.2 = (bf16[256,2048]{1,0:T(8,128)(2,1)S(1)}, bf16[256,2048]{1,0:T(8,128)(2,1)}, u32[]{:S(2)}) copy-start(bf16[256,2048]{1,0:T(8,128)(2,1)} %tokens.1) | copy-start | bytes 3145732
  481.1 6.9 %copy-start.3 = (f32[256,2048]{1,0:T(8,128)S(1)}, f32[256,2048]{1,0:T(8,128)}, u32[]{:S(2)}) copy-start(f32[256,2048]{1,0:T(8,128)} %get-tuple-element.40) | copy-start | bytes 6291460
  481.1 6.9 %copy-start.10 = (f32[2048]{0:T(1024)S(1)}, f32[2048]{0:T(1024)}, u32[]{:S(2)}) copy-start(f32[2048]{0:T(1024)} %param.14) | copy-start | bytes 24580
  484.3 5.4 %copy-start.13 = (f32[2048]{0:T(1024)S(1)}, f32[2048]{0:T(1024)}, u32[]{:S(2)}) copy-start(f32[2048]{0:T(1024)} %param.23) | copy-start | bytes 24580
  484.3 5.4 %copy-start.14 = (f32[2048]{0:T(1024)S(1)}, f32[2048]{0:T(1024)}, u32[]{:S(2)}) copy-start(f32[2048]{0:T(1024)} %param.19) | copy-start | bytes 24580
  487.3 2.3 copy-start.5
  487.3 2.3 copy-start.8
  492.6 26.7 %copy-start.7 = (f32[256,2048]{1,0:T(8,128)S(1)}, f32[256,2048]{1,0:T(8,128)}, u32[]{:S(2)}) copy-start(f32[256,2048]{1,0:T(8,128)} %get-tuple-element.137) | copy-start | bytes 6291460
  511.5 9.1 %copy-start.11 = (f32[2048]{0:T(1024)}, f32[2048]{0:T(1024)S(1)}, u32[]{:S(2)}) copy-start(f32[2048]{0:T(1024)S(1)} %get-tuple-element.136) | copy-start | bytes 24580
Sparse Core Ops, SparseCore 0:
  10.2 43.8 all-gather.5
  56.2 92.2 all-gather.3
  150.7 80.7 all-gather.7
  237.5 36.2 reduce-scatter.2
  276.0 127.1 reduce-scatter.4

commit v5 on v4

--- a/solution.py
+++ b/solution.py
@@ -351,13 +351,6 @@
         ),
         name="up_stage",
     )(tokens, gain.reshape(1, -1), shift.reshape(1, -1), cot, up_master, up_bias.reshape(1, -1))
-
-
-def normalize(values, gain_vec, shift_vec):
-    centre = values - jnp.mean(values, axis=-1, keepdims=True)
-    spread = jnp.mean(centre * centre, axis=-1, keepdims=True)
-    scaled = centre * lax.rsqrt(spread + EPSILON)
-    return scaled * gain_vec + shift_vec
 
 
 def attention_kernel(start, q_in, k_in, v_in, out_grad, rot, out, q_grad, k_grad, v_grad, q_sum, k_sum, v_sum, bias, k_acc, v_acc):
@@ -502,83 +495,9 @@
     )(start, projected, projected, projected, out_grad, rotary_lanes(length))
 
 
-def sums_kernel(dp_size, mp_size, every, group, every_out, group_out, first, second, send_1, recv_1, send_2, recv_2):
-    me, z, c, mp = place()
-    split = every.shape[0]
-    bar = pltpu.get_barrier_semaphore()
-    for k in range(1, mp_size):
-        pl.semaphore_signal(bar, 1, device_id=(me, lax.rem(mp + k, mp_size)), device_id_type=MESH)
-    for k in range(1, dp_size):
-        pl.semaphore_signal(bar, 1, device_id=(lax.rem(me + k, dp_size), mp), device_id_type=MESH)
-    pl.semaphore_wait(bar, mp_size + dp_size - 2)
-
-    def copy_1(k):
-        return remote(
-            every, first.at[mp], send_1.at[k], recv_1.at[mp], me, lax.rem(mp + k, mp_size)
-        )
-
-    def copy_2(k):
-        return remote(
-            second.at[me], second.at[me], send_2.at[k], recv_2.at[me], lax.rem(me + k, dp_size), mp
-        )
-
-    for k in range(1, mp_size):
-        copy_1(k).start()
-    first[mp] = every[...]
-    second[me, split:] = group[...]
-    for k in range(1, mp_size):
-        origin = lax.rem(mp + k, mp_size)
-        remote(every, first.at[origin], send_1.at[0], recv_1.at[origin], me, origin).wait_recv()
-    total = first[0]
-    for k in range(1, mp_size):
-        total = total + first[k]
-    second[me, :split] = total
-    for k in range(1, dp_size):
-        copy_2(k).start()
-    for k in range(1, dp_size):
-        origin = lax.rem(me + k, dp_size)
-        remote(second.at[origin], second.at[origin], send_2.at[0], recv_2.at[origin], origin, mp).wait_recv()
-    total = second[0]
-    for k in range(1, dp_size):
-        total = total + second[k]
-    every_out[...] = total[:split]
-    group_out[...] = total[split:]
-    for k in range(1, mp_size):
-        copy_1(k).wait_send()
-    for k in range(1, dp_size):
-        copy_2(k).wait_send()
-
-
-def tiled(vectors):
-    flat = jnp.concatenate([v.reshape(-1) for v in vectors])
-    return jnp.pad(flat, (0, -flat.shape[0] % 1024)).reshape(-1, 128)
-
-
-def untiled(table, vectors):
-    flat, place_at, parts = table.reshape(-1), 0, []
-    for v in vectors:
-        parts.append(flat[place_at : place_at + v.size].reshape(v.shape))
-        place_at += v.size
-    return parts
-
-
-def all_sums(dp_size, mp_size, every, group):
-    one, two = tiled(every), tiled(group)
-    shape = jax.ShapeDtypeStruct
-    totals = pl.pallas_call(
-        partial(sums_kernel, dp_size, mp_size),
-        out_shape=(shape(one.shape, F32), shape(two.shape, F32)),
-        in_specs=[VM] * 2,
-        out_specs=[VM] * 2,
-        scratch_shapes=[
-            pltpu.VMEM((mp_size, *one.shape), F32),
-            pltpu.VMEM((dp_size, one.shape[0] + two.shape[0], 128), F32),
-            *[pltpu.SemaphoreType.DMA((n,)) for n in (mp_size, mp_size, dp_size, dp_size)],
-        ],
-        compiler_params=pltpu.CompilerParams(collective_id=2, has_side_effects=True),
-        name="all_sums",
-    )(one, two)
-    return untiled(totals[0], every), untiled(totals[1], group)
+def flat(ref, cols):
+    values = ref[..., cols]
+    return values.reshape(-1, values.shape[-1])
 
 
 class RowScatter:
@@ -600,13 +519,15 @@
     def block(self, t, core, store):
         b = 2 * t + core
         cols = pl.ds(pl.multiple_of(b * self.depth, self.depth), self.depth)
-        self.flip[...] = self.left[:, cols].T
+        self.flip[...] = flat(self.left, cols).T
         place_at = 0
         for right in self.rights:
-            tile = min(512, right.shape[1])
-            for n in range(0, right.shape[1], tile):
-                store(slice(place_at + n, place_at + n + tile), dot(self.flip[...], right[:, n : n + tile]))
-            place_at += right.shape[1]
+            width = right.shape[-1]
+            tile = min(512, width)
+            for n in range(0, width, tile):
+                product = dot(self.flip[...], flat(right, slice(n, n + tile)))
+                store(slice(place_at + n, place_at + n + tile), product)
+            place_at += width
 
     def sibling(self, t):
         me, z, c, mp = place()
@@ -724,11 +645,17 @@
                 self.landed(self.chips, q)
                 result[r] += self.land[self.chips, r].astype(F32)
 
-    def drain(self):
-        me, z, c, mp = place()
-
+    def drain_swap(self):
         def step(t, carry):
             self.sibling(t).wait_send()
+            return carry
+
+        lax.fori_loop(0, self.chips, step, 0)
+
+    def drain(self):
+        me, z, c, mp = place()
+
+        def step(t, carry):
             for q in range(self.pieces):
 
                 @pl.when(t < z)
@@ -746,7 +673,6 @@
 
 def row_scatter_scratch(chips, depth, width):
     return [
-        pltpu.VMEM((chips, depth, width), BF),
         pltpu.VMEM((chips, depth, width), BF),
         pltpu.VMEM((chips + 1, depth, width), BF),
         pltpu.SemaphoreType.DMA((chips,)),
@@ -758,131 +684,323 @@
 
 
 class GroupScatter:
-    def __init__(self, size, parts, land, send, recv):
-        self.size, self.parts, self.land, self.send, self.recv = size, parts, land, send, recv
-
-    def copy(self, k):
+    def __init__(self, size, blocks, parts, land, send, recv):
+        self.size, self.blocks, self.parts, self.land, self.send, self.recv = size, blocks, parts, land, send, recv
+        self.depth = parts.shape[2] // blocks
+
+    def copy(self, k, j):
         me, z, c, mp = place()
         peer = lax.rem(mp + k, self.size)
+        cols = pl.ds(pl.multiple_of(j * self.depth, self.depth), self.depth)
         return remote(
-            self.parts.at[peer], self.land.at[mp], self.send.at[k], self.recv.at[mp], me, peer
-        )
-
-    def start(self):
-        me, z, c, mp = place()
+            self.parts.at[peer, :, cols],
+            self.land.at[mp, :, cols],
+            self.send.at[k, j],
+            self.recv.at[mp, j],
+            me,
+            peer,
+        )
+
+    def start(self, j):
         for k in range(1, self.size):
-            self.copy(k).start()
-
-    def finish(self, result):
-        me, z, c, mp = place()
-        own = pltpu.make_async_copy(self.parts.at[mp], self.land.at[mp], self.send.at[0])
-        own.start()
-        own.wait()
+            self.copy(k, j).start()
+
+    def arrive(self):
+        me, z, c, mp = place()
+
+        def step(j, carry):
+            cols = pl.ds(pl.multiple_of(j * self.depth, self.depth), self.depth)
+            for k in range(1, self.size):
+                origin = lax.rem(mp + k, self.size)
+                here = self.land.at[origin, :, cols]
+                remote(here, here, self.send.at[0, 0], self.recv.at[origin, j], me, origin).wait_recv()
+            return carry
+
+        lax.fori_loop(0, self.blocks, step, 0)
+
+    def total(self, rows):
+        me, z, c, mp = place()
+        sums = self.parts[mp, rows].astype(F32)
         for k in range(1, self.size):
-            origin = lax.rem(mp + k, self.size)
-            here = self.land.at[origin]
-            remote(here, here, self.send.at[0], self.recv.at[origin], me, origin).wait_recv()
-        total = self.land[0].astype(F32)
-        for k in range(1, self.size):
-            total = total + self.land[k].astype(F32)
-        result[...] = total
+            sums = sums + self.land[lax.rem(mp + k, self.size), rows].astype(F32)
+        return sums
 
     def drain(self):
-        for k in range(1, self.size):
-            self.copy(k).wait_send()
+        def step(j, carry):
+            for k in range(1, self.size):
+                self.copy(k, j).wait_send()
+            return carry
+
+        lax.fori_loop(0, self.blocks, step, 0)
 
 
 def grad_kernel(
     dp_size,
     mp_size,
     x_all,
+    pre_grad,
+    attended,
+    hidden_all,
+    qkv_full,
+    up_full,
+    dense_full,
+    down_full,
     query_grad,
     key_grad,
     value_grad,
-    pre_grad,
-    mixed,
-    normed,
+    query_sum,
+    key_sum,
+    value_sum,
+    up_sum,
+    tokens,
+    cot,
+    gain,
+    out_bias,
     qkv_share,
     up_share,
-    mixed_sum,
-    normed_sum,
+    output,
+    input_grad,
+    totals,
+    x_buf,
+    pre,
+    mixed_buf,
+    attended_buf,
+    hidden_buf,
+    wide_buf,
+    thin_buf,
     flip,
+    give,
+    first,
+    second,
+    load_sem,
+    stream_sem,
     *scratch,
 ):
+    me, z, c, mp = place()
     chips = dp_size // 2
-    qkv_scratch, up_scratch, rest = scratch[:8], scratch[8:16], scratch[16:]
-    qkv = RowScatter(chips, x_all, (query_grad, key_grad, value_grad), flip, *qkv_scratch[:3], qkv_scratch[3:])
-    up = RowScatter(chips, x_all, (pre_grad,), flip, *up_scratch[:3], up_scratch[3:])
-    normed_group = GroupScatter(mp_size, normed, *rest[:3])
-    mixed_group = GroupScatter(mp_size, mixed, *rest[3:6])
-    greet(chips, mp_size)
-    normed_group.start()
-    mixed_group.start()
+    rows, model = tokens.shape
+    width, inner = query_grad.shape[1], up_sum.shape[1]
+    depth = model // dp_size
+    qkv_scratch, up_scratch, rest = scratch[:7], scratch[7:14], scratch[14:]
+    grads = (query_grad, key_grad, value_grad)
+    give_qkv = give.at[:, :, pl.ds(0, 3 * width)]
+    give_up = give.at[:, :, pl.ds(0, inner)]
+    qkv = RowScatter(chips, x_buf, grads, flip, give_qkv, *qkv_scratch[:2], qkv_scratch[2:])
+    up = RowScatter(chips, x_buf, (pre,), flip, give_up, *up_scratch[:2], up_scratch[2:])
+    normed_group = GroupScatter(mp_size, dp_size, x_buf, *rest[:3])
+    mixed_group = GroupScatter(mp_size, dp_size, mixed_buf, *rest[3:6])
+    send_1, recv_1, send_2, recv_2 = rest[6:]
+
+    loads = [
+        pltpu.make_async_copy(source, target, load_sem.at[n])
+        for n, (source, target) in enumerate(
+            ((x_all, x_buf), (pre_grad, pre), (attended, attended_buf), (hidden_all, hidden_buf))
+        )
+    ]
+    for load in loads:
+        load.start()
+
+    def stream(wide, thin):
+        def copies(j):
+            slot = lax.rem(j, 2)
+            r = pl.ds(pl.multiple_of(j * depth, depth), depth)
+            return (
+                pltpu.make_async_copy(wide.at[r], wide_buf.at[slot], stream_sem.at[0, slot]),
+                pltpu.make_async_copy(
+                    thin.at[r], thin_buf.at[slot, :, pl.ds(0, thin.shape[1])], stream_sem.at[1, slot]
+                ),
+            )
+
+        return copies
+
+    normed_stream = stream(up_full, qkv_full)
+    mixed_stream = stream(down_full, dense_full)
+
+    def partial_sums(copies, wide, thins, target, group_out):
+        half = mp_size // 2
+
+        def step(j, carry):
+            slot = lax.rem(j, 2)
+            for copy in copies(j):
+                copy.wait()
+
+            @pl.when(j + 1 < dp_size)
+            def _():
+                for copy in copies(j + 1):
+                    copy.start()
+
+            cols = pl.ds(pl.multiple_of(j * depth, depth), depth)
+            for h in range(2):
+                group = pl.ds(h * half, half)
+                left = wide[group].reshape(half * rows, inner)
+                sums = dot(left, wide_buf[slot], 1, 1)
+                for n, thin in enumerate(thins):
+                    left = thin[pl.ds(h * half * rows, half * rows), :]
+                    sums = sums + dot(left, thin_buf[slot, :, n * width : (n + 1) * width], 1, 1)
+                target[group, :, cols] = sums.astype(BF).reshape(half, rows, depth)
+            group_out.start(j)
+            return carry
+
+        lax.fori_loop(0, dp_size, step, 0)
+
+    for copy in mixed_stream(0):
+        copy.start()
+    greet_all(dp_size, mp_size)
+    loads[0].wait()
     qkv.swap()
     qkv.collect()
-    up.swap()
+    loads[2].wait()
+    loads[3].wait()
+    partial_sums(mixed_stream, hidden_buf, (attended_buf,), mixed_buf, mixed_group)
+    for copy in normed_stream(0):
+        copy.start()
     if chips > 2:
         qkv.relay(1)
+    loads[1].wait()
+    qkv.drain_swap()
+    up.swap()
     up.collect()
+    if chips > 3:
+        qkv.relay(2)
+    partial_sums(normed_stream, pre, grads, x_buf, normed_group)
+    for s in range(3, chips - 1):
+        qkv.relay(s)
+    if chips > 2:
+        up.relay(1)
+    qkv.finish(qkv_share)
     for s in range(2, chips - 1):
-        qkv.relay(s)
-    qkv.finish(qkv_share)
-    for s in range(1, chips - 1):
         up.relay(s)
-    normed_group.finish(normed_sum)
-    mixed_group.finish(mixed_sum)
+
+    normed_group.arrive()
+    tile = 64
+    second[me] = jnp.zeros((8, model), F32)
+
+    def norm_back(i, carry):
+        r = pl.ds(pl.multiple_of(i * tile, tile), tile)
+        values = tokens[r].astype(F32)
+        centre = values - jnp.mean(values, axis=-1, keepdims=True)
+        spread = jnp.mean(centre * centre, axis=-1, keepdims=True)
+        inverse = lax.rsqrt(spread + EPSILON)
+        xhat = centre * inverse
+        normed_grad = normed_group.total(r)
+        e = normed_grad * gain[...]
+        turned = e - jnp.mean(e, axis=-1, keepdims=True) - xhat * jnp.mean(e * xhat, axis=-1, keepdims=True)
+        cot_rows = cot[r].astype(F32)
+        input_grad[r] = (cot_rows + turned * inverse).astype(BF)
+        second[me, 0:1] += jnp.sum(normed_grad * xhat, axis=0, keepdims=True)
+        second[me, 1:2] += jnp.sum(normed_grad, axis=0, keepdims=True)
+        second[me, 2:3] += jnp.sum(cot_rows, axis=0, keepdims=True)
+        return carry
+
+    lax.fori_loop(0, rows // tile, norm_back, 0)
+    second[me, 3:4, :inner] = up_sum[...]
+    for n, vector in enumerate((query_sum, key_sum, value_sum)):
+        second[me, 4:5, n * width : (n + 1) * width] = vector[...]
+    first[mp] = second[me]
+
+    def copy_1(k):
+        return remote(
+            first.at[mp], first.at[mp], send_1.at[k], recv_1.at[mp], me, lax.rem(mp + k, mp_size)
+        )
+
+    def copy_2(k):
+        return remote(
+            second.at[me], second.at[me], send_2.at[k], recv_2.at[me], lax.rem(me + k, dp_size), mp
+        )
+
+    for k in range(1, mp_size):
+        copy_1(k).start()
+    mixed_group.arrive()
+
+    def add_up(i, carry):
+        r = pl.ds(pl.multiple_of(i * tile, tile), tile)
+        output[r] = (tokens[r].astype(F32) + mixed_group.total(r) + out_bias[...]).astype(BF)
+        return carry
+
+    lax.fori_loop(0, rows // tile, add_up, 0)
+    for k in range(1, mp_size):
+        origin = lax.rem(mp + k, mp_size)
+        remote(first.at[origin], first.at[origin], send_1.at[0], recv_1.at[origin], me, origin).wait_recv()
+    total = first[0]
+    for k in range(1, mp_size):
+        total = total + first[k]
+    second[me, 0:3] = total[0:3]
+    for k in range(1, dp_size):
+        copy_2(k).start()
     up.finish(up_share)
-    for stream in (qkv, up, normed_group, mixed_group):
-        stream.drain()
-
-
-def grad_stage(dp_size, mp_size, x_all, query_grad, key_grad, value_grad, pre_grad, mixed, normed):
-    length, model = x_all.shape
-    rows = length // mp_size
+    for k in range(1, dp_size):
+        origin = lax.rem(me + k, dp_size)
+        remote(second.at[origin], second.at[origin], send_2.at[0], recv_2.at[origin], origin, mp).wait_recv()
+    total = second[0]
+    for k in range(1, dp_size):
+        total = total + second[k]
+    totals[...] = total
+    for k in range(1, mp_size):
+        copy_1(k).wait_send()
+    for k in range(1, dp_size):
+        copy_2(k).wait_send()
+    up.drain_swap()
+    for stream_out in (qkv, up, normed_group, mixed_group):
+        stream_out.drain()
+
+
+def greet_all(dp_size, mp_size):
+    me, z, c, mp = place()
+    bar = pltpu.get_barrier_semaphore()
+    for k in range(1, mp_size):
+        pl.semaphore_signal(bar, 1, device_id=(me, lax.rem(mp + k, mp_size)), device_id_type=MESH)
+    for k in range(1, dp_size):
+        pl.semaphore_signal(bar, 1, device_id=(lax.rem(me + k, dp_size), mp), device_id_type=MESH)
+    pl.semaphore_wait(bar, mp_size + dp_size - 2)
+
+
+def grad_stage(dp_size, mp_size, hbm_args, grads, sums, tokens, cot, gain, out_bias):
+    x_all, pre_grad, attended, hidden_all = hbm_args[:4]
+    rows, model = tokens.shape
+    length = rows * mp_size
     depth, chips = model // dp_size, dp_size // 2
-    width, hidden = query_grad.shape[1], pre_grad.shape[1]
+    width, inner = grads[0].shape[1], pre_grad.shape[2]
+    wide = max(3 * width, inner)
     shape = jax.ShapeDtypeStruct
-    group = [
-        pltpu.VMEM((mp_size, rows, model), BF),
-        pltpu.SemaphoreType.DMA((mp_size,)),
-        pltpu.SemaphoreType.DMA((mp_size,)),
-    ]
+    semaphores = pltpu.SemaphoreType.DMA
+    blocks = (mp_size, dp_size)
+    group = [pltpu.VMEM((mp_size, rows, model), BF), semaphores(blocks), semaphores(blocks)]
     return pl.pallas_call(
         partial(grad_kernel, dp_size, mp_size),
         out_shape=(
             shape((depth, 3 * width), F32),
-            shape((depth, hidden), F32),
-            shape((rows, model), F32),
-            shape((rows, model), F32),
+            shape((depth, inner), F32),
+            shape((rows, model), BF),
+            shape((rows, model), BF),
+            shape((8, model), F32),
         ),
-        in_specs=[VM] * 5 + [ANY] * 2,
-        out_specs=[VM] * 4,
+        in_specs=[ANY] * len(hbm_args) + [VM] * 11,
+        out_specs=[VM] * 5,
         scratch_shapes=[
+            pltpu.VMEM((mp_size, rows, model), BF),
+            pltpu.VMEM((mp_size, rows, inner), BF),
+            pltpu.VMEM((mp_size, rows, model), BF),
+            pltpu.VMEM((length, width), BF),
+            pltpu.VMEM((mp_size, rows, inner), BF),
+            pltpu.VMEM((2, depth, inner), BF),
+            pltpu.VMEM((2, depth, 3 * width), BF),
             pltpu.VMEM((depth, length), BF),
+            pltpu.VMEM((chips, depth, wide), BF),
+            pltpu.VMEM((mp_size, 8, model), F32),
+            pltpu.VMEM((dp_size, 8, model), F32),
+            semaphores((4,)),
+            semaphores((2, 2)),
             *row_scatter_scratch(chips, depth, 3 * width),
-            *row_scatter_scratch(chips, depth, hidden),
+            *row_scatter_scratch(chips, depth, inner),
             *group,
             *group,
+            *[semaphores((n,)) for n in (mp_size, mp_size, dp_size, dp_size)],
         ],
         compiler_params=pltpu.CompilerParams(
-            collective_id=3, has_side_effects=True, vmem_limit_bytes=60 << 20
+            collective_id=3, has_side_effects=True, vmem_limit_bytes=63 << 20
         ),
         name="grad_stage",
-    )(
-        x_all,
-        query_grad,
-        key_grad,
-        value_grad,
-        pre_grad,
-        mixed.astype(BF).reshape(mp_size, rows, model),
-        normed.astype(BF).reshape(mp_size, rows, model),
-    )
-
-
-def right_product(left_side, right_side):
-    return lax.dot_general(
-        left_side, right_side, (((1,), (1,)), ((), ())), preferred_element_type=jnp.float32
-    )
+    )(*hbm_args, *grads, *sums, tokens, cot, gain.reshape(1, -1), out_bias.reshape(1, -1))
 
 
 def rows_product(left_side, right_side):
@@ -912,7 +1030,6 @@
     starts,
     cotangent,
 ):
-    token_float = tokens.astype(jnp.float32)
     dp_size, mp_size = lax.axis_size("dp"), lax.axis_size("mp")
     x_all, cot_all, up_all, hidden_all, slope_all = up_stage(
         dp_size, mp_size, tokens, ln_gain, ln_bias, cotangent, fc1_weight, fc1_bias
@@ -923,7 +1040,7 @@
     hidden_low = hidden_all.reshape(-1, up_all.shape[-1])
     slope = slope_all.reshape(hidden_low.shape)
     masters = (
-        qkv_weight.astype(jnp.bfloat16),
+        qkv_weight.astype(jnp.bfloat16).reshape(qkv_weight.shape[0], -1),
         dense_weight.astype(jnp.bfloat16),
         fc2_weight.astype(jnp.bfloat16),
     )
@@ -932,51 +1049,51 @@
         lax.all_gather(masters[1], "dp", axis=0, tiled=True),
         lax.all_gather(masters[2], "dp", axis=0, tiled=True),
     )
-    model_width = qkv_full.shape[0]
-    local_width = qkv_full.shape[2]
+    local_width = dense_full.shape[1]
     projected = jnp.dot(
-        gathered, qkv_full.reshape(model_width, 3 * local_width), preferred_element_type=jnp.float32
+        gathered, qkv_full, preferred_element_type=jnp.float32
     ) + qkv_bias.reshape(3 * local_width)
     attended_grad = jnp.dot(out_rows, dense_full, preferred_element_type=jnp.float32).astype(
         jnp.bfloat16
     )
+    down_grad = rows_product(out_rows, hidden_low).astype(jnp.bfloat16)
+    projected, down_grad = lax.optimization_barrier((projected, down_grad))
     attended, query_grad, key_grad, value_grad, query_sum, key_sum, value_sum = attention(
         projected, attended_grad, starts
     )
-    attn_part = right_product(attended, dense_full)
-    mlp_part = right_product(hidden_low, down_full)
     dense_grad = rows_product(out_rows, attended)
-    down_grad = rows_product(out_rows, hidden_low)
     hidden_grad = jnp.dot(out_rows, down_full, preferred_element_type=jnp.float32)
     pre_grad = (hidden_grad * slope).astype(jnp.bfloat16)
+    down_share = low_scatter(down_grad, "dp")
+    pre_grad, dense_grad, down_share = lax.optimization_barrier(
+        (pre_grad, dense_grad.astype(jnp.bfloat16), down_share)
+    )
     up_bias_grad = jnp.sum(pre_grad.astype(jnp.float32), axis=0)
-    projected_grad = jnp.concatenate([query_grad, key_grad, value_grad], axis=1)
-    qkv_bias_grad = jnp.concatenate([query_sum, key_sum, value_sum], axis=0)
-    attn_input = right_product(projected_grad, qkv_full.reshape(model_width, 3 * local_width))
-    mlp_input = right_product(pre_grad, up_full)
-    qkv_share, up_share, mixed_sum, normed_grad = grad_stage(
+    qkv_share, up_share, output, input_grad, totals = grad_stage(
         dp_size,
         mp_size,
-        gathered,
-        query_grad,
-        key_grad,
-        value_grad,
-        pre_grad,
-        attn_part + mlp_part,
-        attn_input + mlp_input,
+        (
+            x_all,
+            pre_grad.reshape(hidden_all.shape),
+            attended,
+            hidden_all,
+            qkv_full,
+            up_full,
+            dense_full,
+            down_full,
+        ),
+        (query_grad, key_grad, value_grad),
+        (query_sum, key_sum, value_sum, up_bias_grad.reshape(1, -1)),
+        tokens,
+        cotangent,
+        ln_gain,
+        dense_bias + fc2_bias,
     )
     qkv_share = qkv_share.reshape(-1, 3, local_width)
-    output = (token_float + mixed_sum + dense_bias + fc2_bias).astype(jnp.bfloat16)
-    norm_value, norm_back = jax.vjp(normalize, token_float, ln_gain, ln_bias)
-    token_grad, gain_grad, shift_grad = norm_back(normed_grad)
-    cot_float = cotangent.astype(jnp.float32)
-    input_grad = (cot_float + token_grad).astype(jnp.bfloat16)
-    out_bias_grad = jnp.sum(cot_float, axis=0)
-    (gain_total, shift_total, bias_total), (qkv_bias_total, up_bias_total) = all_sums(
-        dp_size, mp_size, (gain_grad, shift_grad, out_bias_grad), (qkv_bias_grad, up_bias_grad)
-    )
+    gain_total, shift_total, bias_total = totals[0], totals[1], totals[2]
+    up_bias_total = totals[3, : up_full.shape[1]]
+    qkv_bias_total = totals[4, : 3 * local_width].reshape(3, local_width)
     dense_share = low_scatter(dense_grad, "dp")
-    down_share = low_scatter(down_grad, "dp")
     return (
         output,
         input_grad,

time: 534 us -> 503 us (0.942)
  matrix products: 90.3 us -> 58.9 us
  waiting for transfers between devices: 0.11 us -> 30.7 us
  Pallas kernels: 390 us -> 360 us
    dot_general x5 -> x1, matrix products: 54.6 us -> 11.8 us  [body(): jnp.dot(gathered, qkv_full, preferred_element_type=jnp.float32)]
    reduce_scatter x2, waiting for transfers between devices: 0.01 us -> 30.6 us  [low_scatter(): lax.psum_scatter(partial_sums.astype(jnp.bfloat16), axis, scatter_dimensi...]
    pallas_call x1, Pallas kernels: 173 us -> 153 us  [grad_stage(): pl.pallas_call(partial(grad_kernel, dp_size, mp_size), out_shape=(shape((...]
    pallas_call x1 -> x0, Pallas kernels: 17 us -> none  [all_sums(): pl.pallas_call(partial(sums_kernel, dp_size, mp_size), out_shape=(shape(o...]
    dot_general x1, matrix products: 11.6 us -> 23 us  [body(): jnp.dot(out_rows, down_full, preferred_element_type=jnp.float32)]
    pallas_call x1, Pallas kernels: 161 us -> 169 us  [up_stage(): pl.pallas_call(partial(up_kernel, dp_size, mp_size), out_shape=outs, in_s...]
    unnamed x44 -> x38, local copies, waits for them, and re-layouts: 7.61 us -> 13.4 us
  transfers between devices with their start and end apart: 5 -> 5, of which waited for: 0 -> 1; matrix products, arithmetic and copies ran while one was open for 22% -> 15% of each run, Pallas kernels for 74% -> 73%
where the time goes in v5:
time: 503 us; the launch traced here: 495 us
  Pallas kernels  360 us (72%)
  matrix products  58.9 us (12%)
  waiting for transfers between devices  30.7 us (6%)
  local copies, waits for them, and re-layouts  18.2 us (4%)
  between operations  14.9 us (3%)
  other arithmetic  12.2 us (2%)
    pallas_call x1, Pallas kernels, up_stage(): pl.pallas_call(partial(up_kernel, dp_size, mp_size), out_shape=outs, in_s...  169 us
    pallas_call x1, Pallas kernels, grad_stage(): pl.pallas_call(partial(grad_kernel, dp_size, mp_size), out_shape=(shape((...  153 us
    pallas_call x1, Pallas kernels, attention(): pl.pallas_call(attention_kernel, grid=(pairs,), in_specs=[pl.BlockSpec(me...  37.7 us
    reduce_scatter x2, waiting for transfers between devices, low_scatter(): lax.psum_scatter(partial_sums.astype(jnp.bfloat16), axis, scatter_dimensi...  30.6 us
    dot_general x1, matrix products, body(): jnp.dot(out_rows, down_full, preferred_element_type=jnp.float32)  23 us
    dot_general x2, matrix products, rows_product(): lax.dot_general(left_side, right_side, (((0,), (0,)), ((), ())), preferre...  17.9 us
    unnamed x38, local copies, waits for them, and re-layouts  13.4 us
    dot_general x1, matrix products, body(): jnp.dot(gathered, qkv_full, preferred_element_type=jnp.float32)  11.8 us
  transfers between devices with their start and end apart: 5, of which 1 were waited for; matrix products, arithmetic and copies ran while one was open for 15% of the time, Pallas kernels for 73%

profile of v5, /device:TPU:0, one launch (start us, length us, event | category | flops | bytes accessed | tf_op | source)
XLA Modules:
  0.0 494.9 jit_solution(352739954098899876)
XLA Ops:
  7.2 0.0 all-gather.6.cloned.1.call-start
  7.2 1.8 copy.28
  9.1 0.0 copy-start.14
  9.1 1.2 copy.29
  10.2 0.0 all-gather.6.cloned.1.call-update
  10.3 0.0 all-gather.8.cloned.1.call-start
  10.3 0.7 convert_element_type.64
  11.1 0.0 all-gather.8.cloned.1.call-update
  11.1 0.0 all-gather.4.cloned.1.call-start
  11.1 1.1 convert_element_type.58
  12.3 0.0 all-gather.4.cloned.1.call-update
  12.3 0.0 reduce-scatter.3.cloned.1.call-start
  12.4 168.9 %up_stage.1 = (bf16[4,256,2048]{2,1,0:T(8,128)(2,1)}, bf16[4,256,2048]{2,1,0:T(8,128)(2,1)}, bf16[8,256,2048]{2,1,0:T(8,128)(2,1)}, bf16[4,256,2048]{2,1,0:T(8,128)(2,1)}, bf16[4,256,2048]{2,1,0:T(8,128)(2,1)}) custom-call(bf16[256,2048]{1,0:T(8,128)(2,1)} %tokens.3, f32[1,2048]{1,0:T(1,128)} %bitcast.38, f32[1,2048]{1,0:T(1,128)} %bitcast.44, ...), custom_call_target="tpu_custom_call" | custom-call | tf_op jit(solution)/shard_map/up_stage/pallas_call | solution.py:333
  181.2 14.1 %bitcast_convert_fusion = bf16[2048,2048]{1,0:T(8,128)(2,1)} fusion(bf16[4,256,2048]{2,1,0:T(8,128)(2,1)} %get-tuple-element.35, bf16[4,256,2048]{2,1,0:T(8,128)(2,1)} %get-tuple-element.37.hidden_all), kind=kOutput, calls=%fused_computation | convolution fusion | flops 8594128896 | bytes 16777216 | tf_op jit(solution)/shard_map/dot_general | solution.py:1007
  195.3 11.8 %convolution_add_fusion.q_in.k_in.v_in = f32[1024,1536]{1,0:T(8,128)} fusion(bf16[1024,2048]{1,0:T(8,128)(2,1)} %bitcast.34, bf16[2048,1536]{1,0:T(8,128)(2,1)} %all-gather.6.cloned.1.call-done.qkv_full, f32[1536]{0:T(1024)S(1)} %add.37), kind=kOutput, calls=%fused_computation.4 | convolution fusion | flops 6444023808 | bytes 16783360 | tf_op jit(solution)/shard_map/dot_general | solution.py:1053
  207.2 0.0 reduce-scatter.3.cloned.1.call-update
  207.2 0.3 reduce-scatter.5.cloned.1.call-start
  207.5 0.3 multiply_cosine_fusion
  207.9 0.2 copy.32
  208.1 0.2 copy.31
  209.1 0.1 negate_select_fusion
  209.1 1.2 pad_maximum_fusion.rot
  210.4 6.2 %convolution_convert_fusion.1.out_grad = bf16[1024,512]{1,0:T(8,128)(2,1)} fusion(bf16[1024,2048]{1,0:T(8,128)(2,1)} %bitcast.49, bf16[2048,512]{1,0:T(8,128)(2,1)} %all-gather.8.cloned.1.call-done.dense_full), kind=kOutput, calls=%fused_computation.7 | convolution fusion | flops 2148007936 | bytes 7340032 | tf_op jit(solution)/shard_map/dot_general | solution.py:1056
  216.6 37.7 %attention.1 = (bf16[1024,512]{1,0:T(8,128)(2,1)S(1)}, bf16[1024,512]{1,0:T(8,128)(2,1)S(1)}, bf16[1024,512]{1,0:T(8,128)(2,1)S(1)}, bf16[1024,512]{1,0:T(8,128)...) custom-call(s32[1]{0:T(128)S(6)} %copy.41.start, ...), custom_call_target="tpu_custom_call" | custom-call | flops 8589934592 | bytes 8388608 | tf_op jit(solution)/shard_map/attention/pallas_call | solution.py:472
  254.2 1.0 copy-done.1
  255.2 1.0 copy-done.2
  256.2 0.6 copy-done.3
  256.8 0.6 copy-done.4
  257.4 0.6 copy-done.5
  258.0 1.0 copy-done
  258.9 0.0 copy-done.15
  258.9 3.8 convolution_convert_fusion
  262.7 23.0 %fusion = bf16[1024,2048]{1,0:T(8,128)(2,1)} fusion(bf16[1024,2048]{1,0:T(8,128)(2,1)} %bitcast.52, bf16[1024,2048]{1,0:T(8,128)(2,1)} %bitcast.50, bf16[2048,2048]{1,0:T(8,128)(2,1)} %all-gather.4.cloned.1.call-done.down_full), kind=kOutput, calls=%fused_computation.2 | convolution fusion | flops 8596226048 | bytes 20971520 | tf_op jit(solution)/shard_map/dot_general | solution.py:1065
  285.8 30.6 %reduce-scatter.3.cloned.1.call-done = bf16[256,2048]{1,0:T(8,128)(2,1)} async-done(((bf16[2048,2048]{1,0:T(8,128)(2,1)}), bf16[256,2048]{1,0:T(8,128)(2,1)}) %reduce-scatter.3.cloned.1.call-update) | async-done | bytes 1048592 | tf_op jit(solution)/shard_map/reduce_scatter | solution.py:1013
  316.4 2.8 convert_element_type.69
  319.2 0.0 reduce-scatter.5.cloned.1.call-update
  319.2 0.6 add.41
  319.8 3.4 convert_reduce_fusion
  323.3 153.0 %grad_stage.1 = (f32[256,1536]{1,0:T(8,128)}, f32[256,2048]{1,0:T(8,128)}, bf16[256,2048]{1,0:T(8,128)(2,1)}, bf16[256,2048]{1,0:T(8,128)(2,1)}, f32[8,2048]{1,0:T(8,128)}) custom-call(bf16[4,256,2048]{2,1,0:T(8,128)(2,1)} %get-tuple-element.34.x_all, bf16[4,256,2048]{2,1,0:T(8,128)(2,1)} %bitcast.31, bf16[1024,512]{1,0:T(8,128)(2,1)} %copy-done, ...), custom_call_target="tpu_custom_call" | custom-call | tf_op jit(solution)/shard_map/grad_stage/pallas_call | solution.py:968
  476.3 2.0 copy.34
  478.3 1.6 copy.35
  479.9 0.6 fusion.1
  480.6 0.6 reshape_squeeze.3
  481.2 1.8 convert_element_type.71
  483.0 0.6 copy.42
  483.6 2.3 copy.43
  485.9 1.0 copy.44
  486.8 1.3 copy.45
  (37 shorter events, 0.2 us)
Async XLA Ops:
  7.2 3.1 copy-start.9
  7.2 4.0 copy-start.6
  7.2 188.1 %all-gather.6.cloned.1.call-start = ((), (), s32[]{:S(2)}) async-start(), calls=%async_computation.3 | async-start | bytes 7077888 | tf_op jit(solution)/shard_map/all_gather | solution.py:1048
  9.1 3.3 copy-start.14
  10.3 200.1 %all-gather.8.cloned.1.call-start = ((), (), s32[]{:S(2)}) async-start(), calls=%async_computation.4 | async-start | bytes 2359296 | tf_op jit(solution)/shard_map/all_gather | solution.py:1049
  11.1 251.6 %all-gather.4.cloned.1.call-start = ((), (), s32[]{:S(2)}) async-start(), calls=%async_computation.2 | async-start | bytes 9437184 | tf_op jit(solution)/shard_map/all_gather | solution.py:1050
  12.3 304.1 %reduce-scatter.3.cloned.1.call-start = ((), (), s32[]{:S(2)}) async-start(), calls=%async_computation.5 | async-start | bytes 9437184 | tf_op jit(solution)/shard_map/reduce_scatter | solution.py:1013
  207.2 274.0 %reduce-scatter.5.cloned.1.call-start = ((), (), s32[]{:S(2)}) async-start(), calls=%async_computation.6 | async-start | bytes 2359296 | tf_op jit(solution)/shard_map/reduce_scatter | solution.py:1013
  216.6 42.4 %copy-start.15 = (bf16[4,256,2048]{2,1,0:T(8,128)(2,1)S(1)}, bf16[4,256,2048]{2,1,0:T(8,128)(2,1)}, u32[]{:S(2)}) copy-start(bf16[4,256,2048]{2,1,0:T(8,128)(2,1)} %get-tuple-element.35) | copy-start | bytes 12582916
  254.2 1.0 copy-start.1
  255.2 1.1 copy-start.2
  256.2 0.6 copy-start.3
  256.8 0.6 copy-start.4
  257.4 0.6 copy-start.5
  258.0 1.0 copy-start
  285.8 33.5 %copy-start.12 = (f32[2048]{0:T(1024)S(1)}, f32[2048]{0:T(1024)}, u32[]{:S(2)}) copy-start(f32[2048]{0:T(1024)} %param.19) | copy-start | bytes 24580
  285.8 33.5 %copy-start.13 = (f32[2048]{0:T(1024)S(1)}, f32[2048]{0:T(1024)}, u32[]{:S(2)}) copy-start(f32[2048]{0:T(1024)} %param.23) | copy-start | bytes 24580
  476.3 3.6 copy-start.11
  476.3 9.6 %copy-start.8 = (bf16[256,2048]{1,0:T(8,128)(2,1)S(1)}, bf16[256,2048]{1,0:T(8,128)(2,1)}, u32[]{:S(2)}) copy-start(bf16[256,2048]{1,0:T(8,128)(2,1)} %get-tuple-element.127) | copy-start | bytes 3145732
  479.9 7.0 %copy-start.7 = (f32[256,2048]{1,0:T(8,128)S(1)}, f32[256,2048]{1,0:T(8,128)}, u32[]{:S(2)}) copy-start(f32[256,2048]{1,0:T(8,128)} %get-tuple-element.134) | copy-start | bytes 6291460
  480.5 7.6 %copy-start.10 = (f32[1,2048]{1,0:T(1,128)}, f32[1,2048]{1,0:T(1,128)S(1)}, u32[]{:S(2)}) copy-start(f32[1,2048]{1,0:T(1,128)S(1)} %get-tuple-element.83) | copy-start | bytes 24580
Sparse Core Ops, SparseCore 0:
  10.4 92.3 all-gather.5
  104.9 32.5 all-gather.7
  139.7 85.7 all-gather.3
  227.6 88.7 reduce-scatter.2
  319.3 43.2 reduce-scatter.4

commit v6 on v5

--- a/solution.py
+++ b/solution.py
@@ -487,7 +487,7 @@
             pltpu.VMEM((length, 128), F32),
             pltpu.VMEM((length, 128), F32),
         ],
-        compiler_params=pltpu.CompilerParams(vmem_limit_bytes=50 << 20),
+        compiler_params=pltpu.CompilerParams(vmem_limit_bytes=62 << 20),
         cost_estimate=pl.CostEstimate(
             flops=16 * length * length * width, bytes_accessed=16 * length * width, transcendentals=length * length * width // 64
         ),
@@ -741,6 +741,7 @@
     pre_grad,
     attended,
     hidden_all,
+    cot_all,
     qkv_full,
     up_full,
     dense_full,
@@ -756,6 +757,7 @@
     cot,
     gain,
     out_bias,
+    dense_share,
     qkv_share,
     up_share,
     output,
@@ -781,10 +783,14 @@
     rows, model = tokens.shape
     width, inner = query_grad.shape[1], up_sum.shape[1]
     depth = model // dp_size
-    qkv_scratch, up_scratch, rest = scratch[:7], scratch[7:14], scratch[14:]
+    qkv_scratch, up_scratch, dense_scratch, rest = scratch[:7], scratch[7:14], scratch[14:21], scratch[21:]
     grads = (query_grad, key_grad, value_grad)
     give_qkv = give.at[:, :, pl.ds(0, 3 * width)]
     give_up = give.at[:, :, pl.ds(0, inner)]
+    give_dense = give.at[:, :, pl.ds(0, width)]
+    dense = RowScatter(
+        chips, mixed_buf, (attended_buf,), flip, give_dense, *dense_scratch[:2], dense_scratch[2:]
+    )
     qkv = RowScatter(chips, x_buf, grads, flip, give_qkv, *qkv_scratch[:2], qkv_scratch[2:])
     up = RowScatter(chips, x_buf, (pre,), flip, give_up, *up_scratch[:2], up_scratch[2:])
     normed_group = GroupScatter(mp_size, dp_size, x_buf, *rest[:3])
@@ -794,7 +800,15 @@
     loads = [
         pltpu.make_async_copy(source, target, load_sem.at[n])
         for n, (source, target) in enumerate(
-            ((x_all, x_buf), (pre_grad, pre), (attended, attended_buf), (hidden_all, hidden_buf))
+            (
+                (cot_all, mixed_buf),
+                (attended, attended_buf),
+                (x_all, x_buf),
+                (pre_grad, pre),
+                (hidden_all, hidden_buf),
+                (tokens, rest[0].at[mp]),
+                (cot, rest[3].at[mp]),
+            )
         )
     ]
     for load in loads:
@@ -847,23 +861,30 @@
         copy.start()
     greet_all(dp_size, mp_size)
     loads[0].wait()
+    loads[1].wait()
+    dense.swap()
+    dense.collect()
+    dense.drain_swap()
+    loads[2].wait()
     qkv.swap()
     qkv.collect()
-    loads[2].wait()
-    loads[3].wait()
+    if chips > 2:
+        dense.relay(1)
+    loads[4].wait()
     partial_sums(mixed_stream, hidden_buf, (attended_buf,), mixed_buf, mixed_group)
     for copy in normed_stream(0):
         copy.start()
+    for s in range(2, chips - 1):
+        dense.relay(s)
     if chips > 2:
         qkv.relay(1)
-    loads[1].wait()
+    loads[3].wait()
     qkv.drain_swap()
     up.swap()
     up.collect()
-    if chips > 3:
-        qkv.relay(2)
+    dense.finish(dense_share)
     partial_sums(normed_stream, pre, grads, x_buf, normed_group)
-    for s in range(3, chips - 1):
+    for s in range(2, chips - 1):
         qkv.relay(s)
     if chips > 2:
         up.relay(1)
@@ -872,12 +893,14 @@
         up.relay(s)
 
     normed_group.arrive()
+    loads[5].wait()
+    loads[6].wait()
     tile = 64
     second[me] = jnp.zeros((8, model), F32)
 
     def norm_back(i, carry):
         r = pl.ds(pl.multiple_of(i * tile, tile), tile)
-        values = tokens[r].astype(F32)
+        values = rest[0][mp, r].astype(F32)
         centre = values - jnp.mean(values, axis=-1, keepdims=True)
         spread = jnp.mean(centre * centre, axis=-1, keepdims=True)
         inverse = lax.rsqrt(spread + EPSILON)
@@ -885,7 +908,7 @@
         normed_grad = normed_group.total(r)
         e = normed_grad * gain[...]
         turned = e - jnp.mean(e, axis=-1, keepdims=True) - xhat * jnp.mean(e * xhat, axis=-1, keepdims=True)
-        cot_rows = cot[r].astype(F32)
+        cot_rows = rest[3][mp, r].astype(F32)
         input_grad[r] = (cot_rows + turned * inverse).astype(BF)
         second[me, 0:1] += jnp.sum(normed_grad * xhat, axis=0, keepdims=True)
         second[me, 1:2] += jnp.sum(normed_grad, axis=0, keepdims=True)
@@ -914,7 +937,7 @@
 
     def add_up(i, carry):
         r = pl.ds(pl.multiple_of(i * tile, tile), tile)
-        output[r] = (tokens[r].astype(F32) + mixed_group.total(r) + out_bias[...]).astype(BF)
+        output[r] = (rest[0][mp, r].astype(F32) + mixed_group.total(r) + out_bias[...]).astype(BF)
         return carry
 
     lax.fori_loop(0, rows // tile, add_up, 0)
@@ -940,7 +963,7 @@
     for k in range(1, dp_size):
         copy_2(k).wait_send()
     up.drain_swap()
-    for stream_out in (qkv, up, normed_group, mixed_group):
+    for stream_out in (dense, qkv, up, normed_group, mixed_group):
         stream_out.drain()
 
 
@@ -955,7 +978,7 @@
 
 
 def grad_stage(dp_size, mp_size, hbm_args, grads, sums, tokens, cot, gain, out_bias):
-    x_all, pre_grad, attended, hidden_all = hbm_args[:4]
+    pre_grad = hbm_args[1]
     rows, model = tokens.shape
     length = rows * mp_size
     depth, chips = model // dp_size, dp_size // 2
@@ -968,14 +991,15 @@
     return pl.pallas_call(
         partial(grad_kernel, dp_size, mp_size),
         out_shape=(
+            shape((depth, width), F32),
             shape((depth, 3 * width), F32),
             shape((depth, inner), F32),
             shape((rows, model), BF),
             shape((rows, model), BF),
             shape((8, model), F32),
         ),
-        in_specs=[ANY] * len(hbm_args) + [VM] * 11,
-        out_specs=[VM] * 5,
+        in_specs=[ANY] * len(hbm_args) + [VM] * 7 + [ANY] * 2 + [VM] * 2,
+        out_specs=[VM] * 6,
         scratch_shapes=[
             pltpu.VMEM((mp_size, rows, model), BF),
             pltpu.VMEM((mp_size, rows, inner), BF),
@@ -988,16 +1012,17 @@
             pltpu.VMEM((chips, depth, wide), BF),
             pltpu.VMEM((mp_size, 8, model), F32),
             pltpu.VMEM((dp_size, 8, model), F32),
-            semaphores((4,)),
+            semaphores((7,)),
             semaphores((2, 2)),
             *row_scatter_scratch(chips, depth, 3 * width),
             *row_scatter_scratch(chips, depth, inner),
+            *row_scatter_scratch(chips, depth, width),
             *group,
             *group,
             *[semaphores((n,)) for n in (mp_size, mp_size, dp_size, dp_size)],
         ],
         compiler_params=pltpu.CompilerParams(
-            collective_id=3, has_side_effects=True, vmem_limit_bytes=63 << 20
+            collective_id=3, has_side_effects=True, vmem_limit_bytes=67043328
         ),
         name="grad_stage",
     )(*hbm_args, *grads, *sums, tokens, cot, gain.reshape(1, -1), out_bias.reshape(1, -1))
@@ -1061,15 +1086,11 @@
     attended, query_grad, key_grad, value_grad, query_sum, key_sum, value_sum = attention(
         projected, attended_grad, starts
     )
-    dense_grad = rows_product(out_rows, attended)
     hidden_grad = jnp.dot(out_rows, down_full, preferred_element_type=jnp.float32)
     pre_grad = (hidden_grad * slope).astype(jnp.bfloat16)
     down_share = low_scatter(down_grad, "dp")
-    pre_grad, dense_grad, down_share = lax.optimization_barrier(
-        (pre_grad, dense_grad.astype(jnp.bfloat16), down_share)
-    )
     up_bias_grad = jnp.sum(pre_grad.astype(jnp.float32), axis=0)
-    qkv_share, up_share, output, input_grad, totals = grad_stage(
+    dense_share, qkv_share, up_share, output, input_grad, totals = grad_stage(
         dp_size,
         mp_size,
         (
@@ -1077,6 +1098,7 @@
             pre_grad.reshape(hidden_all.shape),
             attended,
             hidden_all,
+            cot_all,
             qkv_full,
             up_full,
             dense_full,
@@ -1093,7 +1115,6 @@
     gain_total, shift_total, bias_total = totals[0], totals[1], totals[2]
     up_bias_total = totals[3, : up_full.shape[1]]
     qkv_bias_total = totals[4, : 3 * local_width].reshape(3, local_width)
-    dense_share = low_scatter(dense_grad, "dp")
     return (
         output,
         input_grad,

time: 503 us -> 484 us (0.962)
  Pallas kernels: 360 us -> 397 us
  waiting for transfers between devices: 30.7 us -> 0.09 us
  matrix products: 58.9 us -> 47.3 us
  other arithmetic: 12.2 us -> 7.08 us
    pallas_call x1, Pallas kernels: 153 us -> 190 us  [grad_stage(): pl.pallas_call(partial(grad_kernel, dp_size, mp_size), out_shape=(shape((...]
    reduce_scatter x2 -> x1, waiting for transfers between devices: 30.6 us -> 0.01 us  [low_scatter(): lax.psum_scatter(partial_sums.astype(jnp.bfloat16), axis, scatter_dimensi...]
    dot_general x1, matrix products: 23 us -> 15.2 us  [body(): jnp.dot(out_rows, down_full, preferred_element_type=jnp.float32)]
    unnamed x38 -> x27, local copies, waits for them, and re-layouts: 13.4 us -> 9.47 us
    dot_general x2 -> x1, matrix products: 17.9 us -> 14.1 us  [rows_product(): lax.dot_general(left_side, right_side, (((0,), (0,)), ((), ())), preferre...]
  transfers between devices with their start and end apart: 5 -> 4, of which waited for: 1 -> 0; matrix products, arithmetic and copies ran while one was open for 15% -> 12% of each run, Pallas kernels for 73% -> 83%
where the time goes in v6:
time: 484 us; the launch traced here: 481 us
  Pallas kernels  397 us (82%)
  matrix products  47.3 us (10%)
  between operations  15.1 us (3%)
  local copies, waits for them, and re-layouts  14.3 us (3%)
  other arithmetic  7.08 us (1%)
    pallas_call x1, Pallas kernels, grad_stage(): pl.pallas_call(partial(grad_kernel, dp_size, mp_size), out_shape=(shape((...  190 us
    pallas_call x1, Pallas kernels, up_stage(): pl.pallas_call(partial(up_kernel, dp_size, mp_size), out_shape=outs, in_s...  169 us
    pallas_call x1, Pallas kernels, attention(): pl.pallas_call(attention_kernel, grid=(pairs,), in_specs=[pl.BlockSpec(me...  37.4 us
    dot_general x1, matrix products, body(): jnp.dot(out_rows, down_full, preferred_element_type=jnp.float32)  15.2 us
    dot_general x1, matrix products, rows_product(): lax.dot_general(left_side, right_side, (((0,), (0,)), ((), ())), preferre...  14.1 us
    dot_general x1, matrix products, body(): jnp.dot(gathered, qkv_full, preferred_element_type=jnp.float32)  11.9 us
  transfers between devices with their start and end apart: 4, of which 0 were waited for; matrix products, arithmetic and copies ran while one was open for 12% of the time, Pallas kernels for 83%

profile of v6, /device:TPU:0, one launch (start us, length us, event | category | flops | bytes accessed | tf_op | source)
XLA Modules:
  0.0 480.8 jit_solution(3028290654777370406)
XLA Ops:
  7.2 0.0 copy-start.3
  7.2 0.0 copy-start
  7.2 0.0 all-gather.6.cloned.1.call-start
  7.2 1.8 copy.28
  9.1 0.0 copy-start.9
  9.1 1.2 copy.29
  10.2 0.0 all-gather.6.cloned.1.call-update
  10.3 0.0 all-gather.8.cloned.1.call-start
  10.3 0.0 copy-done.3
  10.3 0.7 convert_element_type.58
  11.1 0.0 all-gather.8.cloned.1.call-update
  11.1 0.0 all-gather.4.cloned.1.call-start
  11.1 0.0 copy-done
  11.1 1.1 convert_element_type.52
  12.3 0.0 all-gather.4.cloned.1.call-update
  12.3 0.0 reduce-scatter.2.cloned.1.call-start
  12.3 0.0 copy-done.9
  12.4 169.1 %up_stage.1 = (bf16[4,256,2048]{2,1,0:T(8,128)(2,1)}, bf16[4,256,2048]{2,1,0:T(8,128)(2,1)}, bf16[8,256,2048]{2,1,0:T(8,128)(2,1)}, bf16[4,256,2048]{2,1,0:T(8,128)(2,1)}, bf16[4,256,2048]{2,1,0:T(8,128)(2,1)}) custom-call(bf16[256,2048]{1,0:T(8,128)(2,1)} %tokens.3, f32[1,2048]{1,0:T(1,128)} %bitcast.38, f32[1,2048]{1,0:T(1,128)} %bitcast.43, ...), custom_call_target="tpu_custom_call" | custom-call | tf_op jit(solution)/shard_map/up_stage/pallas_call | solution.py:333
  181.4 14.1 %bitcast_convert_fusion = bf16[2048,2048]{1,0:T(8,128)(2,1)} fusion(bf16[4,256,2048]{2,1,0:T(8,128)(2,1)} %get-tuple-element.33.cot_all, bf16[4,256,2048]{2,1,0:T(8,128)(2,1)} %get-tuple-element.35.hidden_all), kind=kOutput, calls=%fused_computation | convolution fusion | flops 8594128896 | bytes 16777216 | tf_op jit(solution)/shard_map/dot_general | solution.py:1032
  195.5 11.9 %convolution_add_fusion.q_in.k_in.v_in = f32[1024,1536]{1,0:T(8,128)} fusion(bf16[1024,2048]{1,0:T(8,128)(2,1)} %bitcast.31, bf16[2048,1536]{1,0:T(8,128)(2,1)} %all-gather.6.cloned.1.call-done.qkv_full, f32[1536]{0:T(1024)S(1)} %add.35), kind=kOutput, calls=%fused_computation.4 | convolution fusion | flops 6444023808 | bytes 16783360 | tf_op jit(solution)/shard_map/dot_general | solution.py:1078
  207.4 0.0 reduce-scatter.2.cloned.1.call-update
  207.4 0.3 multiply_cosine_fusion
  207.8 0.2 copy.32
  208.0 0.2 copy.31
  208.9 0.0 copy-done.7
  208.9 0.0 copy-done.8
  208.9 0.6 add.39
  209.6 0.1 negate_select_fusion
  209.7 1.2 pad_maximum_fusion.rot
  210.9 6.2 %convolution_convert_fusion.out_grad = bf16[1024,512]{1,0:T(8,128)(2,1)} fusion(bf16[1024,2048]{1,0:T(8,128)(2,1)} %bitcast.32, bf16[2048,512]{1,0:T(8,128)(2,1)} %all-gather.8.cloned.1.call-done.dense_full), kind=kOutput, calls=%fused_computation.6 | convolution fusion | flops 2148007936 | bytes 7340032 | tf_op jit(solution)/shard_map/dot_general | solution.py:1081
  217.1 37.4 %attention.1 = (bf16[1024,512]{1,0:T(8,128)(2,1)}, bf16[1024,512]{1,0:T(8,128)(2,1)}, bf16[1024,512]{1,0:T(8,128)(2,1)}, bf16[1024,512]{1,0:T(8,128)(2,1)}, f32[...) custom-call(s32[1]{0:T(128)S(6)} %copy.42.start, f32[1024,1536]{1,0:T(8,128)} %convolution_add_fusion.q_in.k_in.v_in, ...), custom_call_target="tpu_custom_call" | custom-call | flops 8589934592 | bytes 8388608 | tf_op jit(solution)/shard_map/attention/pallas_call | solution.py:472
  254.5 0.0 all-gather.4.cloned.1.call-done.down_full
  254.5 15.2 %convert_reduce_fusion = (f32[2048]{0:T(1024)}, bf16[1024,2048]{1,0:T(8,128)(2,1)}) fusion(bf16[1024,2048]{1,0:T(8,128)(2,1)} %bitcast.49, bf16[1024,2048]{1,0:T(8,128)(2,1)} %bitcast.33, bf16[2048,2048]{1,0:T(8,128)(2,1)} %all-gather.4.cloned.1.call-done.down_full), kind=kOutput, calls=%fused_computation.3 | convolution fusion | flops 8600418304 | bytes 20979712 | tf_op jit(solution)/shard_map/dot_general | solution.py:1089
  269.7 190.3 %grad_stage.1 = (f32[256,512]{1,0:T(8,128)}, f32[256,1536]{1,0:T(8,128)}, f32[256,2048]{1,0:T(8,128)}, bf16[256,2048]{1,0:T(8,128)(2,1)}, bf16[256,2048]{1,0:T(8,128)(2,1)}, /*index=5*/f32[8,2048]{1,0:T(8,128)}) custom-call(bf16[4,256,2048]{2,1,0:T(8,128)(2,1)} %get-tuple-element.32.x_all, bf16[4,256,2048]{2,1,0:T(8,128)(2,1)} %bitcast.34, ...), custom_call_target="tpu_custom_call" | custom-call | tf_op jit(solution)/shard_map/grad_stage/pallas_call | solution.py:991
  460.1 0.0 copy-start.6
  460.1 1.9 copy.34
  462.0 0.0 copy-start.2
  462.0 1.6 copy.35
  463.6 0.0 copy-done.6
  463.6 0.6 fusion.1
  464.3 0.6 reshape_squeeze.3
  464.9 2.9 convert_element_type.63
  467.8 0.6 copy.43
  468.4 2.3 copy.44
  470.7 1.0 copy.45
  471.7 0.8 copy.46
  472.5 0.0 copy-done.5
  472.5 1.3 copy.47
  (20 shorter events, 0.2 us)
Async XLA Ops:
  7.2 3.1 copy-start.3
  7.2 4.0 copy-start
  7.2 188.3 %all-gather.6.cloned.1.call-start = ((), (), s32[]{:S(2)}) async-start(), calls=%async_computation.2 | async-start | bytes 7077888 | tf_op jit(solution)/shard_map/all_gather | solution.py:1073
  9.1 3.3 copy-start.9
  10.3 200.6 %all-gather.8.cloned.1.call-start = ((), (), s32[]{:S(2)}) async-start(), calls=%async_computation.3 | async-start | bytes 2359296 | tf_op jit(solution)/shard_map/all_gather | solution.py:1074
  11.1 243.5 %all-gather.4.cloned.1.call-start = ((), (), s32[]{:S(2)}) async-start(), calls=%async_computation.1 | async-start | bytes 9437184 | tf_op jit(solution)/shard_map/all_gather | solution.py:1075
  12.3 452.6 %reduce-scatter.2.cloned.1.call-start = ((), (), s32[]{:S(2)}) async-start(), calls=%async_computation.4 | async-start | bytes 9437184 | tf_op jit(solution)/shard_map/reduce_scatter | solution.py:1038
  207.4 1.5 copy-start.7
  207.4 1.5 copy-start.8
  460.1 3.5 copy-start.6
  462.0 8.7 %copy-start.2 = (bf16[256,2048]{1,0:T(8,128)(2,1)S(1)}, bf16[256,2048]{1,0:T(8,128)(2,1)}, u32[]{:S(2)}) copy-start(bf16[256,2048]{1,0:T(8,128)(2,1)} %get-tuple-element.125) | copy-start | bytes 3145732
  464.2 8.3 %copy-start.5 = (f32[1,2048]{1,0:T(1,128)}, f32[1,2048]{1,0:T(1,128)S(1)}, u32[]{:S(2)}) copy-start(f32[1,2048]{1,0:T(1,128)S(1)} %get-tuple-element.79) | copy-start | bytes 24580
  464.9 7.6 %copy-start.1 = (f32[256,2048]{1,0:T(8,128)S(1)}, f32[256,2048]{1,0:T(8,128)}, u32[]{:S(2)}) copy-start(f32[256,2048]{1,0:T(8,128)} %get-tuple-element.132) | copy-start | bytes 6291460
  464.9 6.8 %copy-start.4 = (f32[256,512]{1,0:T(8,128)S(1)}, f32[256,512]{1,0:T(8,128)}, u32[]{:S(2)}) copy-start(f32[256,512]{1,0:T(8,128)} %get-tuple-element.130) | copy-start | bytes 1572868
Sparse Core Ops, SparseCore 0:
  10.4 92.3 all-gather.5
  104.9 32.5 all-gather.7
  139.7 85.7 all-gather.3
  227.6 118.1 reduce-scatter.1

commit v7 on v6

--- a/solution.py
+++ b/solution.py
@@ -223,11 +223,17 @@
     cot,
     up_master,
     up_bias,
+    qkv_bias,
+    qkv_low,
+    dense_low,
     x_out,
     cot_out,
     up_out,
     hidden_out,
     slope_out,
+    qkv_out,
+    dense_out,
+    projected_out,
     x_all,
     up_all,
     acc,
@@ -238,6 +244,8 @@
     chips = dp_size // 2
     row_sems, x_sems, cot_sems = sems[0:4], sems[4:6], sems[6:8]
     out_sem = sems[8]
+    qkv_gather = RowGather(chips, qkv_low, qkv_out, sems[9:13])
+    dense_gather = RowGather(chips, dense_low, dense_out, sems[13:17])
     me, z, c, mp = place()
     rows = tokens.shape[0]
     length = rows * mp_size
@@ -257,6 +265,12 @@
     weights.start()
     own_cot = pltpu.make_async_copy(cot, cot_out.at[mp], out_sem.at[0])
     own_cot.start()
+    own_blocks = [
+        pltpu.make_async_copy(qkv_low, qkv_out.at[me], out_sem.at[5]),
+        pltpu.make_async_copy(dense_low, dense_out.at[me], out_sem.at[6]),
+    ]
+    for copy in own_blocks:
+        copy.start()
 
     def product(oz, first=False):
         cols = pl.ds(pl.multiple_of(oz * (2 * depth), 2 * depth), 2 * depth)
@@ -276,8 +290,8 @@
         lax.fori_loop(0, mp_size * (width // 512), tile, 0)
 
     x_gather.relay()
+    weights.stage(1)
     x_gather.finish()
-    weights.stage(1)
     cot_gather.start()
     x_copy = pltpu.make_async_copy(x_all, x_out, out_sem.at[1])
     x_copy.start()
@@ -286,6 +300,8 @@
     for k in range(1, chips):
         if k > 1:
             weights.stage(k)
+        if k == min(2, chips - 1):
+            qkv_gather.start()
         for oz, valid in ((z + k, z + k < chips), (z - k, z - k >= 0)):
 
             @pl.when(valid)
@@ -297,6 +313,8 @@
             cot_gather.relay()
     up_copy = pltpu.make_async_copy(up_all, up_out, out_sem.at[2])
     up_copy.start()
+    qkv_gather.stage(1)
+    dense_gather.start()
 
     def finish(i, carry):
         r, n = i // (width // 512), lax.rem(i, width // 512)
@@ -311,15 +329,42 @@
     slope_copy = pltpu.make_async_copy(slope, slope_out, out_sem.at[4])
     hidden_copy.start()
     slope_copy.start()
+    for k in range(2, chips):
+        qkv_gather.stage(k)
+        dense_gather.stage(k - 1)
+    for oz in range(chips):
+        qkv_gather.wait_block(2 * oz + 1 - c)
+    weights.drain()
+    up_copy.wait()
+    own_blocks[0].wait()
+    thirds = qkv_low.shape[1]
+    qkv_load = pltpu.make_async_copy(qkv_out, up_all.at[:, :, pl.ds(0, thirds)], out_sem.at[5])
+    qkv_load.start()
+    qkv_load.wait()
+    part = 512 if thirds % 512 == 0 else 256
+
+    def project(i, carry):
+        r, n = i // (thirds // part), lax.rem(i, thirds // part)
+        n0 = pl.ds(pl.multiple_of(n * part, part), part)
+        acc[r, :, n0] = dot(x_all[r], up_all[:, :, n0].reshape(dp_size * depth, part)) + qkv_bias[:, n0]
+        return carry
+
+    lax.fori_loop(0, mp_size * (thirds // part), project, 0)
+    projected_copy = pltpu.make_async_copy(acc.at[:, :, pl.ds(0, thirds)], projected_out, out_sem.at[2])
+    projected_copy.start()
+    dense_gather.stage(chips - 1)
+    for oz in range(chips):
+        dense_gather.wait_block(2 * oz + 1 - c)
+    qkv_gather.drain()
+    dense_gather.drain()
     cot_gather.finish()
-    weights.drain()
     x_gather.drain()
     cot_gather.drain()
-    for copy in (own_cot, x_copy, up_copy, hidden_copy, slope_copy):
+    for copy in (own_cot, x_copy, projected_copy, hidden_copy, slope_copy, own_blocks[1]):
         copy.wait()
 
 
-def up_stage(dp_size, mp_size, tokens, gain, shift, cot, up_master, up_bias):
+def up_stage(dp_size, mp_size, tokens, gain, shift, cot, up_master, up_bias, qkv_bias, qkv_low, dense_low):
     rows, model = tokens.shape
     depth, width = up_master.shape
     shape = jax.ShapeDtypeStruct
@@ -329,12 +374,15 @@
         shape((dp_size, depth, width), BF),
         shape((mp_size, rows, width), BF),
         shape((mp_size, rows, width), BF),
+        shape((dp_size, *qkv_low.shape), BF),
+        shape((dp_size, *dense_low.shape), BF),
+        shape((mp_size, rows, qkv_low.shape[1]), F32),
     )
     return pl.pallas_call(
         partial(up_kernel, dp_size, mp_size),
         out_shape=outs,
-        in_specs=[VM] * 6,
-        out_specs=[ANY] * 5,
+        in_specs=[VM] * 7 + [ANY] * 2,
+        out_specs=[ANY] * 8,
         scratch_shapes=[
             pltpu.VMEM((mp_size, rows, model), BF),
             pltpu.VMEM((dp_size, depth, width), BF),
@@ -344,29 +392,63 @@
             *row_gather_sems(dp_size),
             *group_gather_sems(mp_size),
             *group_gather_sems(mp_size),
-            pltpu.SemaphoreType.DMA((5,)),
+            pltpu.SemaphoreType.DMA((7,)),
+            *row_gather_sems(dp_size),
+            *row_gather_sems(dp_size),
         ],
         compiler_params=pltpu.CompilerParams(
             collective_id=1, has_side_effects=True, vmem_limit_bytes=58 << 20
         ),
         name="up_stage",
-    )(tokens, gain.reshape(1, -1), shift.reshape(1, -1), cot, up_master, up_bias.reshape(1, -1))
-
-
-def attention_kernel(start, q_in, k_in, v_in, out_grad, rot, out, q_grad, k_grad, v_grad, q_sum, k_sum, v_sum, bias, k_acc, v_acc):
+    )(tokens, gain.reshape(1, -1), shift.reshape(1, -1), cot, up_master, up_bias.reshape(1, -1), qkv_bias, qkv_low, dense_low)
+
+
+def attention_kernel(
+    dp_size,
+    mp_size,
+    pairs,
+    bias,
+    q_in,
+    k_in,
+    v_in,
+    out_grad,
+    rot,
+    cot_all,
+    hidden,
+    down_low,
+    out,
+    q_grad,
+    k_grad,
+    v_grad,
+    q_sum,
+    k_sum,
+    v_sum,
+    down_share,
+    down_full,
+    k_acc,
+    v_acc,
+    flip,
+    give,
+    own_sem,
+    *scratch,
+):
     length = q_in.shape[0]
     block = 256
     blocks = length // block
 
+    chips = dp_size // 2
+    me, z, c, mp = place()
+    down = RowScatter(chips, cot_all, (hidden,), flip, give, *scratch[:2], scratch[2:7])
+    gather = RowGather(chips, down_low, down_full, scratch[7:])
+    own_block = pltpu.make_async_copy(down_low, down_full.at[me], own_sem)
+
     @pl.when(pl.program_id(0) == 0)
     def _():
-        first = start[0]
-        for i in range(blocks):
-            high = min(length, block * (i + 2)) - block * i
-            keys = block * i + lax.broadcasted_iota(jnp.int32, (high, block), 0)
-            places = block * i + lax.broadcasted_iota(jnp.int32, (high, block), 1)
-            inside = (keys >= first) & (keys < first + PIECE) & (places >= first) & (places < first + PIECE)
-            bias[i, :high] = jnp.where((keys <= places) | inside, 0.0, NEGATIVE)
+        greet(chips, mp_size)
+        gather.start()
+        own_block.start()
+        down.swap()
+        down.collect()
 
     def turn(values, sign):
         return (
@@ -440,6 +522,34 @@
     v_grad[...] = v_acc[...].astype(BF)
     for total_out, rows_out in ((q_sum, q_grad), (k_sum, k_grad), (v_sum, v_grad)):
         total_out[...] = jnp.sum(rows_out[...].astype(F32), axis=0, keepdims=True)
+    for i in range(pairs):
+
+        @pl.when(pl.program_id(0) == i)
+        def _():
+            for s in range(chips - 1):
+                if min(s, pairs - 1) == i:
+                    gather.stage(s + 1)
+                    if s > 0:
+                        down.relay(s)
+            if i == pairs - 1:
+                down.finish(down_share)
+                for oz in range(chips):
+                    gather.wait_block(2 * oz + 1 - c)
+                own_block.wait()
+                down.drain_swap()
+                down.drain()
+                gather.drain()
+
+
+def mask_bias(start, length):
+    block = 256
+    parts = []
+    for i in range(length // block):
+        keys = block * i + lax.broadcasted_iota(jnp.int32, (2 * block, block), 0)
+        places = block * i + lax.broadcasted_iota(jnp.int32, (2 * block, block), 1)
+        inside = (keys >= start) & (keys < start + PIECE) & (places >= start) & (places < start + PIECE)
+        parts.append(jnp.where((keys <= places) | inside, 0.0, NEGATIVE))
+    return jnp.stack(parts)
 
 
 def rotary_lanes(length):
@@ -460,39 +570,66 @@
     )
 
 
-def attention(projected, out_grad, start):
+def attention(dp_size, mp_size, projected, out_grad, start, cot_all, hidden, down_low):
     length, width = out_grad.shape
-    pairs = width // 128
+    pairs, chips = width // 128, dp_size // 2
+    depth, inner = down_low.shape
     shape = jax.ShapeDtypeStruct
 
     def rows(shift):
         return pl.BlockSpec((length, 128), lambda i: (0, i + shift))
 
+    def whole(*dims):
+        return pl.BlockSpec(dims, lambda i: (0,) * len(dims), pipeline_mode=pl.Buffered(1))
+
     total = pl.BlockSpec((1, 128), lambda i: (0, i))
     return pl.pallas_call(
-        attention_kernel,
+        partial(attention_kernel, dp_size, mp_size, pairs),
         grid=(pairs,),
         in_specs=[
-            pl.BlockSpec(memory_space=pltpu.SMEM),
+            whole(length // 256, 512, 256),
             rows(0),
             rows(pairs),
             rows(2 * pairs),
             rows(0),
-            pl.BlockSpec((3, length, 128), lambda i: (0, 0, 0)),
+            whole(3, length, 128),
+            whole(*cot_all.shape),
+            whole(*hidden.shape),
+            ANY,
         ],
-        out_specs=[rows(0)] * 4 + [total] * 3,
-        out_shape=[shape((length, width), BF)] * 4 + [shape((1, width), F32)] * 3,
+        out_specs=[rows(0)] * 4 + [total] * 3 + [pl.BlockSpec((depth, inner), lambda i: (0, 0)), ANY],
+        out_shape=[shape((length, width), BF)] * 4
+        + [shape((1, width), F32)] * 3
+        + [shape((depth, inner), F32), shape((dp_size, depth, inner), BF)],
         scratch_shapes=[
-            pltpu.VMEM((length // 256, 512, 256), F32),
             pltpu.VMEM((length, 128), F32),
             pltpu.VMEM((length, 128), F32),
+            pltpu.VMEM((depth, length), BF),
+            pltpu.VMEM((chips, depth, inner), BF),
+            pltpu.SemaphoreType.DMA,
+            *row_scatter_scratch(chips, depth, inner),
+            *row_gather_sems(dp_size),
         ],
-        compiler_params=pltpu.CompilerParams(vmem_limit_bytes=62 << 20),
+        compiler_params=pltpu.CompilerParams(
+            collective_id=4, has_side_effects=True, vmem_limit_bytes=62 << 20
+        ),
         cost_estimate=pl.CostEstimate(
-            flops=16 * length * length * width, bytes_accessed=16 * length * width, transcendentals=length * length * width // 64
+            flops=16 * length * length * width + 2 * length * cot_all.shape[1] * inner,
+            bytes_accessed=16 * length * width,
+            transcendentals=length * length * width // 64,
         ),
         name="attention",
-    )(start, projected, projected, projected, out_grad, rotary_lanes(length))
+    )(
+        mask_bias(start[0], length),
+        projected,
+        projected,
+        projected,
+        out_grad,
+        rotary_lanes(length),
+        cot_all,
+        hidden,
+        down_low,
+    )
 
 
 def flat(ref, cols):
@@ -889,8 +1026,6 @@
     if chips > 2:
         up.relay(1)
     qkv.finish(qkv_share)
-    for s in range(2, chips - 1):
-        up.relay(s)
 
     normed_group.arrive()
     loads[5].wait()
@@ -933,6 +1068,8 @@
 
     for k in range(1, mp_size):
         copy_1(k).start()
+    for s in range(2, chips - 1):
+        up.relay(s)
     mixed_group.arrive()
 
     def add_up(i, carry):
@@ -1028,18 +1165,6 @@
     )(*hbm_args, *grads, *sums, tokens, cot, gain.reshape(1, -1), out_bias.reshape(1, -1))
 
 
-def rows_product(left_side, right_side):
-    return lax.dot_general(
-        left_side, right_side, (((0,), (0,)), ((), ())), preferred_element_type=jnp.float32
-    )
-
-
-def low_scatter(partial_sums, axis):
-    return lax.psum_scatter(
-        partial_sums.astype(jnp.bfloat16), axis, scatter_dimension=0, tiled=True
-    ).astype(jnp.float32)
-
-
 def body(
     tokens,
     ln_gain,
@@ -1056,39 +1181,39 @@
     cotangent,
 ):
     dp_size, mp_size = lax.axis_size("dp"), lax.axis_size("mp")
-    x_all, cot_all, up_all, hidden_all, slope_all = up_stage(
-        dp_size, mp_size, tokens, ln_gain, ln_bias, cotangent, fc1_weight, fc1_bias
+    x_all, cot_all, up_all, hidden_all, slope_all, qkv_all, dense_all, projected = up_stage(
+        dp_size,
+        mp_size,
+        tokens,
+        ln_gain,
+        ln_bias,
+        cotangent,
+        fc1_weight,
+        fc1_bias,
+        qkv_bias.reshape(1, -1),
+        qkv_weight.astype(BF).reshape(qkv_weight.shape[0], -1),
+        dense_weight.astype(BF),
     )
     gathered = x_all.reshape(-1, x_all.shape[-1])
     out_rows = cot_all.reshape(gathered.shape)
     up_full = up_all.reshape(-1, up_all.shape[-1])
     hidden_low = hidden_all.reshape(-1, up_all.shape[-1])
     slope = slope_all.reshape(hidden_low.shape)
-    masters = (
-        qkv_weight.astype(jnp.bfloat16).reshape(qkv_weight.shape[0], -1),
-        dense_weight.astype(jnp.bfloat16),
-        fc2_weight.astype(jnp.bfloat16),
-    )
-    qkv_full, dense_full, down_full = (
-        lax.all_gather(masters[0], "dp", axis=0, tiled=True),
-        lax.all_gather(masters[1], "dp", axis=0, tiled=True),
-        lax.all_gather(masters[2], "dp", axis=0, tiled=True),
-    )
+    qkv_full = qkv_all.reshape(-1, qkv_all.shape[-1])
+    dense_full = dense_all.reshape(-1, dense_all.shape[-1])
     local_width = dense_full.shape[1]
-    projected = jnp.dot(
-        gathered, qkv_full, preferred_element_type=jnp.float32
-    ) + qkv_bias.reshape(3 * local_width)
+    projected = projected.reshape(gathered.shape[0], -1)
     attended_grad = jnp.dot(out_rows, dense_full, preferred_element_type=jnp.float32).astype(
         jnp.bfloat16
     )
-    down_grad = rows_product(out_rows, hidden_low).astype(jnp.bfloat16)
-    projected, down_grad = lax.optimization_barrier((projected, down_grad))
-    attended, query_grad, key_grad, value_grad, query_sum, key_sum, value_sum = attention(
-        projected, attended_grad, starts
+    attended, query_grad, key_grad, value_grad, query_sum, key_sum, value_sum, down_share, down_all = (
+        attention(
+            dp_size, mp_size, projected, attended_grad, starts, out_rows, hidden_low, fc2_weight.astype(BF)
+        )
     )
+    down_full = down_all.reshape(-1, down_all.shape[-1])
     hidden_grad = jnp.dot(out_rows, down_full, preferred_element_type=jnp.float32)
     pre_grad = (hidden_grad * slope).astype(jnp.bfloat16)
-    down_share = low_scatter(down_grad, "dp")
     up_bias_grad = jnp.sum(pre_grad.astype(jnp.float32), axis=0)
     dense_share, qkv_share, up_share, output, input_grad, totals = grad_stage(
         dp_size,

time: 484 us -> 465 us (0.961)
  matrix products: 47.3 us -> 21.2 us
  Pallas kernels: 397 us -> 418 us
  between operations: 15.1 us -> 1.57 us
    pallas_call x1, Pallas kernels: 37.4 us -> 101 us  [attention(): pl.pallas_call(partial(attention_kernel, dp_size, mp_size, pairs), grid=(...]
    pallas_call x1, Pallas kernels: 190 us -> 156 us  [grad_stage(): pl.pallas_call(partial(grad_kernel, dp_size, mp_size), out_shape=(shape((...]
    dot_general x2 -> x0, matrix products: 25.9 us -> none  [the longest x1 14.1 us: rows_product(): lax.dot_general(left_side, right_side, (((0,), (0,)), ((), ())), preferre...]
    pallas_call x1, Pallas kernels: 169 us -> 160 us  [up_stage(): pl.pallas_call(partial(up_kernel, dp_size, mp_size), out_shape=outs, in_s...]
    unnamed x27 -> x33, local copies, waits for them, and re-layouts: 9.47 us -> 12.6 us
  transfers between devices with their start and end apart: 4 -> 0, of which waited for: 0 -> 0; matrix products, arithmetic and copies ran while one was open for 12% -> 0% of each run, Pallas kernels for 83% -> 0%
where the time goes in v7:
time: 465 us; the launch traced here: 464 us
  Pallas kernels  418 us (90%)
  matrix products  21.2 us (5%)
  local copies, waits for them, and re-layouts  17.4 us (4%)
  other arithmetic  6.46 us (1%)
    pallas_call x1, Pallas kernels, up_stage(): pl.pallas_call(partial(up_kernel, dp_size, mp_size), out_shape=outs, in_s...  160 us
    pallas_call x1, Pallas kernels, grad_stage(): pl.pallas_call(partial(grad_kernel, dp_size, mp_size), out_shape=(shape((...  156 us
    pallas_call x1, Pallas kernels, attention(): pl.pallas_call(partial(attention_kernel, dp_size, mp_size, pairs), grid=(...  101 us
    dot_general x1, matrix products, body(): jnp.dot(out_rows, down_full, preferred_element_type=jnp.float32)  15.1 us
    unnamed x33, local copies, waits for them, and re-layouts  12.6 us

profile of v7, /device:TPU:0, one launch (start us, length us, event | category | flops | bytes accessed | tf_op | source)
XLA Modules:
  0.0 464.3 jit_solution(5820705497233137500)
XLA Ops:
  1.4 0.2 or_select_fusion
  1.6 0.2 or_select_fusion.1
  1.9 0.2 or_select_fusion.2
  2.1 0.1 fusion.2
  2.2 0.0 copy-start.3
  2.3 1.5 pad_maximum_fusion.bias
  3.7 0.6 copy-done.3
  4.4 0.3 copy.27
  4.6 1.2 copy.28.qkv_low
  5.8 0.0 copy-done.5
  5.8 0.7 convert_element_type.47.dense_low
  6.5 0.0 copy-done.11
  6.5 0.6 copy.34
  7.1 160.3 %up_stage.1 = (bf16[4,256,2048]{2,1,0:T(8,128)(2,1)}, bf16[4,256,2048]{2,1,0:T(8,128)(2,1)}, bf16[8,256,2048]{2,1,0:T(8,128)(2,1)}, bf16[4,256,2048]{2,1,0:T(8,1...) custom-call(bf16[256,2048]{1,0:T(8,128)(2,1)} %tokens.3, ...), custom_call_target="tpu_custom_call" | custom-call | tf_op jit(solution)/shard_map/up_stage/pallas_call | solution.py:381
  167.5 6.2 %convolution_convert_fusion.out_grad = bf16[1024,512]{1,0:T(8,128)(2,1)} fusion(bf16[1024,2048]{1,0:T(8,128)(2,1)} %bitcast.41, bf16[2048,512]{1,0:T(8,128)(2,1)} %bitcast.47), kind=kOutput, calls=%fused_computation.5 | convolution fusion | flops 2148007936 | bytes 7340032 | tf_op jit(solution)/shard_map/dot_general | solution.py:1206
  173.6 0.3 multiply_cosine_fusion
  174.0 0.2 copy.30
  174.2 0.1 negate_select_fusion
  174.4 0.2 copy.29
  174.6 0.0 copy-start
  174.6 1.2 pad_maximum_fusion.1.rot
  175.9 0.9 copy-done
  176.7 1.1 convert_element_type.51.down_low
  177.8 101.5 %attention.1 = (bf16[1024,512]{1,0:T(8,128)(2,1)}, bf16[1024,512]{1,0:T(8,128)(2,1)}, bf16[1024,512]{1,0:T(8,128)(2,1)}, bf16[1024,512]{1,0:T(8,128)(2,1)}, f32[...) custom-call(f32[4,512,256]{2,1,0:T(8,128)} %pad_maximum_fusion.bias,, ...), custom_call_target="tpu_custom_call" | custom-call | flops 17179869184 | bytes 8388608 | tf_op jit(solution)/shard_map/attention/pallas_call | solution.py:586
  279.3 0.0 copy-start.9
  279.4 0.0 copy-start.10
  279.4 15.1 %convert_reduce_fusion = (f32[2048]{0:T(1024)}, bf16[1024,2048]{1,0:T(8,128)(2,1)}) fusion(bf16[1024,2048]{1,0:T(8,128)(2,1)} %bitcast.67, bf16[1024,2048]{1,0:T(8,128)(2,1)} %bitcast.43, bf16[2048,2048]{1,0:T(8,128)(2,1)} %bitcast.37), kind=kOutput, calls=%fused_computation.2 | convolution fusion | flops 8600418304 | bytes 20979712 | tf_op jit(solution)/shard_map/dot_general | solution.py:1215
  294.4 0.0 copy-done.9
  294.5 0.0 copy-done.10
  294.5 0.6 add.89
  295.1 155.8 %grad_stage.1 = (f32[256,512]{1,0:T(8,128)}, f32[256,1536]{1,0:T(8,128)}, f32[256,2048]{1,0:T(8,128)}, bf16[256,2048]{1,0:T(8,128)(2,1)}, bf16[256,2048]{1,0:T(8,128)(2,1)}, /*index=5*/f32[8,2048]{1,0:T(8,128)}) custom-call(bf16[4,256,2048]{2,1,0:T(8,128)(2,1)} %get-tuple-element.35.x_all, bf16[4,256,2048]{2,1,0:T(8,128)(2,1)} %bitcast.45, ...), custom_call_target="tpu_custom_call" | custom-call | tf_op jit(solution)/shard_map/grad_stage/pallas_call | solution.py:1128
  450.9 1.9 copy.32
  452.8 0.0 copy-start.8
  452.8 0.0 copy-start.4
  452.8 1.6 copy.33
  454.4 0.0 copy-done.8
  454.4 0.6 fusion.10
  455.1 0.6 reshape_squeeze.3
  455.7 0.6 copy.42
  456.3 2.4 copy.43
  458.7 0.0 copy-done.4
  458.7 1.0 copy.44
  459.6 0.0 copy-done.7
  459.6 0.8 copy.45
  460.4 0.2 copy-done.2
  460.6 1.3 copy.46
  462.0 1.0 copy-done.1
  463.0 1.3 copy.47
  (27 shorter events, 0.3 us)
Async XLA Ops:
  2.2 2.1 copy-start.3
  3.7 2.1 copy-start.5
  4.4 2.2 copy-start.11
  174.6 2.2 copy-start
  279.3 15.1 %copy-start.9 = (f32[2048]{0:T(1024)S(1)}, f32[2048]{0:T(1024)}, u32[]{:S(2)}) copy-start(f32[2048]{0:T(1024)} %param.19) | copy-start | bytes 24580
  279.4 15.1 %copy-start.10 = (f32[2048]{0:T(1024)S(1)}, f32[2048]{0:T(1024)}, u32[]{:S(2)}) copy-start(f32[2048]{0:T(1024)} %param.23) | copy-start | bytes 24580
  452.8 1.6 copy-start.8
  452.8 5.9 %copy-start.4 = (bf16[256,2048]{1,0:T(8,128)(2,1)S(1)}, bf16[256,2048]{1,0:T(8,128)(2,1)}, u32[]{:S(2)}) copy-start(bf16[256,2048]{1,0:T(8,128)(2,1)} %get-tuple-element.143) | copy-start | bytes 3145732
  455.1 4.6 copy-start.7
  456.3 3.3 copy-start.6
  458.7 2.0 copy-start.2
  460.6 2.3 copy-start.1

commit v8 on v7

--- a/solution.py
+++ b/solution.py
@@ -329,27 +329,45 @@
     slope_copy = pltpu.make_async_copy(slope, slope_out, out_sem.at[4])
     hidden_copy.start()
     slope_copy.start()
-    for k in range(2, chips):
-        qkv_gather.stage(k)
-        dense_gather.stage(k - 1)
-    for oz in range(chips):
-        qkv_gather.wait_block(2 * oz + 1 - c)
     weights.drain()
     up_copy.wait()
     own_blocks[0].wait()
     thirds = qkv_low.shape[1]
-    qkv_load = pltpu.make_async_copy(qkv_out, up_all.at[:, :, pl.ds(0, thirds)], out_sem.at[5])
-    qkv_load.start()
-    qkv_load.wait()
     part = 512 if thirds % 512 == 0 else 256
 
-    def project(i, carry):
-        r, n = i // (thirds // part), lax.rem(i, thirds // part)
-        n0 = pl.ds(pl.multiple_of(n * part, part), part)
-        acc[r, :, n0] = dot(x_all[r], up_all[:, :, n0].reshape(dp_size * depth, part)) + qkv_bias[:, n0]
-        return carry
-
-    lax.fori_loop(0, mp_size * (thirds // part), project, 0)
+    def project(oz, begins=False):
+        qkv_gather.wait_block(2 * oz + 1 - c)
+        pair = pl.ds(2 * oz, 2)
+        load = pltpu.make_async_copy(
+            qkv_out.at[pair], up_all.at[pair, :, pl.ds(0, thirds)], out_sem.at[5]
+        )
+        load.start()
+        load.wait()
+        cols = pl.ds(pl.multiple_of(oz * (2 * depth), 2 * depth), 2 * depth)
+
+        def tile(i, carry):
+            r, n = i // (thirds // part), lax.rem(i, thirds // part)
+            n0 = pl.ds(pl.multiple_of(n * part, part), part)
+            term = dot(x_all[r, :, cols], up_all[pair, :, n0].reshape(2 * depth, part))
+            if begins:
+                acc[r, :, n0] = term + qkv_bias[:, n0]
+            else:
+                acc[r, :, n0] += term
+            return carry
+
+        lax.fori_loop(0, mp_size * (thirds // part), tile, 0)
+
+    project(z, True)
+    for k in range(1, chips):
+        if k > 1:
+            qkv_gather.stage(k)
+            dense_gather.stage(k - 1)
+        for oz, valid in ((z + k, z + k < chips), (z - k, z - k >= 0)):
+
+            @pl.when(valid)
+            def _():
+                project(oz)
+
     projected_copy = pltpu.make_async_copy(acc.at[:, :, pl.ds(0, thirds)], projected_out, out_sem.at[2])
     projected_copy.start()
     dense_gather.stage(chips - 1)

time: 465 us -> 465 us (level); the launches traced: 464 us -> 458 us
  Pallas kernels: 418 us -> 411 us
    pallas_call x1, Pallas kernels: 160 us -> 154 us  [up_stage(): pl.pallas_call(partial(up_kernel, dp_size, mp_size), out_shape=outs, in_s...]
where the time goes in v8:
time: 465 us; the launch traced here: 458 us
  Pallas kernels  411 us (88%)
  matrix products  21.2 us (5%)
  local copies, waits for them, and re-layouts  17.4 us (4%)
  other arithmetic  6.46 us (1%)
    pallas_call x1, Pallas kernels, grad_stage(): pl.pallas_call(partial(grad_kernel, dp_size, mp_size), out_shape=(shape((...  156 us
    pallas_call x1, Pallas kernels, up_stage(): pl.pallas_call(partial(up_kernel, dp_size, mp_size), out_shape=outs, in_s...  154 us
    pallas_call x1, Pallas kernels, attention(): pl.pallas_call(partial(attention_kernel, dp_size, mp_size, pairs), grid=(...  101 us
    dot_general x1, matrix products, body(): jnp.dot(out_rows, down_full, preferred_element_type=jnp.float32)  15.1 us
    unnamed x33, local copies, waits for them, and re-layouts  12.6 us

profile of v8, /device:TPU:0, one launch (start us, length us, event | category | flops | bytes accessed | tf_op | source)
XLA Modules:
  0.0 458.4 jit_solution(6160419236341954601)
XLA Ops:
  1.4 0.2 or_select_fusion
  1.6 0.2 or_select_fusion.1
  1.9 0.2 or_select_fusion.2
  2.1 0.1 fusion.2
  2.2 0.0 copy-start.3
  2.3 1.5 pad_maximum_fusion.bias
  3.7 0.6 copy-done.3
  4.4 0.3 copy.27
  4.6 1.2 copy.28.qkv_low
  5.8 0.0 copy-done.5
  5.8 0.7 convert_element_type.47.dense_low
  6.5 0.0 copy-done.11
  6.5 0.6 copy.34
  7.1 154.0 %up_stage.1 = (bf16[4,256,2048]{2,1,0:T(8,128)(2,1)}, bf16[4,256,2048]{2,1,0:T(8,128)(2,1)}, bf16[8,256,2048]{2,1,0:T(8,128)(2,1)}, bf16[4,256,2048]{2,1,0:T(8,1...) custom-call(bf16[256,2048]{1,0:T(8,128)(2,1)} %tokens.3, ...), custom_call_target="tpu_custom_call" | custom-call | tf_op jit(solution)/shard_map/up_stage/pallas_call | solution.py:399
  161.2 6.2 %convolution_convert_fusion.out_grad = bf16[1024,512]{1,0:T(8,128)(2,1)} fusion(bf16[1024,2048]{1,0:T(8,128)(2,1)} %bitcast.41, bf16[2048,512]{1,0:T(8,128)(2,1)} %bitcast.47), kind=kOutput, calls=%fused_computation.5 | convolution fusion | flops 2148007936 | bytes 7340032 | tf_op jit(solution)/shard_map/dot_general | solution.py:1224
  167.4 0.3 multiply_cosine_fusion
  167.7 0.2 copy.30
  167.9 0.1 negate_select_fusion
  168.1 0.2 copy.29
  168.3 0.0 copy-start
  168.3 1.2 pad_maximum_fusion.1.rot
  169.6 0.9 copy-done
  170.4 1.1 convert_element_type.51.down_low
  171.6 101.5 %attention.1 = (bf16[1024,512]{1,0:T(8,128)(2,1)}, bf16[1024,512]{1,0:T(8,128)(2,1)}, bf16[1024,512]{1,0:T(8,128)(2,1)}, bf16[1024,512]{1,0:T(8,128)(2,1)}, f32[...) custom-call(f32[4,512,256]{2,1,0:T(8,128)} %pad_maximum_fusion.bias,, ...), custom_call_target="tpu_custom_call" | custom-call | flops 17179869184 | bytes 8388608 | tf_op jit(solution)/shard_map/attention/pallas_call | solution.py:604
  273.0 0.0 copy-start.9
  273.0 0.0 copy-start.10
  273.0 15.1 %convert_reduce_fusion = (f32[2048]{0:T(1024)}, bf16[1024,2048]{1,0:T(8,128)(2,1)}) fusion(bf16[1024,2048]{1,0:T(8,128)(2,1)} %bitcast.67, bf16[1024,2048]{1,0:T(8,128)(2,1)} %bitcast.43, bf16[2048,2048]{1,0:T(8,128)(2,1)} %bitcast.37), kind=kOutput, calls=%fused_computation.2 | convolution fusion | flops 8600418304 | bytes 20979712 | tf_op jit(solution)/shard_map/dot_general | solution.py:1233
  288.1 0.0 copy-done.9
  288.1 0.0 copy-done.10
  288.1 0.6 add.89
  288.7 155.8 %grad_stage.1 = (f32[256,512]{1,0:T(8,128)}, f32[256,1536]{1,0:T(8,128)}, f32[256,2048]{1,0:T(8,128)}, bf16[256,2048]{1,0:T(8,128)(2,1)}, bf16[256,2048]{1,0:T(8,128)(2,1)}, /*index=5*/f32[8,2048]{1,0:T(8,128)}) custom-call(bf16[4,256,2048]{2,1,0:T(8,128)(2,1)} %get-tuple-element.35.x_all, bf16[4,256,2048]{2,1,0:T(8,128)(2,1)} %bitcast.45, ...), custom_call_target="tpu_custom_call" | custom-call | tf_op jit(solution)/shard_map/grad_stage/pallas_call | solution.py:1146
  444.6 1.9 copy.32
  446.4 0.0 copy-start.8
  446.5 0.0 copy-start.4
  446.5 1.6 copy.33
  448.1 0.0 copy-done.8
  448.1 0.6 fusion.10
  448.7 0.6 reshape_squeeze.3
  449.3 0.6 copy.42
  449.9 2.4 copy.43
  452.3 0.0 copy-done.4
  452.3 1.0 copy.44
  453.3 0.0 copy-done.7
  453.3 0.8 copy.45
  454.1 0.2 copy-done.2
  454.3 1.3 copy.46
  455.6 1.0 copy-done.1
  456.7 1.3 copy.47
  (27 shorter events, 0.3 us)
Async XLA Ops:
  2.2 2.1 copy-start.3
  3.7 2.1 copy-start.5
  4.4 2.2 copy-start.11
  168.3 2.2 copy-start
  273.0 15.1 %copy-start.9 = (f32[2048]{0:T(1024)S(1)}, f32[2048]{0:T(1024)}, u32[]{:S(2)}) copy-start(f32[2048]{0:T(1024)} %param.19) | copy-start | bytes 24580
  273.0 15.1 %copy-start.10 = (f32[2048]{0:T(1024)S(1)}, f32[2048]{0:T(1024)}, u32[]{:S(2)}) copy-start(f32[2048]{0:T(1024)} %param.23) | copy-start | bytes 24580
  446.4 1.6 copy-start.8
  446.5 5.9 %copy-start.4 = (bf16[256,2048]{1,0:T(8,128)(2,1)S(1)}, bf16[256,2048]{1,0:T(8,128)(2,1)}, u32[]{:S(2)}) copy-start(bf16[256,2048]{1,0:T(8,128)(2,1)} %get-tuple-element.143) | copy-start | bytes 3145732
  448.7 4.6 copy-start.7
  449.9 3.3 copy-start.6
  452.3 2.0 copy-start.2
  454.3 2.3 copy-start.1

commit v9 on v8

--- a/solution.py
+++ b/solution.py
@@ -362,11 +362,16 @@
         if k > 1:
             qkv_gather.stage(k)
             dense_gather.stage(k - 1)
-        for oz, valid in ((z + k, z + k < chips), (z - k, z - k >= 0)):
-
-            @pl.when(valid)
+        def side(i, carry):
+            oz = jnp.where(i == 0, z + k, z - k)
+
+            @pl.when((oz >= 0) & (oz < chips))
             def _():
                 project(oz)
+
+            return carry
+
+        lax.fori_loop(0, 2, side, 0)
 
     projected_copy = pltpu.make_async_copy(acc.at[:, :, pl.ds(0, thirds)], projected_out, out_sem.at[2])
     projected_copy.start()

time: 465 us -> 458 us (0.985); the launches traced: 458 us -> 458 us
  no operation moved by 1% of the time
where the time goes in v9:
time: 458 us
  Pallas kernels  411 us (90%)
  matrix products  21.2 us (5%)
  local copies, waits for them, and re-layouts  17.4 us (4%)
  other arithmetic  6.46 us (1%)
    pallas_call x1, Pallas kernels, grad_stage(): pl.pallas_call(partial(grad_kernel, dp_size, mp_size), out_shape=(shape((...  156 us
    pallas_call x1, Pallas kernels, up_stage(): pl.pallas_call(partial(up_kernel, dp_size, mp_size), out_shape=outs, in_s...  154 us
    pallas_call x1, Pallas kernels, attention(): pl.pallas_call(partial(attention_kernel, dp_size, mp_size, pairs), grid=(...  101 us
    dot_general x1, matrix products, body(): jnp.dot(out_rows, down_full, preferred_element_type=jnp.float32)  15.1 us
    unnamed x33, local copies, waits for them, and re-layouts  12.6 us

profile of v9, /device:TPU:0, one launch (start us, length us, event | category | flops | bytes accessed | tf_op | source)
XLA Modules:
  0.0 458.0 jit_solution(14971360140338550575)
XLA Ops:
  1.4 0.2 or_select_fusion
  1.6 0.2 or_select_fusion.1
  1.9 0.2 or_select_fusion.2
  2.1 0.1 fusion.2
  2.2 0.0 copy-start.3
  2.3 1.5 pad_maximum_fusion.bias
  3.7 0.6 copy-done.3
  4.4 0.3 copy.27
  4.6 1.2 copy.28.qkv_low
  5.8 0.0 copy-done.5
  5.8 0.7 convert_element_type.47.dense_low
  6.5 0.0 copy-done.11
  6.5 0.6 copy.34
  7.1 154.1 %up_stage.1 = (bf16[4,256,2048]{2,1,0:T(8,128)(2,1)}, bf16[4,256,2048]{2,1,0:T(8,128)(2,1)}, bf16[8,256,2048]{2,1,0:T(8,128)(2,1)}, bf16[4,256,2048]{2,1,0:T(8,1...) custom-call(bf16[256,2048]{1,0:T(8,128)(2,1)} %tokens.3, ...), custom_call_target="tpu_custom_call" | custom-call | tf_op jit(solution)/shard_map/up_stage/pallas_call | solution.py:404
  161.2 6.2 %convolution_convert_fusion.out_grad = bf16[1024,512]{1,0:T(8,128)(2,1)} fusion(bf16[1024,2048]{1,0:T(8,128)(2,1)} %bitcast.41, bf16[2048,512]{1,0:T(8,128)(2,1)} %bitcast.47), kind=kOutput, calls=%fused_computation.5 | convolution fusion | flops 2148007936 | bytes 7340032 | tf_op jit(solution)/shard_map/dot_general | solution.py:1229
  167.4 0.3 multiply_cosine_fusion
  167.7 0.2 copy.30
  168.0 0.1 negate_select_fusion
  168.1 0.2 copy.29
  168.3 0.0 copy-start
  168.4 1.2 pad_maximum_fusion.1.rot
  169.6 0.9 copy-done
  170.5 1.1 convert_element_type.51.down_low
  171.6 101.5 %attention.1 = (bf16[1024,512]{1,0:T(8,128)(2,1)}, bf16[1024,512]{1,0:T(8,128)(2,1)}, bf16[1024,512]{1,0:T(8,128)(2,1)}, bf16[1024,512]{1,0:T(8,128)(2,1)}, f32[...) custom-call(f32[4,512,256]{2,1,0:T(8,128)} %pad_maximum_fusion.bias,, ...), custom_call_target="tpu_custom_call" | custom-call | flops 17179869184 | bytes 8388608 | tf_op jit(solution)/shard_map/attention/pallas_call | solution.py:609
  273.0 0.0 copy-start.9
  273.1 0.0 copy-start.10
  273.1 15.1 %convert_reduce_fusion = (f32[2048]{0:T(1024)}, bf16[1024,2048]{1,0:T(8,128)(2,1)}) fusion(bf16[1024,2048]{1,0:T(8,128)(2,1)} %bitcast.67, bf16[1024,2048]{1,0:T(8,128)(2,1)} %bitcast.43, bf16[2048,2048]{1,0:T(8,128)(2,1)} %bitcast.37), kind=kOutput, calls=%fused_computation.2 | convolution fusion | flops 8600418304 | bytes 20979712 | tf_op jit(solution)/shard_map/dot_general | solution.py:1238
  288.1 0.0 copy-done.9
  288.1 0.0 copy-done.10
  288.1 0.6 add.89
  288.8 155.8 %grad_stage.1 = (f32[256,512]{1,0:T(8,128)}, f32[256,1536]{1,0:T(8,128)}, f32[256,2048]{1,0:T(8,128)}, bf16[256,2048]{1,0:T(8,128)(2,1)}, bf16[256,2048]{1,0:T(8,128)(2,1)}, /*index=5*/f32[8,2048]{1,0:T(8,128)}) custom-call(bf16[4,256,2048]{2,1,0:T(8,128)(2,1)} %get-tuple-element.35.x_all, bf16[4,256,2048]{2,1,0:T(8,128)(2,1)} %bitcast.45, ...), custom_call_target="tpu_custom_call" | custom-call | tf_op jit(solution)/shard_map/grad_stage/pallas_call | solution.py:1151
  444.6 1.9 copy.32
  446.5 0.0 copy-start.8
  446.5 0.0 copy-start.4
  446.5 1.6 copy.33
  448.1 0.0 copy-done.8
  448.1 0.6 fusion.10
  448.8 0.6 reshape_squeeze.3
  449.4 0.6 copy.42
  450.0 2.4 copy.43
  452.3 0.0 copy-done.4
  452.3 1.0 copy.44
  453.3 0.0 copy-done.6
  453.3 0.8 copy.45
  454.1 0.2 copy-done.2
  454.3 1.3 copy.46
  455.7 1.0 copy-done.1
  456.7 1.3 copy.47
  (27 shorter events, 0.3 us)
Async XLA Ops:
  2.2 2.1 copy-start.3
  3.7 2.1 copy-start.5
  4.4 2.2 copy-start.11
  168.3 2.2 copy-start
  273.0 15.1 %copy-start.9 = (f32[2048]{0:T(1024)S(1)}, f32[2048]{0:T(1024)}, u32[]{:S(2)}) copy-start(f32[2048]{0:T(1024)} %param.19) | copy-start | bytes 24580
  273.1 15.1 %copy-start.10 = (f32[2048]{0:T(1024)S(1)}, f32[2048]{0:T(1024)}, u32[]{:S(2)}) copy-start(f32[2048]{0:T(1024)} %param.23) | copy-start | bytes 24580
  446.5 1.6 copy-start.8
  446.5 5.9 %copy-start.4 = (bf16[256,2048]{1,0:T(8,128)(2,1)S(1)}, bf16[256,2048]{1,0:T(8,128)(2,1)}, u32[]{:S(2)}) copy-start(bf16[256,2048]{1,0:T(8,128)(2,1)} %get-tuple-element.143) | copy-start | bytes 3145732
  448.7 4.6 copy-start.7
  450.0 3.3 copy-start.6
  452.3 2.0 copy-start.2
  454.3 2.3 copy-start.1
